TPU v7x, 32 devices: a whole 2x2x4 slice. The times are simulated.
32 devices in a mesh: fsdp: 16 (over z, y, x), tensor: 2 (over core).
Axes of the slice: x: 2, y: 2, z: 4, core: 2. Of those that a mesh axis runs over, the one named last changes fastest.
Arguments:
- inputs: float32 [16384, 768], P(('fsdp', 'tensor')), may hold values from -6 to 6
- segment_ids: int32 [16384], P('fsdp'), may hold values from 0 to 39, never falling along the last dimension, each value on 1 to 800 neighbouring positions
- qkv_weight: float32 [3, 768, 768], P(None, 'fsdp', 'tensor'), may hold values from -0.21875 to 0.21875
- out_weight: float32 [768, 768], P('tensor', 'fsdp'), may hold values from -0.875 to 0.875
- up_weight: float32 [768, 3072], P('fsdp', 'tensor'), may hold values from -0.21875 to 0.21875
- down_weight: float32 [3072, 768], P('tensor', 'fsdp'), may hold values from -0.109375 to 0.109375
- gain_one: float32 [768], P('fsdp'), may hold values from 0.5 to 1.5
- shift_one: float32 [768], P('fsdp'), may hold values from -4 to 4
- gain_two: float32 [768], P('fsdp'), may hold values from 0.5 to 1.5
- shift_two: float32 [768], P('fsdp'), may hold values from -4 to 4
- cotangent: bfloat16 [16384, 768], P(('fsdp', 'tensor')), may hold values from -6 to 6
Outputs:
- outputs: float32 [16384, 768], P(('fsdp', 'tensor'))
- input_grad: float32 [16384, 768], P(('fsdp', 'tensor'))
- qkv_grad: float32 [3, 768, 768], P(None, 'fsdp', 'tensor')
- out_grad: float32 [768, 768], P('tensor', 'fsdp')
- up_grad: float32 [768, 3072], P('fsdp', 'tensor')
- down_grad: float32 [3072, 768], P('tensor', 'fsdp')
- gain_one_grad: float32 [768], P('fsdp')
- shift_one_grad: float32 [768], P('fsdp')
- gain_two_grad: float32 [768], P('fsdp')
- shift_two_grad: float32 [768], P('fsdp')
Inputs may be any that keep to these rules, and one draw needn't show every extreme that they name: `segment_ids`: ids never fall along the tokens; each document holds 1 to 800 tokens and one holds exactly 800; a document may run past a sequence's end, and attention never crosses a sequence's end.
All inputs are finite; a program needn't handle non-finite values.
Results may differ from a plain program's by a relative error of at most 0.015.
Values may be sent and summed in bfloat16 or wider, within the bound.
No kernel may reach another device: no remote copies, remote signals or barrier semaphores. Data moves between devices by JAX's collectives and lax.ppermute only.
A program may use at most 128 MiB of HBM per device.

v0:
```python
import functools
import math

import jax
import jax.numpy as jnp
from jax import lax
from jax.experimental import pallas as pl
from jax.experimental.pallas import tpu as pltpu
from jax.sharding import PartitionSpec as P

HD = 64
EPS = 1e-05
LOW = jnp.bfloat16
WIDE = jnp.float32
BLOCKS = 16
ROWS = 256
LANES = 128
LOG2E = math.log2(math.e)
MASKED = -1e30


def nn(a, b):
    return jnp.dot(a, b, preferred_element_type=WIDE)


def nt(a, b):
    return lax.dot_general(a, b, (((1,), (1,)), ((), ())), preferred_element_type=WIDE)


def tn(a, b):
    return lax.dot_general(a, b, (((0,), (0,)), ((), ())), preferred_element_type=WIDE)


def cost(flops, moved, special=0):
    return pl.CostEstimate(flops=int(flops), bytes_accessed=int(moved), transcendentals=int(special))


def params():
    return pltpu.CompilerParams(
        dimension_semantics=("arbitrary",), vmem_limit_bytes=60 * 1024 * 1024
    )


def fixed(shape, index=None):
    place = index or (0,) * len(shape)
    return pl.BlockSpec(shape, lambda i, *_: place, pipeline_mode=pl.Buffered(1))


def kept(shape, index=None):
    place = index or (0,) * len(shape)
    return pl.BlockSpec(shape, lambda i, *_: place)


def by_row(width, rows=ROWS):
    return pl.BlockSpec((rows, width), lambda i, *_: (i, 0))


def hat_of(values):
    centre = values - jnp.mean(values, axis=-1, keepdims=True)
    rate = lax.rsqrt(jnp.mean(centre * centre, axis=-1, keepdims=True) + EPS)
    return centre * rate, rate


def norm_back(grad, hat, rate, gain):
    scaled = grad * gain
    return rate * (
        scaled
        - jnp.mean(scaled, axis=-1, keepdims=True)
        - hat * jnp.mean(scaled * hat, axis=-1, keepdims=True)
    )


def at_block(table, place, rows):
    return pl.ds(pl.multiple_of(table[place] * rows, 16), rows)


def enter_kernel(table, own, other, wa, wb, normed, proj, whole, vectors, loose):
    step = pl.program_id(0)
    rows = wa.shape[0] // BLOCKS
    cut = wa.shape[1]
    rest = whole.shape[1] - cut

    @pl.when(step == 0)
    def _():
        for j in range(BLOCKS):
            to = slice(j * rows, (j + 1) * rows)
            whole[to, :cut] = wa[at_block(table, j, rows), :]
            late = wb[at_block(table, BLOCKS + j, rows), :]
            whole[to, cut:] = late[:, :rest]
            loose[to, :] = late[:, rest:].astype(WIDE)
        vectors[...] = loose[...].T[:8]

    mine = (step // 2) == table[2 * BLOCKS]
    values = jnp.where(mine, own[...], other[...])
    hat, _ = hat_of(values)
    low = (hat * vectors[0:1, :] + vectors[1:2, :]).astype(LOW)
    normed[...] = low
    proj[...] = nn(low, whole[...]).astype(LOW)


def enter(table, own, other, wa, wb):
    half, width = own.shape
    total = wa.shape[1] + wb.shape[1] - LANES
    steps = 2 * half // ROWS
    pair = pl.BlockSpec((ROWS, width), lambda i, *_: (i % (steps // 2), 0))
    return pl.pallas_call(
        enter_kernel,
        grid_spec=pltpu.PrefetchScalarGridSpec(
            num_scalar_prefetch=1,
            grid=(steps,),
            in_specs=[pair, pair, fixed(wa.shape), fixed(wb.shape)],
            out_specs=[by_row(width), by_row(total), kept((width, total)), kept((8, width))],
            scratch_shapes=[pltpu.VMEM((width, LANES), WIDE)],
        ),
        out_shape=[
            jax.ShapeDtypeStruct((2 * half, width), LOW),
            jax.ShapeDtypeStruct((2 * half, total), LOW),
            jax.ShapeDtypeStruct((width, total), LOW),
            jax.ShapeDtypeStruct((8, width), WIDE),
        ],
        compiler_params=params(),
        cost_estimate=cost(4 * half * width * total, 12 * half * width, 0),
        name="enter",
    )(table, own, other, wa, wb)


def build_bias(bias, seg_col, seg_row):
    length = bias.shape[0]
    for start in range(0, length, ROWS):
        lanes = slice(start, start + ROWS)
        until = start + ROWS
        shape = (until, ROWS)
        key_at = lax.broadcasted_iota(jnp.int32, shape, 0)
        query_at = lax.broadcasted_iota(jnp.int32, shape, 1) + start
        same = jnp.broadcast_to(seg_col[:until, 0:1], shape) == jnp.broadcast_to(
            seg_row[0:1, lanes], shape
        )
        bias[:until, lanes] = jnp.where((key_at <= query_at) & same, 0.0, MASKED)


def one_head(flipped, head):
    empty = jnp.zeros((HD, flipped.shape[1]), flipped.dtype)
    if head == 0:
        return jnp.concatenate([flipped[:HD], empty], axis=0)
    return jnp.concatenate([empty, flipped[HD:]], axis=0)


def attend_kernel(queries, keys, values, seg_col, seg_row, out, lse, bias):
    @pl.when(pl.program_id(0) == 0)
    def _():
        build_bias(bias, seg_col, seg_row)

    length = queries.shape[0]
    q_flip = queries[...].T
    v_flip = values[...].T
    sides = [one_head(q_flip, head) for head in range(2)]
    for start in range(0, length, ROWS):
        lanes = slice(start, start + ROWS)
        until = start + ROWS
        pieces = []
        for head in range(2):
            scores = nn(keys[:until], sides[head][:, lanes]) * (HD**-0.5 * LOG2E)
            scores = scores + bias[:until, lanes]
            top = jnp.max(scores, axis=0, keepdims=True)
            expo = jnp.exp2(scores - top)
            total = jnp.sum(expo, axis=0, keepdims=True)
            flat = nn(v_flip[head * HD : (head + 1) * HD, :until], expo.astype(LOW))
            pieces.append(flat / total)
            lse[head : head + 1, lanes] = top + jnp.log(total) * LOG2E
        out[lanes, :] = jnp.concatenate(pieces, axis=0).T.astype(LOW)


def attend(proj, seg_col, seg_row):
    length = proj.shape[0]
    pairs = proj.shape[1] // (3 * LANES)

    def part(k):
        return pl.BlockSpec((length, LANES), lambda i: (0, k * pairs + i))

    return pl.pallas_call(
        attend_kernel,
        grid=(pairs,),
        in_specs=[part(0), part(1), part(2), fixed(seg_col.shape), fixed(seg_row.shape)],
        out_specs=[
            pl.BlockSpec((length, LANES), lambda i: (0, i)),
            pl.BlockSpec((8, length), lambda i: (i, 0)),
        ],
        out_shape=[
            jax.ShapeDtypeStruct((length, pairs * LANES), LOW),
            jax.ShapeDtypeStruct((8 * pairs, length), WIDE),
        ],
        scratch_shapes=[pltpu.VMEM((length, length), WIDE)],
        compiler_params=params(),
        cost_estimate=cost(
            8 * pairs * length * length * LANES, 8 * length * pairs * LANES, pairs * length * length
        ),
        name="attend",
    )(proj, proj, proj, seg_col, seg_row)


def attend_back_kernel(
    queries, keys, values, out, grad, lse, seg_col, seg_row, result, bias, k_sum, v_sum
):
    @pl.when(pl.program_id(0) == 0)
    def _():
        build_bias(bias, seg_col, seg_row)

    length = queries.shape[0]
    scale = HD**-0.5
    q_flip = queries[...].T
    k_flip = keys[...].T
    g_flip = grad[...].T
    product = out[...].T.astype(WIDE) * g_flip.astype(WIDE)
    k_sum[...] = jnp.zeros_like(k_sum)
    v_sum[...] = jnp.zeros_like(v_sum)
    q_sides = [one_head(q_flip, head) for head in range(2)]
    g_sides = [one_head(g_flip, head) for head in range(2)]
    for start in range(0, length, ROWS):
        lanes = slice(start, start + ROWS)
        until = start + ROWS
        pieces = []
        for head in range(2):
            scores = nn(keys[:until], q_sides[head][:, lanes]) * (scale * LOG2E)
            probs = jnp.exp2(scores + bias[:until, lanes] - lse[head : head + 1, lanes])
            v_sum[head, :until] += nn(probs.astype(LOW), grad[lanes, :])
            centre = jnp.sum(
                product[head * HD : (head + 1) * HD, lanes], axis=0, keepdims=True
            )
            pull = nn(values[:until], g_sides[head][:, lanes])
            pull = (probs * (pull - centre)).astype(LOW)
            k_sum[head, :until] += nn(pull, queries[lanes, :])
            pieces.append(nn(k_flip[head * HD : (head + 1) * HD, :until], pull))
        result[0, lanes, :] = (jnp.concatenate(pieces, axis=0) * scale).T.astype(LOW)
    first = lax.broadcasted_iota(jnp.int32, (length, LANES), 1) < HD
    result[1] = (jnp.where(first, k_sum[0], k_sum[1]) * scale).astype(LOW)
    result[2] = jnp.where(first, v_sum[0], v_sum[1]).astype(LOW)


def attend_back(proj, out, grad, lse, seg_col, seg_row):
    length = proj.shape[0]
    pairs = proj.shape[1] // (3 * LANES)

    def part(k):
        return pl.BlockSpec((length, LANES), lambda i: (0, k * pairs + i))

    return pl.pallas_call(
        attend_back_kernel,
        grid=(pairs,),
        in_specs=[
            part(0),
            part(1),
            part(2),
            part(0),
            part(0),
            pl.BlockSpec((8, length), lambda i: (i, 0)),
            fixed(seg_col.shape),
            fixed(seg_row.shape),
        ],
        out_specs=pl.BlockSpec((3, length, LANES), lambda i: (0, 0, i)),
        out_shape=jax.ShapeDtypeStruct((3, length, pairs * LANES), LOW),
        scratch_shapes=[
            pltpu.VMEM((length, length), WIDE),
            pltpu.VMEM((2, length, LANES), WIDE),
            pltpu.VMEM((2, length, LANES), WIDE),
        ],
        compiler_params=params(),
        cost_estimate=cost(
            20 * pairs * length * length * LANES,
            16 * length * pairs * LANES,
            pairs * length * length,
        ),
        name="attend_back",
    )(proj, proj, proj, out, grad, lse, seg_col, seg_row)


def leave_kernel(table, att, packed, part, whole):
    rows = packed.shape[0] // BLOCKS

    @pl.when(pl.program_id(0) == 0)
    def _():
        for j in range(BLOCKS):
            whole[j * rows : (j + 1) * rows, :] = packed[at_block(table, j, rows), :]

    part[...] = nt(att[...], whole[...]).astype(LOW)


def leave(table, att, packed):
    length, inner = att.shape
    width = packed.shape[0]
    last = packed.shape[1] // inner - 1
    return pl.pallas_call(
        leave_kernel,
        grid_spec=pltpu.PrefetchScalarGridSpec(
            num_scalar_prefetch=1,
            grid=(length // ROWS,),
            in_specs=[by_row(inner), fixed((width, inner), (0, last))],
            out_specs=[by_row(width), kept((width, inner))],
        ),
        out_shape=[
            jax.ShapeDtypeStruct((length, width), LOW),
            jax.ShapeDtypeStruct((width, inner), LOW),
        ],
        compiler_params=params(),
        cost_estimate=cost(2 * length * inner * width, 4 * length * width),
        name="leave",
    )(table, att, packed)


def middle_kernel(table, own, other, part, far, vectors, middle, normed):
    mine = (pl.program_id(0) // 2) == table[2 * BLOCKS]
    tokens = jnp.where(mine, own[...], other[...])
    values = tokens + (part[...].astype(WIDE) + far[...].astype(WIDE))
    middle[...] = values
    hat, _ = hat_of(values)
    normed[...] = (hat * vectors[2:3, :] + vectors[3:4, :]).astype(LOW)


def second_norm(table, own, other, part, far, vectors):
    length, width = part.shape
    steps = length // ROWS
    pair = pl.BlockSpec((ROWS, width), lambda i, *_: (i % (steps // 2), 0))
    return pl.pallas_call(
        middle_kernel,
        grid_spec=pltpu.PrefetchScalarGridSpec(
            num_scalar_prefetch=1,
            grid=(steps,),
            in_specs=[pair, pair, by_row(width), by_row(width), fixed((8, width))],
            out_specs=[by_row(width), by_row(width)],
        ),
        out_shape=[
            jax.ShapeDtypeStruct((length, width), WIDE),
            jax.ShapeDtypeStruct((length, width), LOW),
        ],
        compiler_params=params(),
        cost_estimate=cost(20 * length * width, 18 * length * width),
        name="second_norm",
    )(table, own, other, part, far, vectors)


SIDE = 256


def feed_kernel(
    table,
    normed,
    grad_own,
    grad_other,
    up,
    down,
    branch,
    pulled,
    up_grad,
    down_grad,
    grad,
    normed_flip,
    grad_flip,
    up_whole,
    down_whole,
    act,
    pre,
    branch_sum,
    pulled_sum,
):
    step = pl.program_id(0)
    length = normed.shape[0]
    half = length // 2
    rows = up.shape[0] // BLOCKS

    @pl.when(step == 0)
    def _():
        mine = table[2 * BLOCKS]
        grad[pl.ds(pl.multiple_of(mine * half, half), half), :] = grad_own[...]
        grad[pl.ds(pl.multiple_of((1 - mine) * half, half), half), :] = grad_other[...]
        normed_flip[...] = normed[...].T
        grad_flip[...] = grad[...].T
        branch_sum[...] = jnp.zeros_like(branch_sum)
        pulled_sum[...] = jnp.zeros_like(pulled_sum)

    for j in range(BLOCKS):
        to = slice(j * rows, (j + 1) * rows)
        up_whole[to, :] = up[at_block(table, j, rows), :]
        down_whole[to, :] = down[at_block(table, BLOCKS + j, rows), :]

    for start in range(0, length, ROWS):
        at = slice(start, start + ROWS)
        wide = nn(normed[at, :], up_whole[...])
        square = wide * wide
        root = math.sqrt(2.0 / math.pi)
        bend = jnp.tanh(wide * (root + root * 0.044715 * square))
        share = 0.5 + 0.5 * bend
        slope = share + 0.5 * wide * (1.0 - bend * bend) * (
            root + 3.0 * root * 0.044715 * square
        )
        act[at, :] = (wide * share).astype(LOW)
        pre[at, :] = (nn(grad[at, :], down_whole[...]) * slope).astype(LOW)
        branch_sum[at, :] += nt(act[at, :], down_whole[...])
        pulled_sum[at, :] += nt(pre[at, :], up_whole[...])

    lifted = nn(normed_flip[...], pre[...]).astype(LOW)
    lowered = nn(grad_flip[...], act[...]).astype(LOW)
    for j in range(BLOCKS):
        take = slice(j * rows, (j + 1) * rows)
        up_grad[at_block(table, j, rows), :] = lifted[take]
        down_grad[at_block(table, BLOCKS + j, rows), :] = lowered[take]

    @pl.when(step == pl.num_programs(0) - 1)
    def _():
        branch[...] = branch_sum[...].astype(LOW)
        pulled[...] = pulled_sum[...].astype(LOW)


def feed(table, normed, grad_own, grad_other, packed, down):
    length, width = normed.shape
    hidden = down.shape[1]
    column = pl.BlockSpec((width, SIDE), lambda i, *_: (0, i))
    token = (length, width)
    return pl.pallas_call(
        feed_kernel,
        grid_spec=pltpu.PrefetchScalarGridSpec(
            num_scalar_prefetch=1,
            grid=(hidden // SIDE,),
            in_specs=[
                fixed(token),
                fixed(grad_own.shape),
                fixed(grad_other.shape),
                column,
                column,
            ],
            out_specs=[kept(token), kept(token), column, column],
            scratch_shapes=[
                pltpu.VMEM(token, LOW),
                pltpu.VMEM((width, length), LOW),
                pltpu.VMEM((width, length), LOW),
                pltpu.VMEM((width, SIDE), LOW),
                pltpu.VMEM((width, SIDE), LOW),
                pltpu.VMEM((length, SIDE), LOW),
                pltpu.VMEM((length, SIDE), LOW),
                pltpu.VMEM(token, WIDE),
                pltpu.VMEM(token, WIDE),
            ],
        ),
        out_shape=[
            jax.ShapeDtypeStruct(token, LOW),
            jax.ShapeDtypeStruct(token, LOW),
            jax.ShapeDtypeStruct((width, hidden), LOW),
            jax.ShapeDtypeStruct((width, hidden), LOW),
        ],
        compiler_params=params(),
        cost_estimate=cost(
            12 * length * width * hidden, 8 * length * width + 8 * width * hidden, length * hidden
        ),
        name="feed",
    )(table, normed, grad_own, grad_other, packed, down)


def middle_back_kernel(
    table,
    pulled,
    far,
    middle,
    grad_own,
    grad_other,
    vectors,
    out_whole,
    att,
    middle_grad,
    att_grad,
    out_grad,
    sums,
    out_sum,
):
    step = pl.program_id(0)
    rows = out_whole.shape[0] // BLOCKS

    @pl.when(step == 0)
    def _():
        out_sum[...] = jnp.zeros_like(out_sum)
        sums[...] = jnp.zeros_like(sums)

    mine = (step // 2) == table[2 * BLOCKS]
    grad = jnp.where(mine, grad_own[...].astype(WIDE), grad_other[...].astype(WIDE))
    pull = pulled[...].astype(WIDE) + far[...].astype(WIDE)
    hat, rate = hat_of(middle[...])
    whole = grad + norm_back(pull, hat, rate, vectors[2:3, :])
    middle_grad[...] = whole
    sums[0:1, :] += jnp.sum(pull * hat, axis=0, keepdims=True)
    sums[1:2, :] += jnp.sum(pull, axis=0, keepdims=True)
    low = whole.astype(LOW)
    att_grad[...] = nn(low, out_whole[...]).astype(LOW)
    out_sum[...] += tn(low, att[...])

    @pl.when(step == pl.num_programs(0) - 1)
    def _():
        for j in range(BLOCKS):
            out_grad[at_block(table, BLOCKS + j, rows), :] = out_sum[
                j * rows : (j + 1) * rows, :
            ].astype(LOW)


def middle_back(table, pulled, far, middle, grad_own, grad_other, vectors, out_whole, att):
    length, width = middle.shape
    inner = att.shape[1]
    steps = length // ROWS
    pair = pl.BlockSpec((ROWS, width), lambda i, *_: (i % (steps // 2), 0))
    return pl.pallas_call(
        middle_back_kernel,
        grid_spec=pltpu.PrefetchScalarGridSpec(
            num_scalar_prefetch=1,
            grid=(steps,),
            in_specs=[
                by_row(width),
                by_row(width),
                by_row(width),
                pair,
                pair,
                fixed((8, width)),
                fixed((width, inner)),
                by_row(inner),
            ],
            out_specs=[
                by_row(width),
                by_row(inner),
                kept((width, inner), (0, 1)),
                kept((8, width)),
            ],
            scratch_shapes=[pltpu.VMEM((width, inner), WIDE)],
        ),
        out_shape=[
            jax.ShapeDtypeStruct((length, width), WIDE),
            jax.ShapeDtypeStruct((length, inner), LOW),
            jax.ShapeDtypeStruct((width, 2 * inner), LOW),
            jax.ShapeDtypeStruct((8, width), WIDE),
        ],
        compiler_params=params(),
        cost_estimate=cost(4 * length * width * inner, 20 * length * width),
        name="middle_back",
    )(table, pulled, far, middle, grad_own, grad_other, vectors, out_whole, att)


def enter_back_kernel(
    table, proj_grad, normed, whole, held, pulled, left, right, normed_flip, pulled_sum
):
    step = pl.program_id(0)
    rows = normed.shape[1] // BLOCKS

    @pl.when(step == 0)
    def _():
        normed_flip[...] = normed[...].T
        pulled_sum[...] = jnp.zeros_like(pulled_sum)

    grad = proj_grad[0]
    weight = nn(normed_flip[...], grad).astype(LOW)

    @pl.when(step < 2)
    def _():
        for j in range(BLOCKS):
            left[at_block(table, j, rows), :] = weight[j * rows : (j + 1) * rows]

    @pl.when(step == 2)
    def _():
        for j in range(BLOCKS):
            right[at_block(table, BLOCKS + j, rows), :] = weight[j * rows : (j + 1) * rows]

    pulled_sum[...] += nt(grad, whole[...])

    @pl.when(step == 2)
    def _():
        pulled[...] = pulled_sum[...].astype(LOW)


def enter_back(table, proj_grad, normed, whole, held):
    length, width = normed.shape
    inner = proj_grad.shape[2]
    return pl.pallas_call(
        enter_back_kernel,
        grid_spec=pltpu.PrefetchScalarGridSpec(
            num_scalar_prefetch=1,
            grid=(3,),
            in_specs=[
                pl.BlockSpec((1, length, inner), lambda i, *_: (i, 0, 0)),
                fixed((length, width)),
                pl.BlockSpec((width, inner), lambda i, *_: (0, i)),
                pl.BlockSpec(memory_space=pl.ANY),
            ],
            out_specs=[
                kept((length, width)),
                pl.BlockSpec((width, inner), lambda i, *_: (0, jnp.minimum(i, 1))),
                kept((width, inner)),
            ],
            scratch_shapes=[pltpu.VMEM((width, length), LOW), pltpu.VMEM((length, width), WIDE)],
        ),
        out_shape=[
            jax.ShapeDtypeStruct((length, width), LOW),
            jax.ShapeDtypeStruct((width, 2 * inner), LOW),
            jax.ShapeDtypeStruct((width, 2 * inner), LOW),
        ],
        input_output_aliases={4: 2},
        compiler_params=params(),
        cost_estimate=cost(12 * length * width * inner, 8 * length * width),
        name="enter_back",
    )(table, proj_grad, normed, whole, held)


def exit_kernel(table, pulled, far, own, other, middle_grad, vectors, result, sums):
    step = pl.program_id(0)

    @pl.when(step == 0)
    def _():
        sums[...] = jnp.zeros_like(sums)

    mine = step >= pl.num_programs(0) // 2
    tokens = jnp.where(mine, own[...], other[...])
    pull = pulled[...].astype(WIDE) + far[...].astype(WIDE)
    hat, rate = hat_of(tokens)
    sums[0:1, :] += jnp.sum(pull * hat, axis=0, keepdims=True)
    sums[1:2, :] += jnp.sum(pull, axis=0, keepdims=True)
    result[...] = middle_grad[...] + norm_back(pull, hat, rate, vectors[0:1, :])


def leave_layer(table, pulled, far, own, other, middle_grad, vectors):
    length, width = pulled.shape
    steps = length // ROWS
    part = steps // 2
    pair = pl.BlockSpec((ROWS, width), lambda i, *_: (i % part, 0))

    def turned(i, places):
        return ((i + part * (1 - places[2 * BLOCKS])) % steps, 0)

    row = pl.BlockSpec((ROWS, width), turned)
    return pl.pallas_call(
        exit_kernel,
        grid_spec=pltpu.PrefetchScalarGridSpec(
            num_scalar_prefetch=1,
            grid=(steps,),
            in_specs=[row, row, pair, pair, row, fixed((8, width))],
            out_specs=[
                pl.BlockSpec((ROWS, width), lambda i, *_: (jnp.maximum(i - part, 0), 0)),
                kept((8, width)),
            ],
        ),
        out_shape=[
            jax.ShapeDtypeStruct((length // 2, width), WIDE),
            jax.ShapeDtypeStruct((8, width), WIDE),
        ],
        compiler_params=params(),
        cost_estimate=cost(20 * length * width, 18 * length * width),
        name="leave_layer",
    )(table, pulled, far, own, other, middle_grad, vectors)


def swap_cores(values):
    return lax.ppermute(values, "tensor", [(0, 1), (1, 0)])


def hop(values, bits, size):
    return lax.ppermute(values, "fsdp", [(i, i ^ bits) for i in range(size)])


def block_places(size, me, core):
    spots = jnp.arange(BLOCKS, dtype=jnp.int32)
    if size != BLOCKS:
        return jnp.concatenate([spots, spots, core[None]])
    away = me ^ spots
    low, mid, high = away & 1, (away >> 1) & 1, away >> 2
    return jnp.concatenate(
        [(low * 2 + mid) * 4 + high, (mid * 2 + low) * 4 + high, core[None]]
    )


def gather_rows(left, right, size):
    if size != BLOCKS:
        return tuple(lax.all_gather(v, "fsdp", axis=0, tiled=True) for v in (left, right))

    def far(values):
        parts = [values] + [hop(values, 4 * k, size) for k in range(1, 4)]
        return jnp.concatenate(parts, axis=0)

    left, right = far(left), far(right)
    for one, two in ((2, 1), (1, 2)):
        left, right = (
            jnp.concatenate([left, hop(left, one, size)], axis=0),
            jnp.concatenate([right, hop(right, two, size)], axis=0),
        )
    return left, right


def scatter_rows(left, right, size):
    if size != BLOCKS:
        return tuple(
            lax.psum_scatter(v.astype(WIDE), "fsdp", scatter_dimension=0, tiled=True)
            for v in (left, right)
        )

    def fold(values, bits):
        half = values.shape[0] // 2
        other = hop(values[half:], bits, size)
        return (values[:half].astype(WIDE) + other.astype(WIDE)).astype(LOW)

    for one, two in ((1, 2), (2, 1)):
        left, right = fold(left, one), fold(right, two)

    def near(values):
        rows = values.shape[0] // 4
        total = values[:rows].astype(WIDE)
        for k in range(1, 4):
            total = total + hop(values[k * rows : (k + 1) * rows], 4 * k, size).astype(WIDE)
        return total

    return near(left), near(right)


def sum_all(values, size):
    if size != BLOCKS:
        return lax.psum(values, "fsdp")
    for k in range(4):
        values = values + hop(values, 1 << k, size)
    return values


def body(
    size,
    inputs,
    segment_ids,
    qkv_weight,
    out_weight,
    up_weight,
    down_weight,
    gain_one,
    shift_one,
    gain_two,
    shift_two,
    cotangent,
):
    me = lax.axis_index("fsdp")
    core = lax.axis_index("tensor")
    rows, width = qkv_weight.shape[1:]
    half = inputs.shape[0]
    length = 2 * half
    table = block_places(size, me, core)

    first = jnp.concatenate(
        [
            qkv_weight.transpose(1, 0, 2).reshape(rows, 3 * width),
            jnp.stack([gain_one, shift_one, gain_two, shift_two], axis=1),
            jnp.zeros((rows, LANES - 4), WIDE),
        ],
        axis=1,
    ).astype(LOW)
    cut = (3 * width + LANES) // 2
    qkv_a, qkv_b = gather_rows(first[:, :cut], first[:, cut:], size)
    up_out, down = gather_rows(
        jnp.concatenate([up_weight, out_weight.T], axis=1).astype(LOW),
        down_weight.T.astype(LOW),
        size,
    )
    other = swap_cores(inputs)
    grad_other = swap_cores(cotangent)
    seg_col = jnp.broadcast_to(segment_ids[:, None], (length, LANES))
    seg_row = jnp.broadcast_to(segment_ids[None, :], (8, length))

    normed_one, proj, qkv_whole, vectors = enter(table, inputs, other, qkv_a, qkv_b)
    att, lse = attend(proj, seg_col, seg_row)
    part, out_whole = leave(table, att, up_out)
    middle, normed_two = second_norm(table, inputs, other, part, swap_cores(part), vectors)
    branch, pulled, up_part, down_part = feed(
        table, normed_two, cotangent, grad_other, up_out, down
    )
    up_grad, down_grad = scatter_rows(up_part, down_part, size)

    def own_half(values):
        return lax.dynamic_slice_in_dim(values, core * half, half, 0)

    far = swap_cores(lax.dynamic_slice_in_dim(branch, (1 - core) * half, half, 0))
    outputs = own_half(middle) + (own_half(branch).astype(WIDE) + far.astype(WIDE))

    middle_grad, att_grad, held, sums_two = middle_back(
        table, pulled, swap_cores(pulled), middle, cotangent, grad_other, vectors, out_whole, att
    )
    proj_grad = attend_back(proj, att, att_grad, lse, seg_col, seg_row)
    pulled, left, right = enter_back(table, proj_grad, normed_one, qkv_whole, held)
    tail_a, tail_b = scatter_rows(left, right, size)
    input_grad, sums_one = leave_layer(
        table, pulled, swap_cores(pulled), inputs, other, middle_grad, vectors
    )
    sums = sum_all(jnp.concatenate([sums_one[:2], sums_two[:2]], axis=0), size)
    sums = lax.dynamic_slice_in_dim(sums, me * rows, rows, 1)
    qkv_grad = jnp.stack([tail_a[:, :width], tail_a[:, width:], tail_b[:, :width]], axis=0)
    return (
        outputs,
        input_grad,
        qkv_grad,
        tail_b[:, width:].T,
        up_grad,
        down_grad.T,
        sums[0],
        sums[1],
        sums[2],
        sums[3],
    )


def solution(mesh):
    tokens = P(("fsdp", "tensor"), None)
    split = P("fsdp")
    weights = (
        P(None, "fsdp", "tensor"),
        P("tensor", "fsdp"),
        P("fsdp", "tensor"),
        P("tensor", "fsdp"),
        split,
        split,
        split,
        split,
    )
    return jax.shard_map(
        functools.partial(body, mesh.shape["fsdp"]),
        mesh=mesh,
        in_specs=(tokens, split) + weights + (tokens,),
        out_specs=(tokens, tokens) + weights,
        check_vma=False,
    )
```

profile of v0, /device:TPU:0, one launch (start us, length us, event | category | flops | bytes accessed | tf_op | source)
XLA Modules:
  0.0 367.9 jit_solution(10435405313301298176)
XLA Ops:
  2.3 3.0 collective-permute-start.18
  13.2 3.9 %collective-permute-start.8 = (bf16[48,640]{1,0:T(8,128)(2,1)S(1)}, bf16[48,640]{1,0:T(8,128)(2,1)S(1)}, u32[]{:S(2)}, u32[]{:S(2)}) collective-permute-start(bf16[48,640]{1,0:T(8,128)(2,1)S(1)} %get-tuple-element.99), channel_id=1, source_target_pairs={{0,24},{2,26},{4,28},{6,30},{8,16},{10,18},{12,20},{14,22},{16,8},... | collective-permute-start | bytes 184328 | tf_op jit(solution)/shard_map/ppermute | solution.py:656
  24.0 4.6 %collective-permute-done.1 = bf16[48,640]{1,0:T(8,128)(2,1)S(1)} collective-permute-done((bf16[48,640]{1,0:T(8,128)(2,1)S(1)}, bf16[48,640]{1,0:T(8,128)(2,1)S(1)}, u32[]{:S(2)}, u32[]{:S(2)}) %collective-permute-start.1) | collective-permute-done | bytes 61472 | tf_op jit(solution)/shard_map/ppermute | solution.py:656
  30.8 3.0 collective-permute-done.2
  33.7 3.4 collective-permute-start.3
  39.9 4.1 %collective-permute-start.13 = (bf16[48,1920]{1,0:T(8,128)(2,1)S(1)}, bf16[48,1920]{1,0:T(8,128)(2,1)S(1)}, u32[]{:S(2)}, u32[]{:S(2)}) collective-permute-start(bf16[48,1920]{1,0:T(8,128)(2,1)S(1)} %get-tuple-element.86), channel_id=1, source_target_pairs={{0,24},{2,26},{4,28},{6,30},{8,16},{10,18},{12,20},{14,22},{16,8},... | collective-permute-start | bytes 552968 | tf_op jit(solution)/shard_map/ppermute | solution.py:656
  57.2 13.7 %collective-permute-done.14 = bf16[192,1920]{1,0:T(8,128)(2,1)S(1)} collective-permute-done((bf16[192,1920]{1,0:T(8,128)(2,1)S(1)}, bf16[192,1920]{1,0:T(8,128)(2,1)S(1)}, u32[]{:S(2)}, u32[]{:S(2)}) %collective-permute-start.14) | collective-permute-done | bytes 737312 | tf_op jit(solution)/shard_map/ppermute | solution.py:656
  79.7 4.6 %collective-permute-done.10 = bf16[384,640]{1,0:T(8,128)(2,1)S(1)} collective-permute-done((bf16[384,640]{1,0:T(8,128)(2,1)S(1)}, bf16[384,640]{1,0:T(8,128)(2,1)S(1)}, u32[]{:S(2)}, u32[]{:S(2)}) %collective-permute-start.10) | collective-permute-done | bytes 491552 | tf_op jit(solution)/shard_map/ppermute | solution.py:656
  84.4 29.5 %collective-permute-done.5 = bf16[384,640]{1,0:T(8,128)(2,1)S(1)} collective-permute-done((bf16[384,640]{1,0:T(8,128)(2,1)S(1)}, bf16[384,640]{1,0:T(8,128)(2,1)S(1)}, u32[]{:S(2)}, u32[]{:S(2)}) %collective-permute-start.5) | collective-permute-done | bytes 491552 | tf_op jit(solution)/shard_map/ppermute | solution.py:656
  116.1 8.4 %enter.1 = (bf16[1024,768]{1,0:T(8,128)(2,1)}, bf16[1024,1152]{1,0:T(8,128)(2,1)}, bf16[768,1152]{1,0:T(8,128)(2,1)}, f32[8,768]{1,0:T(8,128)}) custom-call(s32[33]{0:T(128)} %pad_add_fusion.table, f32[512,768]{1,0:T(8,128)} %own.5, f32[512,768]{1,0:T(8,128)} %copy-done.2, bf16[768,640]{1,0:T(8,128)(2,1)} %copy-done.23, bf16[768,640]{1,0:T(8,128)(2,1)} %copy-done.25), custom_call_target="tpu_custom_call" | custom-call | flops 1811939328 | bytes 4718592 | tf_op jit(solution)/shard_map/enter/pallas_call | solution.py:106
  126.1 14.8 %attend.1 = (bf16[1024,384]{1,0:T(8,128)(2,1)}, f32[24,1024]{1,0:T(8,128)}) custom-call(bf16[1024,1152]{1,0:T(8,128)(2,1)} %get-tuple-element.33.queries.keys.values, bf16[1024,1152]{1,0:T(8,128)(2,1)} %get-tuple-element.33.queries.keys.values, bf16[1024,1152]{1,0:T(8,128)(2,1)} %get-tuple-element.33.queries.keys.values, ...), custom_call_target="tpu_custom_call" | custom-call | flops 3221225472 | bytes 3145728 | tf_op jit(solution)/shard_map/attend/pallas_call | solution.py:180
  144.1 5.3 %leave.1 = (bf16[1024,768]{1,0:T(8,128)(2,1)}, bf16[768,384]{1,0:T(8,128)(2,1)}) custom-call(s32[33]{0:T(128)} %pad_add_fusion.table, bf16[1024,384]{1,0:T(8,128)(2,1)} %get-tuple-element.34.att.out, bf16[768,1920]{1,0:T(8,128)(2,1)} %copy-done.5), custom_call_target="tpu_custom_call" | custom-call | flops 603979776 | bytes 3145728 | tf_op jit(solution)/shard_map/leave/pallas_call | solution.py:291
  154.2 26.8 %collective-permute-done.22 = bf16[384,1536]{1,0:T(8,128)(2,1)S(1)} collective-permute-done((bf16[384,1536]{1,0:T(8,128)(2,1)}, bf16[384,1536]{1,0:T(8,128)(2,1)S(1)}, u32[]{:S(2)}, u32[]{:S(2)}) %collective-permute-start.22) | collective-permute-done | bytes 1179680 | tf_op jit(solution)/shard_map/ppermute | solution.py:656
  183.3 7.2 %second_norm.1 = (f32[1024,768]{1,0:T(8,128)}, bf16[1024,768]{1,0:T(8,128)(2,1)}) custom-call(s32[33]{0:T(128)} %pad_add_fusion.table, f32[512,768]{1,0:T(8,128)} %own.5, f32[512,768]{1,0:T(8,128)} %copy-done.2, bf16[1024,768]{1,0:T(8,128)(2,1)} %get-tuple-element.35.part, bf16[1024,768]{1,0:T(8,128)(2,1)} %copy-done.9, f32[8,768]{1,0:T(8,128)} %get-tuple-element.36.vectors), custom_call_target="tpu_custom_call" | custom-call | flops 15728640 | bytes 14155776 | tf_op jit(solution)/shard_map/second_norm/pallas_call | solution.py:322
  190.5 26.9 %feed.1 = (bf16[1024,768]{1,0:T(8,128)(2,1)}, bf16[1024,768]{1,0:T(8,128)(2,1)}, bf16[768,1536]{1,0:T(8,128)(2,1)}, bf16[768,1536]{1,0:T(8,128)(2,1)}) custom-call(s32[33]{0:T(128)} %pad_add_fusion.table, bf16[1024,768]{1,0:T(8,128)(2,1)} %get-tuple-element.38.normed, bf16[512,768]{1,0:T(8,128)(2,1)} %grad_own.3, ...), custom_call_target="tpu_custom_call" | custom-call | flops 14495514624 | bytes 15728640 | tf_op jit(solution)/shard_map/feed/pallas_call | solution.py:417
  229.1 18.6 %collective-permute-done.41 = bf16[384,1536]{1,0:T(8,128)(2,1)} collective-permute-done((bf16[384,1536]{1,0:T(8,128)(2,1)}, bf16[384,1536]{1,0:T(8,128)(2,1)}, u32[]{:S(2)}, u32[]{:S(2)}) %collective-permute-start.41) | collective-permute-done | bytes 1179680 | tf_op jit(solution)/shard_map/ppermute | solution.py:656
  250.7 3.2 collective-permute-done.36
  256.8 10.0 %middle_back.1 = (f32[1024,768]{1,0:T(8,128)}, bf16[1024,384]{1,0:T(8,128)(2,1)}, bf16[768,768]{1,0:T(8,128)(2,1)}, f32[8,768]{1,0:T(8,128)}) custom-call(s32[33]{0:T(128)} %pad_add_fusion.table, bf16[1024,768]{1,0:T(8,128)(2,1)} %get-tuple-element.40.pulled, bf16[1024,768]{1,0:T(8,128)(2,1)} %collective-permute-done.24.far, ...), custom_call_target="tpu_custom_call" | custom-call | flops 1207959552 | bytes 15728640 | tf_op jit(solution)/shard_map/middle_back/pallas_call | solution.py:505
  266.8 15.5 %attend_back.1.proj_grad = bf16[3,1024,384]{2,1,0:T(8,128)(2,1)} custom-call(bf16[1024,1152]{1,0:T(8,128)(2,1)} %get-tuple-element.33.queries.keys.values, bf16[1024,1152]{1,0:T(8,128)(2,1)} %get-tuple-element.33.queries.keys.values, bf16[1024,1152]{1,0:T(8,128)(2,1)} %get-tuple-element.33.queries.keys.values, bf16[1024,384]{1,0:T(8,128)(2,1)} %get-tuple-element.34.att.out, ...), custom_call_target="tpu_custom_call" | custom-call | flops 8053063680 | bytes 6291456 | tf_op jit(solution)/shard_map/attend_back/pallas_call | solution.py:246
  282.3 11.3 %enter_back.1 = (bf16[1024,768]{1,0:T(8,128)(2,1)}, bf16[768,768]{1,0:T(8,128)(2,1)}, bf16[768,768]{1,0:T(8,128)(2,1)}) custom-call(s32[33]{0:T(128)} %pad_add_fusion.table, bf16[3,1024,384]{2,1,0:T(8,128)(2,1)} %attend_back.1.proj_grad, bf16[1024,768]{1,0:T(8,128)(2,1)} %get-tuple-element.44.normed, ...), custom_call_target="tpu_custom_call", output_to_operand_aliasing={{2}: (4, {})} | custom-call | flops 3623878656 | bytes 6291456 | tf_op jit(solution)/shard_map/enter_back/pallas_call | solution.py:574
  307.1 5.9 %collective-permute-done.44 = bf16[48,1536]{1,0:T(8,128)(2,1)S(1)} collective-permute-done((bf16[48,1536]{1,0:T(8,128)(2,1)S(1)}, bf16[48,1536]{1,0:T(8,128)(2,1)S(1)}, u32[]{:S(2)}, u32[]{:S(2)}) %collective-permute-start.44) | collective-permute-done | bytes 147488 | tf_op jit(solution)/shard_map/ppermute | solution.py:656
  320.7 6.2 %collective-permute-done.39 = bf16[48,1536]{1,0:T(8,128)(2,1)S(1)} collective-permute-done((bf16[48,1536]{1,0:T(8,128)(2,1)S(1)}, bf16[48,1536]{1,0:T(8,128)(2,1)S(1)}, u32[]{:S(2)}, u32[]{:S(2)}) %collective-permute-start.39) | collective-permute-done | bytes 147488 | tf_op jit(solution)/shard_map/ppermute | solution.py:656
  334.8 3.0 collective-permute-start.33
  342.0 7.9 %leave_layer.1 = (f32[512,768]{1,0:T(8,128)}, f32[8,768]{1,0:T(8,128)}) custom-call(s32[33]{0:T(128)} %pad_add_fusion.table, bf16[1024,768]{1,0:T(8,128)(2,1)} %get-tuple-element.47.pulled, bf16[1024,768]{1,0:T(8,128)(2,1)} %copy-done.10, f32[512,768]{1,0:T(8,128)} %own.5, f32[512,768]{1,0:T(8,128)} %copy-done.2, f32[1024,768]{1,0:T(8,128)} %get-tuple-element.48.middle_grad, ...), custom_call_target="tpu_custom_call" | custom-call | flops 15728640 | bytes 14155776 | tf_op jit(solution)/shard_map/leave_layer/pallas_call | solution.py:630
  (221 shorter events, 126.0 us)
Async XLA Ops:
  2.3 46.8 %collective-permute-start.18 = (bf16[48,1536]{1,0:T(8,128)(2,1)S(1)}, bf16[48,1536]{1,0:T(8,128)(2,1)}, u32[]{:S(2)}, u32[]{:S(2)}) collective-permute-start(bf16[48,1536]{1,0:T(8,128)(2,1)S(1)} %get-tuple-element.57), channel_id=1, source_target_pairs={{0,8},{2,10},{4,12},{6,14},{8,0},{10,2},{12,4},{14,6},{16,24},{18,... | collective-permute-start | bytes 442376 | tf_op jit(solution)/shard_map/ppermute | solution.py:656
  5.4 45.4 %collective-permute-start.19 = (bf16[48,1536]{1,0:T(8,128)(2,1)S(1)}, bf16[48,1536]{1,0:T(8,128)(2,1)}, u32[]{:S(2)}, u32[]{:S(2)}) collective-permute-start(bf16[48,1536]{1,0:T(8,128)(2,1)S(1)} %get-tuple-element.57), channel_id=1, source_target_pairs={{0,16},{2,18},{4,20},{6,22},{8,24},{10,26},{12,28},{14,30},{16,0},... | collective-permute-start | bytes 442376 | tf_op jit(solution)/shard_map/ppermute | solution.py:656
  19.9 24.8 %collective-permute-start.11 = (bf16[48,1920]{1,0:T(8,128)(2,1)S(1)}, bf16[48,1920]{1,0:T(8,128)(2,1)S(1)}, u32[]{:S(2)}, u32[]{:S(2)}) collective-permute-start(bf16[48,1920]{1,0:T(8,128)(2,1)S(1)} %get-tuple-element.86), channel_id=1, source_target_pairs={{0,8},{2,10},{4,12},{6,14},{8,0},{10,2},{12,4},{14,6},{16,24},{18,... | collective-permute-start | bytes 552968 | tf_op jit(solution)/shard_map/ppermute | solution.py:656
  20.5 24.8 %collective-permute-start.12 = (bf16[48,1920]{1,0:T(8,128)(2,1)S(1)}, bf16[48,1920]{1,0:T(8,128)(2,1)S(1)}, u32[]{:S(2)}, u32[]{:S(2)}) collective-permute-start(bf16[48,1920]{1,0:T(8,128)(2,1)S(1)} %get-tuple-element.86), channel_id=1, source_target_pairs={{0,16},{2,18},{4,20},{6,22},{8,24},{10,26},{12,28},{14,30},{16,0},... | collective-permute-start | bytes 552968 | tf_op jit(solution)/shard_map/ppermute | solution.py:656
  45.4 69.6 %collective-permute-start = (f32[512,768]{1,0:T(8,128)S(1)}, f32[512,768]{1,0:T(8,128)S(1)}, u32[]{:S(2)}, u32[]{:S(2)}) collective-permute-start(f32[512,768]{1,0:T(8,128)S(1)} %copy-done.1), channel_id=1, source_target_pairs={{0,1},{1,0},{2,3},{3,2},{4,5},{5,4},{6,7},{7,6},{8,9},{9,8},{10,11... | collective-permute-start | bytes 4718600 | tf_op jit(solution)/shard_map/ppermute | solution.py:652
  47.6 26.6 %collective-permute-start.9 = (bf16[192,640]{1,0:T(8,128)(2,1)S(1)}, bf16[192,640]{1,0:T(8,128)(2,1)S(1)}, u32[]{:S(2)}, u32[]{:S(2)}) collective-permute-start(bf16[192,640]{1,0:T(8,128)(2,1)S(1)} %pad_maximum_fusion.3), channel_id=1, source_target_pairs={{0,2},{2,0},{4,6},{6,4},{8,10},{10,8},{12,14},{14,12},{16,18},{18,... | collective-permute-start | bytes 737288 | tf_op jit(solution)/shard_map/ppermute | solution.py:656
  49.2 26.7 %collective-permute-start.4 = (bf16[192,640]{1,0:T(8,128)(2,1)S(1)}, bf16[192,640]{1,0:T(8,128)(2,1)S(1)}, u32[]{:S(2)}, u32[]{:S(2)}) collective-permute-start(bf16[192,640]{1,0:T(8,128)(2,1)S(1)} %pad_maximum_fusion.2), channel_id=1, source_target_pairs={{0,4},{2,6},{4,0},{6,2},{8,12},{10,14},{12,8},{14,10},{16,20},{18,... | collective-permute-start | bytes 737288 | tf_op jit(solution)/shard_map/ppermute | solution.py:656
  50.7 20.2 %collective-permute-start.14 = (bf16[192,1920]{1,0:T(8,128)(2,1)S(1)}, bf16[192,1920]{1,0:T(8,128)(2,1)S(1)}, u32[]{:S(2)}, u32[]{:S(2)}) collective-permute-start(bf16[192,1920]{1,0:T(8,128)(2,1)S(1)} %pad_maximum_fusion), channel_id=1, source_target_pairs={{0,4},{2,6},{4,0},{6,2},{8,12},{10,14},{12,8},{14,10},{16,20},{18,... | collective-permute-start | bytes 2211848 | tf_op jit(solution)/shard_map/ppermute | solution.py:656
  53.6 95.8 %collective-permute-start.21 = (bf16[192,1536]{1,0:T(8,128)(2,1)}, bf16[192,1536]{1,0:T(8,128)(2,1)}, u32[]{:S(2)}, u32[]{:S(2)}) collective-permute-start(bf16[192,1536]{1,0:T(8,128)(2,1)} %pad_maximum_fusion.1), channel_id=1, source_target_pairs={{0,2},{2,0},{4,6},{6,4},{8,10},{10,8},{12,14},{14,12},{16,18},{18,... | collective-permute-start | bytes 1769480 | tf_op jit(solution)/shard_map/ppermute | solution.py:656
  71.9 69.0 %collective-permute-start.15 = (bf16[384,1920]{1,0:T(8,128)(2,1)}, bf16[384,1920]{1,0:T(8,128)(2,1)}, u32[]{:S(2)}, u32[]{:S(2)}) collective-permute-start(bf16[384,1920]{1,0:T(8,128)(2,1)} %get-tuple-element.58), channel_id=1, source_target_pairs={{0,2},{2,0},{4,6},{6,4},{8,10},{10,8},{12,14},{14,12},{16,18},{18,... | collective-permute-start | bytes 4423688 | tf_op jit(solution)/shard_map/ppermute | solution.py:656
  76.0 38.0 %collective-permute-start.5 = (bf16[384,640]{1,0:T(8,128)(2,1)S(1)}, bf16[384,640]{1,0:T(8,128)(2,1)S(1)}, u32[]{:S(2)}, u32[]{:S(2)}) collective-permute-start(bf16[384,640]{1,0:T(8,128)(2,1)S(1)} %get-tuple-element.76), channel_id=1, source_target_pairs={{0,2},{2,0},{4,6},{6,4},{8,10},{10,8},{12,14},{14,12},{16,18},{18,... | collective-permute-start | bytes 1474568 | tf_op jit(solution)/shard_map/ppermute | solution.py:656
  149.4 32.8 %collective-permute-start.16 = (bf16[1024,768]{1,0:T(8,128)(2,1)}, bf16[1024,768]{1,0:T(8,128)(2,1)S(1)}, u32[]{:S(2)}, u32[]{:S(2)}) collective-permute-start(bf16[1024,768]{1,0:T(8,128)(2,1)} %get-tuple-element.35.part), channel_id=1, source_target_pairs={{0,1},{1,0},{2,3},{3,2},{4,5},{5,4},{6,7},{7,6},{8,9},{9,8},{10,11... | collective-permute-start | bytes 4718600 | tf_op jit(solution)/shard_map/ppermute | solution.py:652
  152.5 28.5 %collective-permute-start.22 = (bf16[384,1536]{1,0:T(8,128)(2,1)}, bf16[384,1536]{1,0:T(8,128)(2,1)S(1)}, u32[]{:S(2)}, u32[]{:S(2)}) collective-permute-start(bf16[384,1536]{1,0:T(8,128)(2,1)} %copy-done.17), channel_id=1, source_target_pairs={{0,4},{2,6},{4,0},{6,2},{8,12},{10,14},{12,8},{14,10},{16,20},{18,... | collective-permute-start | bytes 3538952 | tf_op jit(solution)/shard_map/ppermute | solution.py:656
  154.0 36.4 %collective-permute-start.17 = (bf16[512,768]{1,0:T(8,128)(2,1)S(1)}, bf16[512,768]{1,0:T(8,128)(2,1)}, u32[]{:S(2)}, u32[]{:S(2)}) collective-permute-start(bf16[512,768]{1,0:T(8,128)(2,1)S(1)} %copy-done.13), channel_id=1, source_target_pairs={{0,1},{1,0},{2,3},{3,2},{4,5},{5,4},{6,7},{7,6},{8,9},{9,8},{10,11... | collective-permute-start | bytes 2359304 | tf_op jit(solution)/shard_map/ppermute | solution.py:652
  219.9 27.8 %collective-permute-start.41 = (bf16[384,1536]{1,0:T(8,128)(2,1)}, bf16[384,1536]{1,0:T(8,128)(2,1)}, u32[]{:S(2)}, u32[]{:S(2)}) collective-permute-start(bf16[384,1536]{1,0:T(8,128)(2,1)} %slice.164), channel_id=1, source_target_pairs={{0,4},{2,6},{4,0},{6,2},{8,12},{10,14},{12,8},{14,10},{16,20},{18,... | collective-permute-start | bytes 3538952 | tf_op jit(solution)/shard_map/ppermute | solution.py:656
  224.8 29.1 %collective-permute-start.36 = (bf16[384,1536]{1,0:T(8,128)(2,1)}, bf16[384,1536]{1,0:T(8,128)(2,1)}, u32[]{:S(2)}, u32[]{:S(2)}) collective-permute-start(bf16[384,1536]{1,0:T(8,128)(2,1)} %slice.156), channel_id=1, source_target_pairs={{0,2},{2,0},{4,6},{6,4},{8,10},{10,8},{12,14},{14,12},{16,18},{18,... | collective-permute-start | bytes 3538952 | tf_op jit(solution)/shard_map/ppermute | solution.py:656
  225.3 31.5 %collective-permute-start.24 = (bf16[1024,768]{1,0:T(8,128)(2,1)}, bf16[1024,768]{1,0:T(8,128)(2,1)}, u32[]{:S(2)}, u32[]{:S(2)}) collective-permute-start(bf16[1024,768]{1,0:T(8,128)(2,1)} %get-tuple-element.40.pulled), channel_id=1, source_target_pairs={{0,1},{1,0},{2,3},{3,2},{4,5},{5,4},{6,7},{7,6},{8,9},{9,8},{10,11... | collective-permute-start | bytes 4718600 | tf_op jit(solution)/shard_map/ppermute | solution.py:652
  250.1 46.1 %collective-permute-start.42 = (bf16[192,1536]{1,0:T(8,128)(2,1)}, bf16[192,1536]{1,0:T(8,128)(2,1)}, u32[]{:S(2)}, u32[]{:S(2)}) collective-permute-start(bf16[192,1536]{1,0:T(8,128)(2,1)} %slice.202), channel_id=1, source_target_pairs={{0,2},{2,0},{4,6},{6,4},{8,10},{10,8},{12,14},{14,12},{16,18},{18,... | collective-permute-start | bytes 1769480 | tf_op jit(solution)/shard_map/ppermute | solution.py:656
  256.3 44.5 %collective-permute-start.37 = (bf16[192,1536]{1,0:T(8,128)(2,1)}, bf16[192,1536]{1,0:T(8,128)(2,1)}, u32[]{:S(2)}, u32[]{:S(2)}) collective-permute-start(bf16[192,1536]{1,0:T(8,128)(2,1)} %slice.196), channel_id=1, source_target_pairs={{0,4},{2,6},{4,0},{6,2},{8,12},{10,14},{12,8},{14,10},{16,20},{18,... | collective-permute-start | bytes 1769480 | tf_op jit(solution)/shard_map/ppermute | solution.py:656
  293.6 47.2 %collective-permute-start.25 = (bf16[1024,768]{1,0:T(8,128)(2,1)}, bf16[1024,768]{1,0:T(8,128)(2,1)S(1)}, u32[]{:S(2)}, u32[]{:S(2)}) collective-permute-start(bf16[1024,768]{1,0:T(8,128)(2,1)} %get-tuple-element.47.pulled), channel_id=1, source_target_pairs={{0,1},{1,0},{2,3},{3,2},{4,5},{5,4},{6,7},{7,6},{8,9},{9,8},{10,11... | collective-permute-start | bytes 4718600 | tf_op jit(solution)/shard_map/ppermute | solution.py:652
  295.6 20.9 %collective-permute-start.26 = (bf16[384,768]{1,0:T(8,128)(2,1)S(1)}, bf16[384,768]{1,0:T(8,128)(2,1)S(1)}, u32[]{:S(2)}, u32[]{:S(2)}) collective-permute-start(bf16[384,768]{1,0:T(8,128)(2,1)S(1)} %slice.136), channel_id=1, source_target_pairs={{0,2},{2,0},{4,6},{6,4},{8,10},{10,8},{12,14},{14,12},{16,18},{18,... | collective-permute-start | bytes 1769480 | tf_op jit(solution)/shard_map/ppermute | solution.py:656
  305.6 22.1 %collective-permute-start.31 = (bf16[384,768]{1,0:T(8,128)(2,1)S(1)}, bf16[384,768]{1,0:T(8,128)(2,1)S(1)}, u32[]{:S(2)}, u32[]{:S(2)}) collective-permute-start(bf16[384,768]{1,0:T(8,128)(2,1)S(1)} %slice.146), channel_id=1, source_target_pairs={{0,4},{2,6},{4,0},{6,2},{8,12},{10,14},{12,8},{14,10},{16,20},{18,... | collective-permute-start | bytes 1769480 | tf_op jit(solution)/shard_map/ppermute | solution.py:656
  334.8 17.2 %collective-permute-start.33 = (bf16[48,768]{1,0:T(8,128)(2,1)S(1)}, bf16[48,768]{1,0:T(8,128)(2,1)S(1)}, u32[]{:S(2)}, u32[]{:S(2)}) collective-permute-start(bf16[48,768]{1,0:T(8,128)(2,1)S(1)} %get-tuple-element.71), channel_id=1, source_target_pairs={{0,8},{2,10},{4,12},{6,14},{8,0},{10,2},{12,4},{14,6},{16,24},{18,... | collective-permute-start | bytes 221192 | tf_op jit(solution)/shard_map/ppermute | solution.py:656
  337.8 14.1 %collective-permute-start.34 = (bf16[48,768]{1,0:T(8,128)(2,1)S(1)}, bf16[48,768]{1,0:T(8,128)(2,1)S(1)}, u32[]{:S(2)}, u32[]{:S(2)}) collective-permute-start(bf16[48,768]{1,0:T(8,128)(2,1)S(1)} %get-tuple-element.73), channel_id=1, source_target_pairs={{0,16},{2,18},{4,20},{6,22},{8,24},{10,26},{12,28},{14,30},{16,0},... | collective-permute-start | bytes 221192 | tf_op jit(solution)/shard_map/ppermute | solution.py:656
  (52 other events, 504.3 us)
where the time goes:
time: 369 us; the launch traced here: 368 us
  waiting for transfers between devices  135 us (37%)
  Pallas kernels  107 us (29%)
  starting transfers between devices  64.7 us (18%)
  local copies, waits for them, and re-layouts  39.6 us (11%)
  other arithmetic  19.9 us (5%)
    ppermute x44, waiting for transfers between devices, hop(): return lax.ppermute(values, 'fsdp', [(i, i ^ bits) for i in range(size)])  135 us
    ppermute x44, starting transfers between devices, hop(): return lax.ppermute(values, 'fsdp', [(i, i ^ bits) for i in range(size)])  64.2 us
    pallas_call x1, Pallas kernels, feed(): pl.pallas_call(feed_kernel, grid_spec=pltpu.PrefetchScalarGridSpec(num_sc...  26.9 us
    unnamed x67, local copies, waits for them, and re-layouts  19.9 us
    pallas_call x1, Pallas kernels, attend_back(): pl.pallas_call(attend_back_kernel, grid=(pairs,), in_specs=[part(0), part...  15.5 us
    pallas_call x1, Pallas kernels, attend(): pl.pallas_call(attend_kernel, grid=(pairs,), in_specs=[part(0), part(1),...  14.8 us
    pallas_call x1, Pallas kernels, enter_back(): pl.pallas_call(enter_back_kernel, grid_spec=pltpu.PrefetchScalarGridSpec(...  11.3 us
    pallas_call x1, Pallas kernels, middle_back(): pl.pallas_call(middle_back_kernel, grid_spec=pltpu.PrefetchScalarGridSpec...  10 us
  transfers between devices with their start and end apart: 50, of which 22 were waited for; matrix products, arithmetic and copies ran while one was open for 13% of the time, Pallas kernels for 22%

commit v1 on v0

v1 whole, which is shorter than its diff:
```python
import functools
import math

import jax
import jax.numpy as jnp
from jax import lax
from jax.experimental import pallas as pl
from jax.experimental.pallas import tpu as pltpu
from jax.sharding import PartitionSpec as P

HD = 64
EPS = 1e-05
LOW = jnp.bfloat16
WIDE = jnp.float32
BLOCKS = 16
ROWS = 256
LANES = 128
LOG2E = math.log2(math.e)
LEFT, RIGHT, DOWN_LEFT, DOWN_RIGHT = (BLOCKS * k for k in range(4))
MASKED = -1e30


def nn(a, b):
    return jnp.dot(a, b, preferred_element_type=WIDE)


def nt(a, b):
    return lax.dot_general(a, b, (((1,), (1,)), ((), ())), preferred_element_type=WIDE)


def tn(a, b):
    return lax.dot_general(a, b, (((0,), (0,)), ((), ())), preferred_element_type=WIDE)


LONG = pl.CostEstimate(flops=10**13, bytes_accessed=10**9, transcendentals=0)


def params():
    return pltpu.CompilerParams(
        dimension_semantics=("arbitrary",), vmem_limit_bytes=60 * 1024 * 1024
    )


def fixed(shape, index=None):
    place = index or (0,) * len(shape)
    return pl.BlockSpec(shape, lambda i, *_: place, pipeline_mode=pl.Buffered(1))


def kept(shape, index=None):
    place = index or (0,) * len(shape)
    return pl.BlockSpec(shape, lambda i, *_: place)


def by_row(width, rows=ROWS):
    return pl.BlockSpec((rows, width), lambda i, *_: (i, 0))


def hat_of(values):
    centre = values - jnp.mean(values, axis=-1, keepdims=True)
    rate = lax.rsqrt(jnp.mean(centre * centre, axis=-1, keepdims=True) + EPS)
    return centre * rate, rate


def norm_back(grad, hat, rate, gain):
    scaled = grad * gain
    return rate * (
        scaled
        - jnp.mean(scaled, axis=-1, keepdims=True)
        - hat * jnp.mean(scaled * hat, axis=-1, keepdims=True)
    )


def take(table, entry, rows, near, far, lanes=slice(None)):
    place = table[entry]
    at = pl.ds(pl.multiple_of((place % (BLOCKS // 2)) * rows, 16), rows)
    return jnp.where(place < BLOCKS // 2, near[at, lanes], far[at, lanes])


def put(table, entry, rows, keep, send, values):
    place = table[entry]
    at = pl.ds(pl.multiple_of((place % (BLOCKS // 2)) * rows, 16), rows)

    @pl.when(place < BLOCKS // 2)
    def _():
        keep[at, :] = values

    @pl.when(place >= BLOCKS // 2)
    def _():
        send[at, :] = values


def enter_kernel(table, tokens, wa, wa2, wb, wb2, normed, proj, whole, vectors, loose):
    step = pl.program_id(0)
    rows = wa.shape[0] // (BLOCKS // 2)
    cut = wa.shape[1]
    rest = whole.shape[1] - cut

    @pl.when(step == 0)
    def _():
        for j in range(BLOCKS):
            to = slice(j * rows, (j + 1) * rows)
            whole[to, :cut] = take(table, LEFT + j, rows, wa, wa2)
            late = take(table, RIGHT + j, rows, wb, wb2)
            whole[to, cut:] = late[:, :rest]
            loose[to, :] = late[:, rest:].astype(WIDE)
        vectors[...] = loose[...].T[:8]

    hat, _ = hat_of(tokens[...])
    low = (hat * vectors[0:1, :] + vectors[1:2, :]).astype(LOW)
    normed[...] = low
    proj[...] = nn(low, whole[...]).astype(LOW)


def enter(table, tokens, *pieces):
    length, width = tokens.shape
    total = pieces[0].shape[1] + pieces[2].shape[1] - LANES
    return pl.pallas_call(
        enter_kernel,
        grid_spec=pltpu.PrefetchScalarGridSpec(
            num_scalar_prefetch=1,
            grid=(length // ROWS,),
            in_specs=[by_row(width)] + [fixed(piece.shape) for piece in pieces],
            out_specs=[by_row(width), by_row(total), kept((width, total)), kept((8, width))],
            scratch_shapes=[pltpu.VMEM((width, LANES), WIDE)],
        ),
        out_shape=[
            jax.ShapeDtypeStruct((length, width), LOW),
            jax.ShapeDtypeStruct((length, total), LOW),
            jax.ShapeDtypeStruct((width, total), LOW),
            jax.ShapeDtypeStruct((8, width), WIDE),
        ],
        compiler_params=params(),
        cost_estimate=LONG,
        name="enter",
    )(table, tokens, *pieces)


def build_bias(bias, seg_col, seg_row):
    length = bias.shape[0]
    for start in range(0, length, ROWS):
        lanes = slice(start, start + ROWS)
        until = start + ROWS
        shape = (until, ROWS)
        key_at = lax.broadcasted_iota(jnp.int32, shape, 0)
        query_at = lax.broadcasted_iota(jnp.int32, shape, 1) + start
        same = jnp.broadcast_to(seg_col[:until, 0:1], shape) == jnp.broadcast_to(
            seg_row[0:1, lanes], shape
        )
        bias[:until, lanes] = jnp.where((key_at <= query_at) & same, 0.0, MASKED)


def one_head(flipped, head):
    empty = jnp.zeros((HD, flipped.shape[1]), flipped.dtype)
    if head == 0:
        return jnp.concatenate([flipped[:HD], empty], axis=0)
    return jnp.concatenate([empty, flipped[HD:]], axis=0)


def attend_kernel(queries, keys, values, seg_col, seg_row, out, lse, bias):
    @pl.when(pl.program_id(0) == 0)
    def _():
        build_bias(bias, seg_col, seg_row)

    length = queries.shape[0]
    q_flip = queries[...].T
    v_flip = values[...].T
    sides = [one_head(q_flip, head) for head in range(2)]
    for start in range(0, length, ROWS):
        lanes = slice(start, start + ROWS)
        until = start + ROWS
        pieces = []
        for head in range(2):
            scores = nn(keys[:until], sides[head][:, lanes]) * (HD**-0.5 * LOG2E)
            scores = scores + bias[:until, lanes]
            top = jnp.max(scores, axis=0, keepdims=True)
            expo = jnp.exp2(scores - top)
            total = jnp.sum(expo, axis=0, keepdims=True)
            flat = nn(v_flip[head * HD : (head + 1) * HD, :until], expo.astype(LOW))
            pieces.append(flat / total)
            lse[head : head + 1, lanes] = top + jnp.log(total) * LOG2E
        out[lanes, :] = jnp.concatenate(pieces, axis=0).T.astype(LOW)


def attend(proj, seg_col, seg_row):
    length = proj.shape[0]
    pairs = proj.shape[1] // (3 * LANES)

    def part(k):
        return pl.BlockSpec((length, LANES), lambda i: (0, k * pairs + i))

    return pl.pallas_call(
        attend_kernel,
        grid=(pairs,),
        in_specs=[part(0), part(1), part(2), fixed(seg_col.shape), fixed(seg_row.shape)],
        out_specs=[
            pl.BlockSpec((length, LANES), lambda i: (0, i)),
            pl.BlockSpec((8, length), lambda i: (i, 0)),
        ],
        out_shape=[
            jax.ShapeDtypeStruct((length, pairs * LANES), LOW),
            jax.ShapeDtypeStruct((8 * pairs, length), WIDE),
        ],
        scratch_shapes=[pltpu.VMEM((length, length), WIDE)],
        compiler_params=params(),
        cost_estimate=LONG,
        name="attend",
    )(proj, proj, proj, seg_col, seg_row)


def attend_back_kernel(
    queries, keys, values, out, grad, lse, seg_col, seg_row, result, bias, k_sum, v_sum
):
    @pl.when(pl.program_id(0) == 0)
    def _():
        build_bias(bias, seg_col, seg_row)

    length = queries.shape[0]
    scale = HD**-0.5
    q_flip = queries[...].T
    k_flip = keys[...].T
    g_flip = grad[...].T
    product = out[...].T.astype(WIDE) * g_flip.astype(WIDE)
    k_sum[...] = jnp.zeros_like(k_sum)
    v_sum[...] = jnp.zeros_like(v_sum)
    q_sides = [one_head(q_flip, head) for head in range(2)]
    g_sides = [one_head(g_flip, head) for head in range(2)]
    for start in range(0, length, ROWS):
        lanes = slice(start, start + ROWS)
        until = start + ROWS
        pieces = []
        for head in range(2):
            scores = nn(keys[:until], q_sides[head][:, lanes]) * (scale * LOG2E)
            probs = jnp.exp2(scores + bias[:until, lanes] - lse[head : head + 1, lanes])
            v_sum[head, :until] += nn(probs.astype(LOW), grad[lanes, :])
            centre = jnp.sum(
                product[head * HD : (head + 1) * HD, lanes], axis=0, keepdims=True
            )
            pull = nn(values[:until], g_sides[head][:, lanes])
            pull = (probs * (pull - centre)).astype(LOW)
            k_sum[head, :until] += nn(pull, queries[lanes, :])
            pieces.append(nn(k_flip[head * HD : (head + 1) * HD, :until], pull))
        result[0, lanes, :] = (jnp.concatenate(pieces, axis=0) * scale).T.astype(LOW)
    first = lax.broadcasted_iota(jnp.int32, (length, LANES), 1) < HD
    result[1] = (jnp.where(first, k_sum[0], k_sum[1]) * scale).astype(LOW)
    result[2] = jnp.where(first, v_sum[0], v_sum[1]).astype(LOW)


def attend_back(proj, out, grad, lse, seg_col, seg_row):
    length = proj.shape[0]
    pairs = proj.shape[1] // (3 * LANES)

    def part(k):
        return pl.BlockSpec((length, LANES), lambda i: (0, k * pairs + i))

    return pl.pallas_call(
        attend_back_kernel,
        grid=(pairs,),
        in_specs=[
            part(0),
            part(1),
            part(2),
            part(0),
            part(0),
            pl.BlockSpec((8, length), lambda i: (i, 0)),
            fixed(seg_col.shape),
            fixed(seg_row.shape),
        ],
        out_specs=pl.BlockSpec((3, length, LANES), lambda i: (0, 0, i)),
        out_shape=jax.ShapeDtypeStruct((3, length, pairs * LANES), LOW),
        scratch_shapes=[
            pltpu.VMEM((length, length), WIDE),
            pltpu.VMEM((2, length, LANES), WIDE),
            pltpu.VMEM((2, length, LANES), WIDE),
        ],
        compiler_params=params(),
        cost_estimate=LONG,
        name="attend_back",
    )(proj, proj, proj, out, grad, lse, seg_col, seg_row)


def leave_kernel(table, att, near, far, part, whole):
    rows = near.shape[0] // (BLOCKS // 2)
    lanes = slice(near.shape[1] - whole.shape[1], None)

    @pl.when(pl.program_id(0) == 0)
    def _():
        for j in range(BLOCKS):
            whole[j * rows : (j + 1) * rows, :] = take(
                table, BLOCKS + j, rows, near, far, lanes
            )

    part[...] = nt(att[...], whole[...]).astype(LOW)


def leave(table, att, near, far):
    length, inner = att.shape
    width = near.shape[0] * 2
    return pl.pallas_call(
        leave_kernel,
        grid_spec=pltpu.PrefetchScalarGridSpec(
            num_scalar_prefetch=1,
            grid=(length // ROWS,),
            in_specs=[by_row(inner), fixed(near.shape), fixed(far.shape)],
            out_specs=[by_row(width), kept((width, inner))],
        ),
        out_shape=[
            jax.ShapeDtypeStruct((length, width), LOW),
            jax.ShapeDtypeStruct((width, inner), LOW),
        ],
        compiler_params=params(),
        cost_estimate=LONG,
        name="leave",
    )(table, att, near, far)


def middle_kernel(tokens, part, far, vectors, middle, normed):
    values = tokens[...] + (part[...].astype(WIDE) + far[...].astype(WIDE))
    middle[...] = values
    hat, _ = hat_of(values)
    normed[...] = (hat * vectors[2:3, :] + vectors[3:4, :]).astype(LOW)


def second_norm(tokens, part, far, vectors):
    length, width = part.shape
    return pl.pallas_call(
        middle_kernel,
        grid=(length // ROWS,),
        in_specs=[by_row(width), by_row(width), by_row(width), fixed((8, width))],
        out_specs=[by_row(width), by_row(width)],
        out_shape=[
            jax.ShapeDtypeStruct((length, width), WIDE),
            jax.ShapeDtypeStruct((length, width), LOW),
        ],
        compiler_params=params(),
        cost_estimate=LONG,
        name="second_norm",
    )(tokens, part, far, vectors)


SIDE = 256


def feed_kernel(
    table,
    normed,
    grad,
    up_a,
    up_a2,
    up_b,
    up_b2,
    down_a,
    down_a2,
    down_b,
    down_b2,
    branch,
    pulled,
    up_keep,
    up_send,
    down_keep,
    down_send,
    normed_flip,
    grad_flip,
    up_whole,
    down_whole,
    act,
    pre,
    branch_sum,
    pulled_sum,
):
    step = pl.program_id(0)
    length = normed.shape[0]
    rows = up_a.shape[0] // (BLOCKS // 2)

    @pl.when(step == 0)
    def _():
        normed_flip[...] = normed[...].T
        grad_flip[...] = grad[...].T
        branch_sum[...] = jnp.zeros_like(branch_sum)
        pulled_sum[...] = jnp.zeros_like(pulled_sum)
        up_cut = up_a.shape[1] // SIDE
        down_cut = down_a.shape[1] // SIDE
        for k in range(up_whole.shape[0]):
            for j in range(BLOCKS):
                to = slice(j * rows, (j + 1) * rows)
                pair, spot = ((up_a, up_a2), k) if k < up_cut else ((up_b, up_b2), k - up_cut)
                lanes = slice(spot * SIDE, (spot + 1) * SIDE)
                up_whole[k, to, :] = take(
                    table, (RIGHT if k >= up_cut else LEFT) + j, rows, *pair, lanes
                )
                pair, spot = (
                    ((down_a, down_a2), k) if k < down_cut else ((down_b, down_b2), k - down_cut)
                )
                lanes = slice(spot * SIDE, (spot + 1) * SIDE)
                down_whole[k, to, :] = take(
                    table, (DOWN_RIGHT if k >= down_cut else DOWN_LEFT) + j, rows, *pair, lanes
                )

    for start in range(0, length, ROWS):
        at = slice(start, start + ROWS)
        wide = nn(normed[at, :], up_whole[step])
        square = wide * wide
        root = math.sqrt(2.0 / math.pi)
        bend = jnp.tanh(wide * (root + root * 0.044715 * square))
        share = 0.5 + 0.5 * bend
        slope = share + 0.5 * wide * (1.0 - bend * bend) * (
            root + 3.0 * root * 0.044715 * square
        )
        act[at, :] = (wide * share).astype(LOW)
        pre[at, :] = (nn(grad[at, :], down_whole[step]) * slope).astype(LOW)
        branch_sum[at, :] += nt(act[at, :], down_whole[step])
        pulled_sum[at, :] += nt(pre[at, :], up_whole[step])

    lifted = nn(normed_flip[...], pre[...]).astype(LOW)
    lowered = nn(grad_flip[...], act[...]).astype(LOW)
    for j in range(BLOCKS):
        block = slice(j * rows, (j + 1) * rows)
        put(table, LEFT + j, rows, up_keep, up_send, lifted[block])
        put(table, RIGHT + j, rows, down_keep, down_send, lowered[block])

    @pl.when(step == pl.num_programs(0) - 1)
    def _():
        branch[...] = branch_sum[...].astype(LOW)
        pulled[...] = pulled_sum[...].astype(LOW)


def feed(table, normed, grad, *pieces):
    length, width = normed.shape
    hidden = pieces[4].shape[1] + pieces[6].shape[1]
    column = pl.BlockSpec((width // 2, SIDE), lambda i, *_: (0, i))
    token = (length, width)
    steps = hidden // SIDE
    return pl.pallas_call(
        feed_kernel,
        grid_spec=pltpu.PrefetchScalarGridSpec(
            num_scalar_prefetch=1,
            grid=(steps,),
            in_specs=[fixed(token), fixed(token)] + [fixed(piece.shape) for piece in pieces],
            out_specs=[kept(token), kept(token), column, column, column, column],
            scratch_shapes=[
                pltpu.VMEM((width, length), LOW),
                pltpu.VMEM((width, length), LOW),
                pltpu.VMEM((steps, width, SIDE), LOW),
                pltpu.VMEM((steps, width, SIDE), LOW),
                pltpu.VMEM((length, SIDE), LOW),
                pltpu.VMEM((length, SIDE), LOW),
                pltpu.VMEM(token, WIDE),
                pltpu.VMEM(token, WIDE),
            ],
        ),
        out_shape=[jax.ShapeDtypeStruct(token, LOW)] * 2
        + [jax.ShapeDtypeStruct((width // 2, hidden), LOW)] * 4,
        compiler_params=params(),
        cost_estimate=LONG,
        name="feed",
    )(table, normed, grad, *pieces)


def middle_back_kernel(
    table,
    pulled,
    far,
    middle,
    grad,
    vectors,
    out_whole,
    att,
    middle_grad,
    att_grad,
    out_keep,
    out_send,
    sums,
    out_sum,
):
    step = pl.program_id(0)
    rows = out_whole.shape[0] // BLOCKS

    @pl.when(step == 0)
    def _():
        out_sum[...] = jnp.zeros_like(out_sum)
        sums[...] = jnp.zeros_like(sums)

    pull = pulled[...].astype(WIDE) + far[...].astype(WIDE)
    hat, rate = hat_of(middle[...])
    whole = grad[...].astype(WIDE) + norm_back(pull, hat, rate, vectors[2:3, :])
    middle_grad[...] = whole
    sums[0:1, :] += jnp.sum(pull * hat, axis=0, keepdims=True)
    sums[1:2, :] += jnp.sum(pull, axis=0, keepdims=True)
    low = whole.astype(LOW)
    att_grad[...] = nn(low, out_whole[...]).astype(LOW)
    out_sum[...] += tn(low, att[...])

    @pl.when(step == pl.num_programs(0) - 1)
    def _():
        for j in range(BLOCKS):
            block = out_sum[j * rows : (j + 1) * rows, :].astype(LOW)
            put(table, RIGHT + j, rows, out_keep, out_send, block)


def middle_back(table, pulled, far, middle, grad, vectors, out_whole, att):
    length, width = middle.shape
    inner = att.shape[1]
    return pl.pallas_call(
        middle_back_kernel,
        grid_spec=pltpu.PrefetchScalarGridSpec(
            num_scalar_prefetch=1,
            grid=(length // ROWS,),
            in_specs=[
                by_row(width),
                by_row(width),
                by_row(width),
                by_row(width),
                fixed((8, width)),
                fixed((width, inner)),
                by_row(inner),
            ],
            out_specs=[
                by_row(width),
                by_row(inner),
                kept((width // 2, inner), (0, 1)),
                kept((width // 2, inner), (0, 1)),
                kept((8, width)),
            ],
            scratch_shapes=[pltpu.VMEM((width, inner), WIDE)],
        ),
        out_shape=[
            jax.ShapeDtypeStruct((length, width), WIDE),
            jax.ShapeDtypeStruct((length, inner), LOW),
            jax.ShapeDtypeStruct((width // 2, 2 * inner), LOW),
            jax.ShapeDtypeStruct((width // 2, 2 * inner), LOW),
            jax.ShapeDtypeStruct((8, width), WIDE),
        ],
        compiler_params=params(),
        cost_estimate=LONG,
        name="middle_back",
    )(table, pulled, far, middle, grad, vectors, out_whole, att)


def weight_back_kernel(
    table,
    proj_grad,
    normed,
    held_keep,
    held_send,
    left_keep,
    left_send,
    right_keep,
    right_send,
    normed_flip,
):
    step = pl.program_id(0)
    rows = normed.shape[1] // BLOCKS

    @pl.when(step == 0)
    def _():
        normed_flip[...] = normed[...].T

    weight = nn(normed_flip[...], proj_grad[0]).astype(LOW)

    @pl.when(step < 2)
    def _():
        for j in range(BLOCKS):
            put(table, LEFT + j, rows, left_keep, left_send, weight[j * rows : (j + 1) * rows])

    @pl.when(step == 2)
    def _():
        for j in range(BLOCKS):
            block = weight[j * rows : (j + 1) * rows]
            put(table, RIGHT + j, rows, right_keep, right_send, block)


def weight_back(table, proj_grad, normed, held_keep, held_send):
    length, width = normed.shape
    inner = proj_grad.shape[2]
    early = pl.BlockSpec((width // 2, inner), lambda i, *_: (0, jnp.minimum(i, 1)))
    late = kept((width // 2, inner))
    return pl.pallas_call(
        weight_back_kernel,
        grid_spec=pltpu.PrefetchScalarGridSpec(
            num_scalar_prefetch=1,
            grid=(3,),
            in_specs=[
                pl.BlockSpec((1, length, inner), lambda i, *_: (i, 0, 0)),
                fixed((length, width)),
                pl.BlockSpec(memory_space=pl.ANY),
                pl.BlockSpec(memory_space=pl.ANY),
            ],
            out_specs=[early, early, late, late],
            scratch_shapes=[pltpu.VMEM((width, length), LOW)],
        ),
        out_shape=[jax.ShapeDtypeStruct((width // 2, 2 * inner), LOW)] * 4,
        input_output_aliases={3: 2, 4: 3},
        compiler_params=params(),
        cost_estimate=LONG,
        name="weight_back",
    )(table, proj_grad, normed, held_keep, held_send)


def token_back_kernel(proj_grad, whole, pulled):
    inner = proj_grad.shape[2]
    total = nt(proj_grad[0], whole[:, :inner])
    for c in range(1, 3):
        total += nt(proj_grad[c], whole[:, c * inner : (c + 1) * inner])
    pulled[...] = total.astype(LOW)


def token_back(proj_grad, whole):
    length, inner = proj_grad.shape[1:]
    width = whole.shape[0]
    return pl.pallas_call(
        token_back_kernel,
        grid=(length // ROWS,),
        in_specs=[
            pl.BlockSpec((3, ROWS, inner), lambda i: (0, i, 0)),
            fixed(whole.shape),
        ],
        out_specs=by_row(width),
        out_shape=jax.ShapeDtypeStruct((length, width), LOW),
        compiler_params=params(),
        cost_estimate=LONG,
        name="token_back",
    )(proj_grad, whole)


def exit_kernel(core, pulled, far, tokens, middle_grad, vectors, result, sums):
    step = pl.program_id(0)

    @pl.when(step == 0)
    def _():
        sums[...] = jnp.zeros_like(sums)

    pull = pulled[...].astype(WIDE) + far[...].astype(WIDE)
    hat, rate = hat_of(tokens[...])
    sums[0:1, :] += jnp.sum(pull * hat, axis=0, keepdims=True)
    sums[1:2, :] += jnp.sum(pull, axis=0, keepdims=True)
    result[...] = middle_grad[...] + norm_back(pull, hat, rate, vectors[0:1, :])


def leave_layer(core, pulled, far, tokens, middle_grad, vectors):
    length, width = pulled.shape
    steps = length // ROWS
    part = steps // 2

    def turned(i, place):
        return ((i + part * (1 - place[0])) % steps, 0)

    row = pl.BlockSpec((ROWS, width), turned)
    return pl.pallas_call(
        exit_kernel,
        grid_spec=pltpu.PrefetchScalarGridSpec(
            num_scalar_prefetch=1,
            grid=(steps,),
            in_specs=[row, row, row, row, fixed((8, width))],
            out_specs=[
                pl.BlockSpec((ROWS, width), lambda i, *_: (jnp.maximum(i - part, 0), 0)),
                kept((8, width)),
            ],
        ),
        out_shape=[
            jax.ShapeDtypeStruct((length // 2, width), WIDE),
            jax.ShapeDtypeStruct((8, width), WIDE),
        ],
        compiler_params=params(),
        cost_estimate=LONG,
        name="leave_layer",
    )(core, pulled, far, tokens, middle_grad, vectors)


def swap_cores(values):
    return lax.ppermute(values, "tensor", [(0, 1), (1, 0)])


def hop(values, bits, size):
    return lax.ppermute(values, "fsdp", [(i, i ^ bits) for i in range(size)])


def block_places(size, me):
    spots = jnp.arange(BLOCKS, dtype=jnp.int32)
    if size != BLOCKS:
        return jnp.concatenate([spots] * 4)
    away = me ^ spots
    low, mid, high = away & 1, (away >> 1) & 1, away >> 2
    return jnp.concatenate(
        [
            low * 8 + mid * 4 + high,
            mid * 8 + low * 4 + high,
            mid * 8 + high * 2 + low,
            low * 8 + high * 2 + mid,
        ]
    )


def vmem_call(kernel, shapes, args, name):
    return pl.pallas_call(
        kernel,
        out_shape=shapes,
        compiler_params=pltpu.CompilerParams(vmem_limit_bytes=60 * 1024 * 1024),
        cost_estimate=LONG,
        name=name,
    )(*args)


def collect(pieces, cut):
    rows, width = pieces[0].shape

    def kernel(*refs):
        left, right = refs[len(pieces) :]
        for k, piece in enumerate(refs[: len(pieces)]):
            at = slice(k * rows, (k + 1) * rows)
            left[at, :] = piece[:, :cut]
            right[at, :] = piece[:, cut:]

    total = rows * len(pieces)
    return vmem_call(
        kernel,
        [jax.ShapeDtypeStruct((total, cut), LOW), jax.ShapeDtypeStruct((total, width - cut), LOW)],
        pieces,
        "collect",
    )


def join(left, left_far, right, right_far, size):
    if size != BLOCKS:
        return jnp.concatenate([left, left_far], 0), jnp.concatenate([right, right_far], 0)

    def kernel(one, one_far, two, two_far, one_out, two_out):
        rows = one.shape[0]
        one_out[:rows, :] = one[...]
        one_out[rows:, :] = one_far[...]
        two_out[:rows, :] = two[...]
        two_out[rows:, :] = two_far[...]

    shapes = [jax.ShapeDtypeStruct((2 * v.shape[0], v.shape[1]), LOW) for v in (left, right)]
    return vmem_call(kernel, shapes, (left, left_far, right, right_far), "join")


def far_rows(values, size):
    if size != BLOCKS:
        whole = lax.all_gather(values, "fsdp", axis=0, tiled=True)
        rows = whole.shape[0] // 4
        return [whole[k * rows : (k + 1) * rows] for k in range(4)]
    return [values] + [hop(values, 4 * k, size) for k in range(1, 4)]


def after(values, *done):
    return lax.optimization_barrier((values, done))[0]


def halves(whole):
    half = whole.shape[0] // 2
    return whole[:half], whole[half:]


def down_stage(left, right, size):
    if size != BLOCKS:
        return left, None, right, None
    return left, hop(left, 1, size), right, hop(right, 2, size)


def beside(left, left_far, right, right_far, size):
    if size != BLOCKS:
        return jnp.concatenate([left, right], axis=1)
    rows, cut = left.shape

    def kernel(one, one_far, two, two_far, out):
        out[:rows, :cut] = one[...]
        out[rows:, :cut] = one_far[...]
        out[:rows, cut:] = two[...]
        out[rows:, cut:] = two_far[...]

    shape = jax.ShapeDtypeStruct((2 * rows, 2 * cut), LOW)
    return vmem_call(kernel, [shape], (left, left_far, right, right_far), "beside")[0]


def in_order(own, core):
    other = swap_cores(own)
    return jnp.where(
        core == 0,
        jnp.concatenate([own, other], axis=0),
        jnp.concatenate([other, own], axis=0),
    )


def second_stage(left, right, size):
    if size != BLOCKS:
        return halves(left) + halves(right)
    return left, hop(left, 2, size), right, hop(right, 1, size)


def third_stage(left, right, size):
    if size != BLOCKS:
        return halves(left) + halves(right)
    return left, hop(left, 1, size), right, hop(right, 2, size)


def fold_half(left, left_far, right, right_far, size):
    if size != BLOCKS:
        return left, left_far, right, right_far

    def kernel(one, one_far, two, two_far, one_low, one_high, two_low, two_high):
        rows = one_low.shape[0]
        for a, b, low, high in (
            (one, one_far, one_low, one_high),
            (two, two_far, two_low, two_high),
        ):
            low[...] = (a[:rows, :].astype(WIDE) + b[:rows, :].astype(WIDE)).astype(LOW)
            high[...] = (a[rows:, :].astype(WIDE) + b[rows:, :].astype(WIDE)).astype(LOW)

    shapes = [
        jax.ShapeDtypeStruct((v.shape[0] // 2, v.shape[1]), LOW)
        for v in (left, left, right, right)
    ]
    return vmem_call(kernel, shapes, (left, left_far, right, right_far), "fold_half")


def fold_quarter(left, left_far, right, right_far, size):
    if size != BLOCKS:
        whole = jnp.concatenate(
            [jnp.concatenate([left, left_far], 0), jnp.concatenate([right, right_far], 0)], 1
        )
        return halves(whole)

    cut = left.shape[1]
    rows = left.shape[0] // 4

    def kernel(one, one_far, two, two_far, *outs):
        for k, out in enumerate(outs):
            at = slice(k * rows, (k + 1) * rows)
            out[:, :cut] = (one[at, :].astype(WIDE) + one_far[at, :].astype(WIDE)).astype(LOW)
            out[:, cut:] = (two[at, :].astype(WIDE) + two_far[at, :].astype(WIDE)).astype(LOW)

    shapes = [jax.ShapeDtypeStruct((rows, cut + right.shape[1]), LOW)] * 4
    return vmem_call(kernel, shapes, (left, left_far, right, right_far), "fold_quarter")


def first_send(left, left_send, right, right_send, size):
    if size != BLOCKS:
        return left, left_send, right, right_send
    return left, hop(left_send, 1, size), right, hop(right_send, 2, size)


def second_send(left, left_send, right, right_send, size):
    if size != BLOCKS:
        return left, left_send, right, right_send
    return left, hop(left_send, 2, size), right, hop(right_send, 1, size)


def third_send(parts, size):
    if size != BLOCKS:
        return parts
    return [parts[0]] + [hop(parts[k], 4 * k, size) for k in range(1, 4)]


def total_of(parts, size):
    if size != BLOCKS:
        whole = jnp.concatenate(parts, axis=0).astype(WIDE)
        return lax.psum_scatter(whole, "fsdp", scatter_dimension=0, tiled=True)
    total = parts[0].astype(WIDE)
    for part in parts[1:]:
        total = total + part.astype(WIDE)
    return total


def sum_all(values, size):
    if size != BLOCKS:
        return lax.psum(values, "fsdp")
    for k in range(4):
        values = values + hop(values, 1 << k, size)
    return values


def body(
    size,
    inputs,
    segment_ids,
    qkv_weight,
    out_weight,
    up_weight,
    down_weight,
    gain_one,
    shift_one,
    gain_two,
    shift_two,
    cotangent,
):
    me = lax.axis_index("fsdp")
    core = lax.axis_index("tensor")
    rows, width = qkv_weight.shape[1:]
    half = inputs.shape[0]
    length = 2 * half
    table = block_places(size, me)

    first = jnp.concatenate(
        [
            qkv_weight.transpose(1, 0, 2).reshape(rows, 3 * width),
            jnp.stack([gain_one, shift_one, gain_two, shift_two], axis=1),
            jnp.zeros((rows, LANES - 4), WIDE),
        ],
        axis=1,
    ).astype(LOW)
    second = jnp.concatenate([up_weight, out_weight.T], axis=1).astype(LOW)
    hidden = down_weight.shape[0]
    third = [v.T.astype(LOW) for v in (down_weight[: hidden // 2], down_weight[hidden // 2 :])]
    first = far_rows(first, size)
    third = down_stage(*third, size)
    tokens = in_order(inputs, core)
    qkv = collect(after(first, tokens), (3 * width + LANES) // 2)
    second = far_rows(after(second, qkv), size)
    third = beside(*third, size)
    qkv = join(*second_stage(*qkv, size), size)
    grad = in_order(cotangent, core)
    seg_col = jnp.broadcast_to(segment_ids[:, None], (length, LANES))
    seg_row = jnp.broadcast_to(segment_ids[None, :], (8, length))
    up_out = collect(after(second, qkv, grad, seg_col, seg_row), SIDE * (-(-second[0].shape[1] // (2 * SIDE))))
    third = far_rows(after(third, up_out), size)
    qkv = third_stage(*qkv, size)
    up_out = second_stage(*up_out, size)

    normed_one, proj, qkv_whole, vectors = enter(table, tokens, *qkv)
    up_out = join(*after(up_out, proj), size)
    proj = after(proj, up_out)
    up_out = third_stage(*up_out, size)
    att, lse = attend(proj, seg_col, seg_row)
    down = collect(after(third, att), hidden // 2)
    att = after(att, down, up_out)
    down = second_stage(*down, size)
    part, out_whole = leave(table, att, *up_out[2:])
    far = after(swap_cores(part), down)
    middle, normed_two = second_norm(tokens, part, far, vectors)
    branch, pulled, *parts = feed(table, normed_two, grad, *up_out, *down)
    parts = first_send(*parts, size)

    middle_grad, att_grad, *held, sums_two = middle_back(
        table, pulled, swap_cores(pulled), middle, grad, vectors, out_whole, att
    )
    proj_grad = attend_back(proj, att, att_grad, lse, seg_col, seg_row)
    parts = fold_half(*after(parts, proj_grad), size)
    proj_grad = after(proj_grad, parts)
    parts = second_send(*parts, size)
    tail = weight_back(table, proj_grad, normed_one, *held)
    parts = fold_quarter(*after(parts, tail), size)
    tail = first_send(*tail, size)
    proj_grad = after(proj_grad, parts)
    parts = third_send(parts, size)
    pulled = token_back(proj_grad, qkv_whole)
    tail = fold_half(*after(tail, pulled), size)
    far = after(swap_cores(pulled), tail)
    tail = second_send(*tail, size)
    input_grad, sums_one = leave_layer(
        core[None], pulled, far, tokens, middle_grad, vectors
    )
    tail = fold_quarter(*after(tail, input_grad), size)
    parts, branch, sums_one = after((parts, branch, sums_one), tail)
    tail = third_send(tail, size)

    def own_half(values):
        return lax.dynamic_slice_in_dim(values, core * half, half, 0)

    far = swap_cores(lax.dynamic_slice_in_dim(branch, (1 - core) * half, half, 0))
    outputs = own_half(middle) + (own_half(branch).astype(WIDE) + far.astype(WIDE))
    feed_grad = total_of(parts, size)
    sums = sum_all(jnp.concatenate([sums_one[:2], sums_two[:2]], axis=0), size)
    tail = total_of(tail, size)
    sums = lax.dynamic_slice_in_dim(sums, me * rows, rows, 1)
    qkv_grad = jnp.stack([tail[:, k * width : (k + 1) * width] for k in range(3)], axis=0)
    return (
        outputs,
        input_grad,
        qkv_grad,
        tail[:, 3 * width :].T,
        feed_grad[:, :hidden],
        feed_grad[:, hidden:].T,
        sums[0],
        sums[1],
        sums[2],
        sums[3],
    )


def solution(mesh):
    tokens = P(("fsdp", "tensor"), None)
    split = P("fsdp")
    weights = (
        P(None, "fsdp", "tensor"),
        P("tensor", "fsdp"),
        P("fsdp", "tensor"),
        P("tensor", "fsdp"),
        split,
        split,
        split,
        split,
    )
    return jax.shard_map(
        functools.partial(body, mesh.shape["fsdp"]),
        mesh=mesh,
        in_specs=(tokens, split) + weights + (tokens,),
        out_specs=(tokens, tokens) + weights,
        check_vma=False,
    )
```

time: 369 us -> 255 us (0.69)
  waiting for transfers between devices: 135 us -> 43.4 us
  local copies, waits for them, and re-layouts: 39.6 us -> 11 us
  Pallas kernels: 107 us -> 135 us
  starting transfers between devices: 64.7 us -> 48.1 us
  other arithmetic: 19.9 us -> 15.4 us
    ppermute x44 -> x39, waiting for transfers between devices: 135 us -> 41.4 us  [hop(): return lax.ppermute(values, 'fsdp', [(i, i ^ bits) for i in range(size)])]
    pallas_call x2 -> x13, Pallas kernels: 18.5 us -> 43.5 us  [the longest x10 24.3 us: vmem_call(): pl.pallas_call(kernel, out_shape=shapes, compiler_params=pltpu.CompilerPa...]
    ppermute x44 -> x39, starting transfers between devices: 64.2 us -> 47.4 us  [hop(): return lax.ppermute(values, 'fsdp', [(i, i ^ bits) for i in range(size)])]
    unnamed x67 -> x30, local copies, waits for them, and re-layouts: 19.9 us -> 3.2 us
    slice x12 -> x0, local copies, waits for them, and re-layouts: 6.67 us -> none  [the longest x8 6.57 us: fold(): other = hop(values[half:], bits, size)]
    convert_element_type x8 -> x0, other arithmetic: 6.02 us -> none  [fold(): return (values[:half].astype(WIDE) + other.astype(WIDE)).astype(LOW)]
    concatenate x8 -> x0, local copies, waits for them, and re-layouts: 5.96 us -> none  [the longest x4 3.29 us: gather_rows(): jnp.concatenate([right, hop(right, two, size)], axis=0)]
    select_n x0 -> x2, other arithmetic: none -> 5.02 us  [in_order(): jnp.where(core == 0, jnp.concatenate([own, other], axis=0), jnp.concatena...]
  transfers between devices with their start and end apart: 50 -> 45, of which waited for: 22 -> 15; matrix products, arithmetic and copies ran while one was open for 13% -> 8% of each run, Pallas kernels for 22% -> 35%
where the time goes in v1:
time: 255 us; the launch traced here: 254 us
  Pallas kernels  135 us (53%)
  starting transfers between devices  48.1 us (19%)
  waiting for transfers between devices  43.4 us (17%)
  other arithmetic  15.4 us (6%)
  local copies, waits for them, and re-layouts  11 us (4%)
    ppermute x39, starting transfers between devices, hop(): return lax.ppermute(values, 'fsdp', [(i, i ^ bits) for i in range(size)])  47.4 us
    ppermute x39, waiting for transfers between devices, hop(): return lax.ppermute(values, 'fsdp', [(i, i ^ bits) for i in range(size)])  41.4 us
    pallas_call x1, Pallas kernels, feed(): pl.pallas_call(feed_kernel, grid_spec=pltpu.PrefetchScalarGridSpec(num_sc...  31.3 us
    pallas_call x10, Pallas kernels, vmem_call(): pl.pallas_call(kernel, out_shape=shapes, compiler_params=pltpu.CompilerPa...  24.3 us
    pallas_call x1, Pallas kernels, attend_back(): pl.pallas_call(attend_back_kernel, grid=(pairs,), in_specs=[part(0), part...  15.4 us
    pallas_call x1, Pallas kernels, attend(): pl.pallas_call(attend_kernel, grid=(pairs,), in_specs=[part(0), part(1),...  14.6 us
    pallas_call x1, Pallas kernels, middle_back(): pl.pallas_call(middle_back_kernel, grid_spec=pltpu.PrefetchScalarGridSpec...  9.99 us
    pallas_call x1, Pallas kernels, enter(): pl.pallas_call(enter_kernel, grid_spec=pltpu.PrefetchScalarGridSpec(num_s...  7.97 us
  transfers between devices with their start and end apart: 45, of which 15 were waited for; matrix products, arithmetic and copies ran while one was open for 8% of the time, Pallas kernels for 35%

profile of v1, /device:TPU:0, one launch (start us, length us, event | category | flops | bytes accessed | tf_op | source)
XLA Modules:
  0.0 253.6 jit_solution(14551289732788697685)
XLA Ops:
  6.0 2.7 %collective-permute-start.1 = (bf16[48,1280]{1,0:T(8,128)(2,1)}, bf16[48,1280]{1,0:T(8,128)(2,1)}, u32[]{:S(2)}, u32[]{:S(2)}) collective-permute-start(bf16[48,1280]{1,0:T(8,128)(2,1)} %concatenate.29.refs_0_), channel_id=1, source_target_pairs={{0,8},{2,10},{4,12},{6,14},{8,0},{10,2},{12,4},{14,6},{16,24},{18,... | collective-permute-start | bytes 368648 | tf_op jit(solution)/shard_map/ppermute | solution.py:673
  8.7 2.6 %collective-permute-start.2 = (bf16[48,1280]{1,0:T(8,128)(2,1)}, bf16[48,1280]{1,0:T(8,128)(2,1)}, u32[]{:S(2)}, u32[]{:S(2)}) collective-permute-start(bf16[48,1280]{1,0:T(8,128)(2,1)} %concatenate.29.refs_0_), channel_id=1, source_target_pairs={{0,16},{2,18},{4,20},{6,22},{8,24},{10,26},{12,28},{14,30},{16,0},... | collective-permute-start | bytes 368648 | tf_op jit(solution)/shard_map/ppermute | solution.py:673
  28.1 3.1 %maximum_select_fusion.1.grad = bf16[1024,768]{1,0:T(8,128)(2,1)} fusion(bf16[512,768]{1,0:T(8,128)(2,1)} %collective-permute-done.11, bf16[512,768]{1,0:T(8,128)(2,1)S(1)} %copy-done.3, pred[]{:T(512)S(6)} %eq.4), kind=kLoop, calls=%fused_computation.1 | loop fusion | flops 7077888 | bytes 3145729 | tf_op jit(solution)/shard_map/jit(_where)/select_n | solution.py:776
  41.9 7.8 %collective-permute-done.9.refs_2_ = bf16[48,1920]{1,0:T(8,128)(2,1)} collective-permute-done((bf16[48,1920]{1,0:T(8,128)(2,1)}, bf16[48,1920]{1,0:T(8,128)(2,1)}, u32[]{:S(2)}, u32[]{:S(2)}) %collective-permute-start.9) | collective-permute-done | bytes 184352 | tf_op jit(solution)/shard_map/ppermute | solution.py:673
  53.4 2.9 %collective-permute-start.17 = (bf16[96,1536]{1,0:T(8,128)(2,1)}, bf16[96,1536]{1,0:T(8,128)(2,1)}, u32[]{:S(2)}, u32[]{:S(2)}) collective-permute-start(bf16[96,1536]{1,0:T(8,128)(2,1)} %beside.1.refs_0_), channel_id=1, source_target_pairs={{0,16},{2,18},{4,20},{6,22},{8,24},{10,26},{12,28},{14,30},{16,0},... | collective-permute-start | bytes 884744 | tf_op jit(solution)/shard_map/ppermute | solution.py:673
  59.4 8.0 %enter.1 = (bf16[1024,768]{1,0:T(8,128)(2,1)}, bf16[1024,1152]{1,0:T(8,128)(2,1)}, bf16[768,1152]{1,0:T(8,128)(2,1)}, f32[8,768]{1,0:T(8,128)}) custom-call(s32[64]{0:T(128)} %pad_add_fusion.table, f32[1024,768]{1,0:T(8,128)} %maximum_select_fusion.tokens, bf16[384,640]{1,0:T(8,128)(2,1)} %get-tuple-element.115.wa, ...), custom_call_target="tpu_custom_call" | custom-call | flops 9999999827968 | bytes 1000000000 | tf_op jit(solution)/shard_map/enter/pallas_call | solution.py:117
  72.4 14.6 %attend.1 = (bf16[1024,384]{1,0:T(8,128)(2,1)}, f32[24,1024]{1,0:T(8,128)}) custom-call(bf16[1024,1152]{1,0:T(8,128)(2,1)} %get-tuple-element.131.queries.keys.values, bf16[1024,1152]{1,0:T(8,128)(2,1)} %get-tuple-element.131.queries.keys.values, bf16[1024,1152]{1,0:T(8,128)(2,1)} %get-tuple-element.131.queries.keys.values, ...), custom_call_target="tpu_custom_call" | custom-call | flops 9999999827968 | bytes 1000000000 | tf_op jit(solution)/shard_map/attend/pallas_call | solution.py:191
  89.4 5.6 %leave.1 = (bf16[1024,768]{1,0:T(8,128)(2,1)}, bf16[768,384]{1,0:T(8,128)(2,1)}) custom-call(s32[64]{0:T(128)} %pad_add_fusion.table, bf16[1024,384]{1,0:T(8,128)(2,1)} %get-tuple-element.140.att.out, bf16[384,896]{1,0:T(8,128)(2,1)} %get-tuple-element.130.near.up_b, bf16[384,896]{1,0:T(8,128)(2,1)} %collective-permute-done.20.far.up_b2), custom_call_target="tpu_custom_call" | custom-call | flops 9999999827968 | bytes 1000000000 | tf_op jit(solution)/shard_map/leave/pallas_call | solution.py:298
  96.6 14.1 %collective-permute-done.22.down_a2 = bf16[384,768]{1,0:T(8,128)(2,1)S(1)} collective-permute-done((bf16[384,768]{1,0:T(8,128)(2,1)S(1)}, bf16[384,768]{1,0:T(8,128)(2,1)S(1)}, u32[]{:S(2)}, u32[]{:S(2)}) %collective-permute-start.22) | collective-permute-done | bytes 589856 | tf_op jit(solution)/shard_map/ppermute | solution.py:673
  113.0 5.4 %second_norm.1 = (f32[1024,768]{1,0:T(8,128)}, bf16[1024,768]{1,0:T(8,128)(2,1)}) custom-call(f32[1024,768]{1,0:T(8,128)} %maximum_select_fusion.tokens, bf16[1024,768]{1,0:T(8,128)(2,1)} %get-tuple-element.141.part, bf16[1024,768]{1,0:T(8,128)(2,1)} %copy-done.10, f32[8,768]{1,0:T(8,128)} %get-tuple-element.143.vectors), custom_call_target="tpu_custom_call" | custom-call | flops 9999999827968 | bytes 1000000000 | tf_op jit(solution)/shard_map/second_norm/pallas_call | solution.py:325
  118.4 31.3 %feed.1 = (bf16[1024,768]{1,0:T(8,128)(2,1)}, bf16[1024,768]{1,0:T(8,128)(2,1)}, bf16[384,1536]{1,0:T(8,128)(2,1)}, bf16[384,1536]{1,0:T(8,128)(2,1)}, bf16[384,...) custom-call(s32[64]{0:T(128)} %pad_add_fusion.table, bf16[1024,768]{1,0:T(8,128)(2,1)} %get-tuple-element.145.normed, ...), custom_call_target="tpu_custom_call" | custom-call | flops 9999999827968 | bytes 1000000000 | tf_op jit(solution)/shard_map/feed/pallas_call | solution.py:432
  154.5 10.0 %middle_back.1 = (f32[1024,768]{1,0:T(8,128)}, bf16[1024,384]{1,0:T(8,128)(2,1)}, bf16[384,768]{1,0:T(8,128)(2,1)}, bf16[384,768]{1,0:T(8,128)(2,1)}, f32[8,768]{1,0:T(8,128)}) custom-call(s32[64]{0:T(128)} %pad_add_fusion.table, bf16[1024,768]{1,0:T(8,128)(2,1)} %get-tuple-element.150.pulled, bf16[1024,768]{1,0:T(8,128)(2,1)} %copy-done.9, ...), custom_call_target="tpu_custom_call" | custom-call | flops 9999999827968 | bytes 1000000000 | tf_op jit(solution)/shard_map/middle_back/pallas_call | solution.py:502
  164.5 15.4 %attend_back.1.proj_grad = bf16[3,1024,384]{2,1,0:T(8,128)(2,1)} custom-call(bf16[1024,1152]{1,0:T(8,128)(2,1)} %get-tuple-element.131.queries.keys.values, bf16[1024,1152]{1,0:T(8,128)(2,1)} %get-tuple-element.131.queries.keys.values, bf16[1024,1152]{1,0:T(8,128)(2,1)} %get-tuple-element.131.queries.keys.values, ...), custom_call_target="tpu_custom_call" | custom-call | flops 9999999827968 | bytes 1000000000 | tf_op jit(solution)/shard_map/attend_back/pallas_call | solution.py:255
  180.0 3.9 %fold_half.2 = (bf16[192,1536]{1,0:T(8,128)(2,1)}, bf16[192,1536]{1,0:T(8,128)(2,1)}, bf16[192,1536]{1,0:T(8,128)(2,1)}, bf16[192,1536]{1,0:T(8,128)(2,1)}) custom-call(bf16[384,1536]{1,0:T(8,128)(2,1)} %get-tuple-element.154.one, bf16[384,1536]{1,0:T(8,128)(2,1)} %collective-permute-done.24.one_far, bf16[384,1536]{1,0:T(8,128)(2,1)} %get-tuple-element.156.two, ...), custom_call_target="tpu_custom_call" | custom-call | flops 9999999827968 | bytes 1000000000 | tf_op jit(solution)/shard_map/fold_half/pallas_call | solution.py:693
  185.9 7.8 %weight_back.1 = (bf16[384,768]{1,0:T(8,128)(2,1)}, bf16[384,768]{1,0:T(8,128)(2,1)}, bf16[384,768]{1,0:T(8,128)(2,1)}, bf16[384,768]{1,0:T(8,128)(2,1)}) custom-call(s32[64]{0:T(128)} %pad_add_fusion.table, bf16[3,1024,384]{2,1,0:T(8,128)(2,1)} %attend_back.1.proj_grad, ...), custom_call_target="tpu_custom_call", output_to_operand_aliasing={{2}: (3, {}), {3}: (4, {})} | custom-call | flops 9999999827968 | bytes 1000000000 | tf_op jit(solution)/shard_map/weight_back/pallas_call | solution.py:576
  197.0 3.3 %collective-permute-done.27.one_far = bf16[192,1536]{1,0:T(8,128)(2,1)} collective-permute-done((bf16[192,1536]{1,0:T(8,128)(2,1)}, bf16[192,1536]{1,0:T(8,128)(2,1)}, u32[]{:S(2)}, u32[]{:S(2)}) %collective-permute-start.27) | collective-permute-done | bytes 589856 | tf_op jit(solution)/shard_map/ppermute | solution.py:673
  201.9 2.7 %fold_quarter.2 = (bf16[48,3072]{1,0:T(8,128)(2,1)}, bf16[48,3072]{1,0:T(8,128)(2,1)}, bf16[48,3072]{1,0:T(8,128)(2,1)}, bf16[48,3072]{1,0:T(8,128)(2,1)}) custom-call(bf16[192,1536]{1,0:T(8,128)(2,1)} %get-tuple-element.170.one, bf16[192,1536]{1,0:T(8,128)(2,1)} %collective-permute-done.27.one_far, bf16[192,1536]{1,0:T(8,128)(2,1)} %get-tuple-element.172.two, ...), custom_call_target="tpu_custom_call" | custom-call | flops 9999999827968 | bytes 1000000000 | tf_op jit(solution)/shard_map/fold_quarter/pallas_call | solution.py:693
  204.5 2.9 %collective-permute-start.30 = (bf16[48,3072]{1,0:T(8,128)(2,1)}, bf16[48,3072]{1,0:T(8,128)(2,1)}, u32[]{:S(2)}, u32[]{:S(2)}) collective-permute-start(bf16[48,3072]{1,0:T(8,128)(2,1)} %get-tuple-element.176), channel_id=1, source_target_pairs={{0,16},{2,18},{4,20},{6,22},{8,24},{10,26},{12,28},{14,30},{16,0},... | collective-permute-start | bytes 884744 | tf_op jit(solution)/shard_map/ppermute | solution.py:673
  208.9 6.1 %token_back.1.pulled = bf16[1024,768]{1,0:T(8,128)(2,1)} custom-call(bf16[3,1024,384]{2,1,0:T(8,128)(2,1)} %attend_back.1.proj_grad, bf16[768,1152]{1,0:T(8,128)(2,1)} %get-tuple-element.180.whole), custom_call_target="tpu_custom_call" | custom-call | flops 9999999827968 | bytes 1000000000 | tf_op jit(solution)/shard_map/token_back/pallas_call | solution.py:609
  215.0 2.7 %fold_half.3 = (bf16[192,768]{1,0:T(8,128)(2,1)}, bf16[192,768]{1,0:T(8,128)(2,1)}, bf16[192,768]{1,0:T(8,128)(2,1)}, bf16[192,768]{1,0:T(8,128)(2,1)}) custom-call(bf16[384,768]{1,0:T(8,128)(2,1)} %get-tuple-element.181.one, bf16[384,768]{1,0:T(8,128)(2,1)} %collective-permute-done.33.one_far, bf16[384,768]{1,0:T(8,128)(2,1)} %get-tuple-element.183.two, ...), custom_call_target="tpu_custom_call" | custom-call | flops 9999999827968 | bytes 1000000000 | tf_op jit(solution)/shard_map/fold_half/pallas_call | solution.py:693
  219.3 6.2 %leave_layer.1 = (f32[512,768]{1,0:T(8,128)}, f32[8,768]{1,0:T(8,128)}) custom-call(s32[1]{0:T(128)} %bitcast.8.core, bf16[1024,768]{1,0:T(8,128)(2,1)} %token_back.1.pulled, bf16[1024,768]{1,0:T(8,128)(2,1)} %collective-permute-done.32.far, f32[1024,768]{1,0:T(8,128)} %maximum_select_fusion.tokens, f32[1024,768]{1,0:T(8,128)} %get-tuple-element.190.middle_grad, ...), custom_call_target="tpu_custom_call" | custom-call | flops 9999999827968 | bytes 1000000000 | tf_op jit(solution)/shard_map/leave_layer/pallas_call | solution.py:647
  231.8 2.8 %collective-permute-start.38 = (bf16[48,1536]{1,0:T(8,128)(2,1)}, bf16[48,1536]{1,0:T(8,128)(2,1)S(1)}, u32[]{:S(2)}, u32[]{:S(2)}) collective-permute-start(bf16[48,1536]{1,0:T(8,128)(2,1)} %get-tuple-element.198), channel_id=1, source_target_pairs={{0,8},{2,10},{4,12},{6,14},{8,0},{10,2},{12,4},{14,6},{16,24},{18,... | collective-permute-start | bytes 442376 | tf_op jit(solution)/shard_map/ppermute | solution.py:673
  242.7 2.7 %collective-permute-done.43 = f32[4,768]{1,0:T(4,128)S(1)} collective-permute-done((f32[4,768]{1,0:T(4,128)S(1)}, f32[4,768]{1,0:T(4,128)S(1)}, u32[]{:S(2)}, u32[]{:S(2)}) %collective-permute-start.43) | collective-permute-done | bytes 12320 | tf_op jit(solution)/shard_map/ppermute | solution.py:673
  246.7 3.4 %collective-permute-done.44 = f32[4,768]{1,0:T(4,128)S(1)} collective-permute-done((f32[4,768]{1,0:T(4,128)S(1)}, f32[4,768]{1,0:T(4,128)S(1)}, u32[]{:S(2)}, u32[]{:S(2)}) %collective-permute-start.44) | collective-permute-done | bytes 12320 | tf_op jit(solution)/shard_map/ppermute | solution.py:673
  (155 shorter events, 84.6 us)
Async XLA Ops:
  0.7 14.6 %collective-permute-start = (f32[512,768]{1,0:T(8,128)}, f32[512,768]{1,0:T(8,128)S(1)}, u32[]{:S(2)}, u32[]{:S(2)}) collective-permute-start(f32[512,768]{1,0:T(8,128)} %param.11), channel_id=1, source_target_pairs={{0,1},{1,0},{2,3},{3,2},{4,5},{5,4},{6,7},{7,6},{8,9},{9,8},{10,11... | collective-permute-start | bytes 4718600 | tf_op jit(solution)/shard_map/ppermute | solution.py:669
  11.3 16.8 %collective-permute-start.11 = (bf16[512,768]{1,0:T(8,128)(2,1)}, bf16[512,768]{1,0:T(8,128)(2,1)}, u32[]{:S(2)}, u32[]{:S(2)}) collective-permute-start(bf16[512,768]{1,0:T(8,128)(2,1)} %param.21), channel_id=1, source_target_pairs={{0,1},{1,0},{2,3},{3,2},{4,5},{5,4},{6,7},{7,6},{8,9},{9,8},{10,11... | collective-permute-start | bytes 2359304 | tf_op jit(solution)/shard_map/ppermute | solution.py:669
  37.9 19.9 %collective-permute-start.6 = (bf16[384,640]{1,0:T(8,128)(2,1)}, bf16[384,640]{1,0:T(8,128)(2,1)}, u32[]{:S(2)}, u32[]{:S(2)}) collective-permute-start(bf16[384,640]{1,0:T(8,128)(2,1)} %get-tuple-element.115.wa), channel_id=1, source_target_pairs={{0,2},{2,0},{4,6},{6,4},{8,10},{10,8},{12,14},{14,12},{16,18},{18,... | collective-permute-start | bytes 1474568 | tf_op jit(solution)/shard_map/ppermute | solution.py:673
  38.5 19.9 %collective-permute-start.7 = (bf16[384,640]{1,0:T(8,128)(2,1)}, bf16[384,640]{1,0:T(8,128)(2,1)}, u32[]{:S(2)}, u32[]{:S(2)}) collective-permute-start(bf16[384,640]{1,0:T(8,128)(2,1)} %get-tuple-element.116.wb), channel_id=1, source_target_pairs={{0,4},{2,6},{4,0},{6,2},{8,12},{10,14},{12,8},{14,10},{16,20},{18,... | collective-permute-start | bytes 1474568 | tf_op jit(solution)/shard_map/ppermute | solution.py:673
  53.4 33.6 %collective-permute-start.16 = (bf16[96,1536]{1,0:T(8,128)(2,1)}, bf16[96,1536]{1,0:T(8,128)(2,1)}, u32[]{:S(2)}, u32[]{:S(2)}) collective-permute-start(bf16[96,1536]{1,0:T(8,128)(2,1)} %beside.1.refs_0_), channel_id=1, source_target_pairs={{0,8},{2,10},{4,12},{6,14},{8,0},{10,2},{12,4},{14,6},{16,24},{18,... | collective-permute-start | bytes 884744 | tf_op jit(solution)/shard_map/ppermute | solution.py:673
  53.4 33.6 %collective-permute-start.17 = (bf16[96,1536]{1,0:T(8,128)(2,1)}, bf16[96,1536]{1,0:T(8,128)(2,1)}, u32[]{:S(2)}, u32[]{:S(2)}) collective-permute-start(bf16[96,1536]{1,0:T(8,128)(2,1)} %beside.1.refs_0_), channel_id=1, source_target_pairs={{0,16},{2,18},{4,20},{6,22},{8,24},{10,26},{12,28},{14,30},{16,0},... | collective-permute-start | bytes 884744 | tf_op jit(solution)/shard_map/ppermute | solution.py:673
  56.3 30.7 %collective-permute-start.18 = (bf16[96,1536]{1,0:T(8,128)(2,1)}, bf16[96,1536]{1,0:T(8,128)(2,1)}, u32[]{:S(2)}, u32[]{:S(2)}) collective-permute-start(bf16[96,1536]{1,0:T(8,128)(2,1)} %beside.1.refs_0_), channel_id=1, source_target_pairs={{0,24},{2,26},{4,28},{6,30},{8,16},{10,18},{12,20},{14,22},{16,8},... | collective-permute-start | bytes 884744 | tf_op jit(solution)/shard_map/ppermute | solution.py:673
  69.9 19.5 %collective-permute-start.19 = (bf16[384,1024]{1,0:T(8,128)(2,1)}, bf16[384,1024]{1,0:T(8,128)(2,1)}, u32[]{:S(2)}, u32[]{:S(2)}) collective-permute-start(bf16[384,1024]{1,0:T(8,128)(2,1)} %get-tuple-element.129.up_a), channel_id=1, source_target_pairs={{0,2},{2,0},{4,6},{6,4},{8,10},{10,8},{12,14},{14,12},{16,18},{18,... | collective-permute-start | bytes 2359304 | tf_op jit(solution)/shard_map/ppermute | solution.py:673
  70.9 18.5 %collective-permute-start.20 = (bf16[384,896]{1,0:T(8,128)(2,1)}, bf16[384,896]{1,0:T(8,128)(2,1)}, u32[]{:S(2)}, u32[]{:S(2)}) collective-permute-start(bf16[384,896]{1,0:T(8,128)(2,1)} %get-tuple-element.130.near.up_b), channel_id=1, source_target_pairs={{0,4},{2,6},{4,0},{6,2},{8,12},{10,14},{12,8},{14,10},{16,20},{18,... | collective-permute-start | bytes 2064392 | tf_op jit(solution)/shard_map/ppermute | solution.py:673
  95.0 16.0 %collective-permute-start.21 = (bf16[1024,768]{1,0:T(8,128)(2,1)}, bf16[1024,768]{1,0:T(8,128)(2,1)S(1)}, u32[]{:S(2)}, u32[]{:S(2)}) collective-permute-start(bf16[1024,768]{1,0:T(8,128)(2,1)} %get-tuple-element.141.part), channel_id=1, source_target_pairs={{0,1},{1,0},{2,3},{3,2},{4,5},{5,4},{6,7},{7,6},{8,9},{9,8},{10,11... | collective-permute-start | bytes 4718600 | tf_op jit(solution)/shard_map/ppermute | solution.py:669
  95.0 15.7 %collective-permute-start.22 = (bf16[384,768]{1,0:T(8,128)(2,1)S(1)}, bf16[384,768]{1,0:T(8,128)(2,1)S(1)}, u32[]{:S(2)}, u32[]{:S(2)}) collective-permute-start(bf16[384,768]{1,0:T(8,128)(2,1)S(1)} %copy-done.11), channel_id=1, source_target_pairs={{0,4},{2,6},{4,0},{6,2},{8,12},{10,14},{12,8},{14,10},{16,20},{18,... | collective-permute-start | bytes 1769480 | tf_op jit(solution)/shard_map/ppermute | solution.py:673
  95.6 15.4 %collective-permute-start.23 = (bf16[384,768]{1,0:T(8,128)(2,1)S(1)}, bf16[384,768]{1,0:T(8,128)(2,1)S(1)}, u32[]{:S(2)}, u32[]{:S(2)}) collective-permute-start(bf16[384,768]{1,0:T(8,128)(2,1)S(1)} %copy-done.12), channel_id=1, source_target_pairs={{0,2},{2,0},{4,6},{6,4},{8,10},{10,8},{12,14},{14,12},{16,18},{18,... | collective-permute-start | bytes 1769480 | tf_op jit(solution)/shard_map/ppermute | solution.py:673
  149.8 30.2 %collective-permute-start.24 = (bf16[384,1536]{1,0:T(8,128)(2,1)}, bf16[384,1536]{1,0:T(8,128)(2,1)}, u32[]{:S(2)}, u32[]{:S(2)}) collective-permute-start(bf16[384,1536]{1,0:T(8,128)(2,1)} %get-tuple-element.147), channel_id=1, source_target_pairs={{0,2},{2,0},{4,6},{6,4},{8,10},{10,8},{12,14},{14,12},{16,18},{18,... | collective-permute-start | bytes 3538952 | tf_op jit(solution)/shard_map/ppermute | solution.py:673
  150.9 29.1 %collective-permute-start.25 = (bf16[384,1536]{1,0:T(8,128)(2,1)}, bf16[384,1536]{1,0:T(8,128)(2,1)}, u32[]{:S(2)}, u32[]{:S(2)}) collective-permute-start(bf16[384,1536]{1,0:T(8,128)(2,1)} %get-tuple-element.149), channel_id=1, source_target_pairs={{0,4},{2,6},{4,0},{6,2},{8,12},{10,14},{12,8},{14,10},{16,20},{18,... | collective-permute-start | bytes 3538952 | tf_op jit(solution)/shard_map/ppermute | solution.py:673
  183.9 16.5 %collective-permute-start.27 = (bf16[192,1536]{1,0:T(8,128)(2,1)}, bf16[192,1536]{1,0:T(8,128)(2,1)}, u32[]{:S(2)}, u32[]{:S(2)}) collective-permute-start(bf16[192,1536]{1,0:T(8,128)(2,1)} %get-tuple-element.159), channel_id=1, source_target_pairs={{0,4},{2,6},{4,0},{6,2},{8,12},{10,14},{12,8},{14,10},{16,20},{18,... | collective-permute-start | bytes 1769480 | tf_op jit(solution)/shard_map/ppermute | solution.py:673
  185.4 16.5 %collective-permute-start.28 = (bf16[192,1536]{1,0:T(8,128)(2,1)}, bf16[192,1536]{1,0:T(8,128)(2,1)}, u32[]{:S(2)}, u32[]{:S(2)}) collective-permute-start(bf16[192,1536]{1,0:T(8,128)(2,1)} %get-tuple-element.161), channel_id=1, source_target_pairs={{0,2},{2,0},{4,6},{6,4},{8,10},{10,8},{12,14},{14,12},{16,18},{18,... | collective-permute-start | bytes 1769480 | tf_op jit(solution)/shard_map/ppermute | solution.py:673
  193.7 21.3 %collective-permute-start.33 = (bf16[384,768]{1,0:T(8,128)(2,1)}, bf16[384,768]{1,0:T(8,128)(2,1)}, u32[]{:S(2)}, u32[]{:S(2)}) collective-permute-start(bf16[384,768]{1,0:T(8,128)(2,1)} %get-tuple-element.167), channel_id=1, source_target_pairs={{0,2},{2,0},{4,6},{6,4},{8,10},{10,8},{12,14},{14,12},{16,18},{18,... | collective-permute-start | bytes 1769480 | tf_op jit(solution)/shard_map/ppermute | solution.py:673
  195.2 19.8 %collective-permute-start.34 = (bf16[384,768]{1,0:T(8,128)(2,1)}, bf16[384,768]{1,0:T(8,128)(2,1)}, u32[]{:S(2)}, u32[]{:S(2)}) collective-permute-start(bf16[384,768]{1,0:T(8,128)(2,1)} %get-tuple-element.169), channel_id=1, source_target_pairs={{0,4},{2,6},{4,0},{6,2},{8,12},{10,14},{12,8},{14,10},{16,20},{18,... | collective-permute-start | bytes 1769480 | tf_op jit(solution)/shard_map/ppermute | solution.py:673
  204.5 25.7 %collective-permute-start.29 = (bf16[48,3072]{1,0:T(8,128)(2,1)}, bf16[48,3072]{1,0:T(8,128)(2,1)}, u32[]{:S(2)}, u32[]{:S(2)}) collective-permute-start(bf16[48,3072]{1,0:T(8,128)(2,1)} %get-tuple-element.175), channel_id=1, source_target_pairs={{0,8},{2,10},{4,12},{6,14},{8,0},{10,2},{12,4},{14,6},{16,24},{18,... | collective-permute-start | bytes 884744 | tf_op jit(solution)/shard_map/ppermute | solution.py:673
  204.5 25.7 %collective-permute-start.30 = (bf16[48,3072]{1,0:T(8,128)(2,1)}, bf16[48,3072]{1,0:T(8,128)(2,1)}, u32[]{:S(2)}, u32[]{:S(2)}) collective-permute-start(bf16[48,3072]{1,0:T(8,128)(2,1)} %get-tuple-element.176), channel_id=1, source_target_pairs={{0,16},{2,18},{4,20},{6,22},{8,24},{10,26},{12,28},{14,30},{16,0},... | collective-permute-start | bytes 884744 | tf_op jit(solution)/shard_map/ppermute | solution.py:673
  207.4 22.8 %collective-permute-start.31 = (bf16[48,3072]{1,0:T(8,128)(2,1)}, bf16[48,3072]{1,0:T(8,128)(2,1)}, u32[]{:S(2)}, u32[]{:S(2)}) collective-permute-start(bf16[48,3072]{1,0:T(8,128)(2,1)} %get-tuple-element.177), channel_id=1, source_target_pairs={{0,24},{2,26},{4,28},{6,30},{8,16},{10,18},{12,20},{14,22},{16,8},... | collective-permute-start | bytes 884744 | tf_op jit(solution)/shard_map/ppermute | solution.py:673
  231.8 18.9 %collective-permute-start.38 = (bf16[48,1536]{1,0:T(8,128)(2,1)}, bf16[48,1536]{1,0:T(8,128)(2,1)S(1)}, u32[]{:S(2)}, u32[]{:S(2)}) collective-permute-start(bf16[48,1536]{1,0:T(8,128)(2,1)} %get-tuple-element.198), channel_id=1, source_target_pairs={{0,8},{2,10},{4,12},{6,14},{8,0},{10,2},{12,4},{14,6},{16,24},{18,... | collective-permute-start | bytes 442376 | tf_op jit(solution)/shard_map/ppermute | solution.py:673
  234.6 16.1 %collective-permute-start.39 = (bf16[48,1536]{1,0:T(8,128)(2,1)}, bf16[48,1536]{1,0:T(8,128)(2,1)S(1)}, u32[]{:S(2)}, u32[]{:S(2)}) collective-permute-start(bf16[48,1536]{1,0:T(8,128)(2,1)} %get-tuple-element.199), channel_id=1, source_target_pairs={{0,16},{2,18},{4,20},{6,22},{8,24},{10,26},{12,28},{14,30},{16,0},... | collective-permute-start | bytes 442376 | tf_op jit(solution)/shard_map/ppermute | solution.py:673
  235.7 15.0 %collective-permute-start.40 = (bf16[48,1536]{1,0:T(8,128)(2,1)}, bf16[48,1536]{1,0:T(8,128)(2,1)S(1)}, u32[]{:S(2)}, u32[]{:S(2)}) collective-permute-start(bf16[48,1536]{1,0:T(8,128)(2,1)} %get-tuple-element.200), channel_id=1, source_target_pairs={{0,24},{2,26},{4,28},{6,30},{8,16},{10,18},{12,20},{14,22},{16,8},... | collective-permute-start | bytes 442376 | tf_op jit(solution)/shard_map/ppermute | solution.py:673
  (36 other events, 288.0 us)

commit v2 on v1

--- a/solution.py
+++ b/solution.py
@@ -14,6 +14,7 @@
 WIDE = jnp.float32
 BLOCKS = 16
 ROWS = 256
+TILE = 32
 LANES = 128
 LOG2E = math.log2(math.e)
 LEFT, RIGHT, DOWN_LEFT, DOWN_RIGHT = (BLOCKS * k for k in range(4))
@@ -37,7 +38,7 @@
 
 def params():
     return pltpu.CompilerParams(
-        dimension_semantics=("arbitrary",), vmem_limit_bytes=60 * 1024 * 1024
+        dimension_semantics=("arbitrary",), vmem_limit_bytes=24 * 1024 * 1024
     )
 
 
@@ -59,6 +60,17 @@
     centre = values - jnp.mean(values, axis=-1, keepdims=True)
     rate = lax.rsqrt(jnp.mean(centre * centre, axis=-1, keepdims=True) + EPS)
     return centre * rate, rate
+
+
+def tiles(rows):
+    return [slice(start, start + TILE) for start in range(0, rows, TILE)]
+
+
+def fold_rows(values):
+    total = values[:8]
+    for start in range(8, values.shape[0], 8):
+        total = total + values[start : start + 8]
+    return total
 
 
 def norm_back(grad, hat, rate, gain):
@@ -89,7 +101,7 @@
         send[at, :] = values
 
 
-def enter_kernel(table, tokens, wa, wa2, wb, wb2, normed, proj, whole, vectors, loose):
+def enter_kernel(table, tokens, wa, wa2, wb, wb2, flip, proj, whole, vectors, loose, normed):
     step = pl.program_id(0)
     rows = wa.shape[0] // (BLOCKS // 2)
     cut = wa.shape[1]
@@ -105,10 +117,11 @@
             loose[to, :] = late[:, rest:].astype(WIDE)
         vectors[...] = loose[...].T[:8]
 
-    hat, _ = hat_of(tokens[...])
-    low = (hat * vectors[0:1, :] + vectors[1:2, :]).astype(LOW)
-    normed[...] = low
-    proj[...] = nn(low, whole[...]).astype(LOW)
+    for at in tiles(tokens.shape[0]):
+        hat, _ = hat_of(tokens[at, :])
+        normed[at, :] = (hat * vectors[0:1, :] + vectors[1:2, :]).astype(LOW)
+    proj[...] = nn(normed[...], whole[...]).astype(LOW)
+    flip[...] = normed[...].T
 
 
 def enter(table, tokens, *pieces):
@@ -120,11 +133,16 @@
             num_scalar_prefetch=1,
             grid=(length // ROWS,),
             in_specs=[by_row(width)] + [fixed(piece.shape) for piece in pieces],
-            out_specs=[by_row(width), by_row(total), kept((width, total)), kept((8, width))],
-            scratch_shapes=[pltpu.VMEM((width, LANES), WIDE)],
+            out_specs=[
+                pl.BlockSpec((width, ROWS), lambda i, *_: (0, i)),
+                by_row(total),
+                kept((width, total)),
+                kept((8, width)),
+            ],
+            scratch_shapes=[pltpu.VMEM((width, LANES), WIDE), pltpu.VMEM((ROWS, width), LOW)],
         ),
         out_shape=[
-            jax.ShapeDtypeStruct((length, width), LOW),
+            jax.ShapeDtypeStruct((width, length), LOW),
             jax.ShapeDtypeStruct((length, total), LOW),
             jax.ShapeDtypeStruct((width, total), LOW),
             jax.ShapeDtypeStruct((8, width), WIDE),
@@ -208,7 +226,7 @@
 
 
 def attend_back_kernel(
-    queries, keys, values, out, grad, lse, seg_col, seg_row, result, bias, k_sum, v_sum
+    queries, keys, values, out, grad, lse, seg_col, seg_row, result, bias, soft, pull
 ):
     @pl.when(pl.program_id(0) == 0)
     def _():
@@ -220,29 +238,34 @@
     k_flip = keys[...].T
     g_flip = grad[...].T
     product = out[...].T.astype(WIDE) * g_flip.astype(WIDE)
-    k_sum[...] = jnp.zeros_like(k_sum)
-    v_sum[...] = jnp.zeros_like(v_sum)
-    q_sides = [one_head(q_flip, head) for head in range(2)]
-    g_sides = [one_head(g_flip, head) for head in range(2)]
-    for start in range(0, length, ROWS):
-        lanes = slice(start, start + ROWS)
-        until = start + ROWS
-        pieces = []
-        for head in range(2):
-            scores = nn(keys[:until], q_sides[head][:, lanes]) * (scale * LOG2E)
-            probs = jnp.exp2(scores + bias[:until, lanes] - lse[head : head + 1, lanes])
-            v_sum[head, :until] += nn(probs.astype(LOW), grad[lanes, :])
-            centre = jnp.sum(
-                product[head * HD : (head + 1) * HD, lanes], axis=0, keepdims=True
-            )
-            pull = nn(values[:until], g_sides[head][:, lanes])
-            pull = (probs * (pull - centre)).astype(LOW)
-            k_sum[head, :until] += nn(pull, queries[lanes, :])
-            pieces.append(nn(k_flip[head * HD : (head + 1) * HD, :until], pull))
-        result[0, lanes, :] = (jnp.concatenate(pieces, axis=0) * scale).T.astype(LOW)
-    first = lax.broadcasted_iota(jnp.int32, (length, LANES), 1) < HD
-    result[1] = (jnp.where(first, k_sum[0], k_sum[1]) * scale).astype(LOW)
-    result[2] = jnp.where(first, v_sum[0], v_sum[1]).astype(LOW)
+    first = lax.broadcasted_iota(jnp.int32, (ROWS, LANES), 1) < HD
+    starts = range(0, length, ROWS)
+    for head in range(2):
+        q_side = one_head(q_flip, head)
+        g_side = one_head(g_flip, head)
+        centre = jnp.sum(product[head * HD : (head + 1) * HD], axis=0, keepdims=True)
+        level = lse[head : head + 1, :]
+        for low in starts:
+            at = slice(low, low + ROWS)
+            for start in range(low, length, ROWS):
+                lanes = slice(start, start + ROWS)
+                scores = nn(keys[at], q_side[:, lanes]) * (scale * LOG2E)
+                probs = jnp.exp2(scores + bias[at, lanes] - level[:, lanes])
+                soft[head, at, lanes] = probs.astype(LOW)
+                drawn = nn(values[at], g_side[:, lanes])
+                pull[head, at, lanes] = (probs * (drawn - centre[:, lanes])).astype(LOW)
+    for low in starts:
+        at = slice(low, low + ROWS)
+        k_parts = [nn(pull[head, at, low:], queries[low:, :]) for head in range(2)]
+        v_parts = [nn(soft[head, at, low:], grad[low:, :]) for head in range(2)]
+        result[1, at] = (jnp.where(first, *k_parts) * scale).astype(LOW)
+        result[2, at] = jnp.where(first, *v_parts).astype(LOW)
+        until = low + ROWS
+        pieces = [
+            nn(k_flip[head * HD : (head + 1) * HD, :until], pull[head, :until, at])
+            for head in range(2)
+        ]
+        result[0, at] = (jnp.concatenate(pieces, axis=0) * scale).T.astype(LOW)
 
 
 def attend_back(proj, out, grad, lse, seg_col, seg_row):
@@ -269,8 +292,8 @@
         out_shape=jax.ShapeDtypeStruct((3, length, pairs * LANES), LOW),
         scratch_shapes=[
             pltpu.VMEM((length, length), WIDE),
-            pltpu.VMEM((2, length, LANES), WIDE),
-            pltpu.VMEM((2, length, LANES), WIDE),
+            pltpu.VMEM((2, length, length), LOW),
+            pltpu.VMEM((2, length, length), LOW),
         ],
         compiler_params=params(),
         cost_estimate=LONG,
@@ -313,103 +336,147 @@
     )(table, att, near, far)
 
 
-def middle_kernel(tokens, part, far, vectors, middle, normed):
-    values = tokens[...] + (part[...].astype(WIDE) + far[...].astype(WIDE))
-    middle[...] = values
-    hat, _ = hat_of(values)
-    normed[...] = (hat * vectors[2:3, :] + vectors[3:4, :]).astype(LOW)
-
-
-def second_norm(tokens, part, far, vectors):
-    length, width = part.shape
-    return pl.pallas_call(
-        middle_kernel,
-        grid=(length // ROWS,),
-        in_specs=[by_row(width), by_row(width), by_row(width), fixed((8, width))],
-        out_specs=[by_row(width), by_row(width)],
-        out_shape=[
-            jax.ShapeDtypeStruct((length, width), WIDE),
-            jax.ShapeDtypeStruct((length, width), LOW),
-        ],
-        compiler_params=params(),
-        cost_estimate=LONG,
-        name="second_norm",
-    )(tokens, part, far, vectors)
-
-
 SIDE = 256
 
 
-def feed_kernel(
+def unpack(table, whole, left, right, near_a, far_a, near_b, far_b):
+    rows = near_a.shape[0] // (BLOCKS // 2)
+    cut = min(near_a.shape[1], whole.shape[1])
+    for j in range(BLOCKS):
+        to = slice(j * rows, (j + 1) * rows)
+        whole[to, :cut] = take(table, left + j, rows, near_a, far_a)
+        lanes = slice(0, whole.shape[1] - cut)
+        whole[to, cut:] = take(table, right + j, rows, near_b, far_b, lanes)
+
+
+def feed_first_kernel(
     table,
-    normed,
-    grad,
+    tokens,
+    part,
+    far,
+    vectors,
     up_a,
     up_a2,
     up_b,
     up_b2,
+    middle,
+    flip,
+    act,
+    slope,
+    whole,
+    normed,
+):
+    @pl.when(pl.program_id(0) == 0)
+    def _():
+        unpack(table, whole, LEFT, RIGHT, up_a, up_a2, up_b, up_b2)
+
+    for at in tiles(tokens.shape[0]):
+        values = tokens[at, :] + (part[at, :].astype(WIDE) + far[at, :].astype(WIDE))
+        middle[at, :] = values
+        hat, _ = hat_of(values)
+        normed[at, :] = (hat * vectors[2:3, :] + vectors[3:4, :]).astype(LOW)
+    root = math.sqrt(2.0 / math.pi)
+    for start in range(0, whole.shape[1], SIDE):
+        lanes = slice(start, start + SIDE)
+        wide = nn(normed[...], whole[:, lanes])
+        square = wide * wide
+        bend = jnp.tanh(wide * (root + root * 0.044715 * square))
+        share = 0.5 + 0.5 * bend
+        act[:, lanes] = (wide * share).astype(LOW)
+        slope[:, lanes] = (
+            share + 0.5 * wide * (1.0 - bend * bend) * (root + 3.0 * root * 0.044715 * square)
+        ).astype(LOW)
+    flip[...] = normed[...].T
+
+
+def feed_first(table, tokens, part, far, vectors, hidden, *pieces):
+    length, width = part.shape
+    return pl.pallas_call(
+        feed_first_kernel,
+        grid_spec=pltpu.PrefetchScalarGridSpec(
+            num_scalar_prefetch=1,
+            grid=(length // ROWS,),
+            in_specs=[by_row(width), by_row(width), by_row(width), fixed((8, width))]
+            + [fixed(piece.shape) for piece in pieces],
+            out_specs=[
+                by_row(width),
+                pl.BlockSpec((width, ROWS), lambda i, *_: (0, i)),
+                by_row(hidden),
+                by_row(hidden),
+                kept((width, hidden)),
+            ],
+            scratch_shapes=[pltpu.VMEM((ROWS, width), LOW)],
+        ),
+        out_shape=[
+            jax.ShapeDtypeStruct((length, width), WIDE),
+            jax.ShapeDtypeStruct((width, length), LOW),
+            jax.ShapeDtypeStruct((length, hidden), LOW),
+            jax.ShapeDtypeStruct((length, hidden), LOW),
+            jax.ShapeDtypeStruct((width, hidden), LOW),
+        ],
+        compiler_params=params(),
+        cost_estimate=LONG,
+        name="feed_first",
+    )(table, tokens, part, far, vectors, *pieces)
+
+
+def feed_tokens_kernel(
+    table,
+    grad,
+    act,
+    slope,
+    up,
     down_a,
     down_a2,
     down_b,
     down_b2,
     branch,
     pulled,
-    up_keep,
-    up_send,
-    down_keep,
-    down_send,
-    normed_flip,
-    grad_flip,
-    up_whole,
-    down_whole,
-    act,
     pre,
-    branch_sum,
-    pulled_sum,
+    whole,
 ):
-    step = pl.program_id(0)
-    length = normed.shape[0]
-    rows = up_a.shape[0] // (BLOCKS // 2)
-
-    @pl.when(step == 0)
-    def _():
-        normed_flip[...] = normed[...].T
-        grad_flip[...] = grad[...].T
-        branch_sum[...] = jnp.zeros_like(branch_sum)
-        pulled_sum[...] = jnp.zeros_like(pulled_sum)
-        up_cut = up_a.shape[1] // SIDE
-        down_cut = down_a.shape[1] // SIDE
-        for k in range(up_whole.shape[0]):
-            for j in range(BLOCKS):
-                to = slice(j * rows, (j + 1) * rows)
-                pair, spot = ((up_a, up_a2), k) if k < up_cut else ((up_b, up_b2), k - up_cut)
-                lanes = slice(spot * SIDE, (spot + 1) * SIDE)
-                up_whole[k, to, :] = take(
-                    table, (RIGHT if k >= up_cut else LEFT) + j, rows, *pair, lanes
-                )
-                pair, spot = (
-                    ((down_a, down_a2), k) if k < down_cut else ((down_b, down_b2), k - down_cut)
-                )
-                lanes = slice(spot * SIDE, (spot + 1) * SIDE)
-                down_whole[k, to, :] = take(
-                    table, (DOWN_RIGHT if k >= down_cut else DOWN_LEFT) + j, rows, *pair, lanes
-                )
-
-    for start in range(0, length, ROWS):
-        at = slice(start, start + ROWS)
-        wide = nn(normed[at, :], up_whole[step])
-        square = wide * wide
-        root = math.sqrt(2.0 / math.pi)
-        bend = jnp.tanh(wide * (root + root * 0.044715 * square))
-        share = 0.5 + 0.5 * bend
-        slope = share + 0.5 * wide * (1.0 - bend * bend) * (
-            root + 3.0 * root * 0.044715 * square
-        )
-        act[at, :] = (wide * share).astype(LOW)
-        pre[at, :] = (nn(grad[at, :], down_whole[step]) * slope).astype(LOW)
-        branch_sum[at, :] += nt(act[at, :], down_whole[step])
-        pulled_sum[at, :] += nt(pre[at, :], up_whole[step])
-
+    @pl.when(pl.program_id(0) == 0)
+    def _():
+        unpack(table, whole, DOWN_LEFT, DOWN_RIGHT, down_a, down_a2, down_b, down_b2)
+
+    for start in range(0, whole.shape[1], SIDE):
+        lanes = slice(start, start + SIDE)
+        drawn = nn(grad[...], whole[:, lanes])
+        pre[:, lanes] = (drawn * slope[:, lanes].astype(WIDE)).astype(LOW)
+    for start in range(0, whole.shape[0], SIDE):
+        lanes = slice(start, start + SIDE)
+        branch[:, lanes] = nt(act[...], whole[lanes, :]).astype(LOW)
+        pulled[:, lanes] = nt(pre[...], up[lanes, :]).astype(LOW)
+
+
+def feed_tokens(table, grad, act, slope, up, *pieces):
+    length, width = grad.shape
+    hidden = act.shape[1]
+    return pl.pallas_call(
+        feed_tokens_kernel,
+        grid_spec=pltpu.PrefetchScalarGridSpec(
+            num_scalar_prefetch=1,
+            grid=(length // ROWS,),
+            in_specs=[by_row(width), by_row(hidden), by_row(hidden), fixed(up.shape)]
+            + [fixed(piece.shape) for piece in pieces],
+            out_specs=[by_row(width), by_row(width), by_row(hidden)],
+            scratch_shapes=[pltpu.VMEM((width, hidden), LOW)],
+        ),
+        out_shape=[
+            jax.ShapeDtypeStruct((length, width), LOW),
+            jax.ShapeDtypeStruct((length, width), LOW),
+            jax.ShapeDtypeStruct((length, hidden), LOW),
+        ],
+        compiler_params=params(),
+        cost_estimate=LONG,
+        name="feed_tokens",
+    )(table, grad, act, slope, up, *pieces)
+
+
+def feed_weights_kernel(
+    table, normed_flip, grad_flip, act, pre, up_keep, up_send, down_keep, down_send
+):
+    rows = normed_flip.shape[0] // BLOCKS
     lifted = nn(normed_flip[...], pre[...]).astype(LOW)
     lowered = nn(grad_flip[...], act[...]).astype(LOW)
     for j in range(BLOCKS):
@@ -417,42 +484,25 @@
         put(table, LEFT + j, rows, up_keep, up_send, lifted[block])
         put(table, RIGHT + j, rows, down_keep, down_send, lowered[block])
 
-    @pl.when(step == pl.num_programs(0) - 1)
-    def _():
-        branch[...] = branch_sum[...].astype(LOW)
-        pulled[...] = pulled_sum[...].astype(LOW)
-
-
-def feed(table, normed, grad, *pieces):
-    length, width = normed.shape
-    hidden = pieces[4].shape[1] + pieces[6].shape[1]
-    column = pl.BlockSpec((width // 2, SIDE), lambda i, *_: (0, i))
-    token = (length, width)
-    steps = hidden // SIDE
-    return pl.pallas_call(
-        feed_kernel,
+
+def feed_weights(table, normed_flip, grad_flip, act, pre):
+    width, length = normed_flip.shape
+    hidden = act.shape[1]
+    column = pl.BlockSpec((length, SIDE), lambda i, *_: (0, i))
+    half = pl.BlockSpec((width // 2, SIDE), lambda i, *_: (0, i))
+    return pl.pallas_call(
+        feed_weights_kernel,
         grid_spec=pltpu.PrefetchScalarGridSpec(
             num_scalar_prefetch=1,
-            grid=(steps,),
-            in_specs=[fixed(token), fixed(token)] + [fixed(piece.shape) for piece in pieces],
-            out_specs=[kept(token), kept(token), column, column, column, column],
-            scratch_shapes=[
-                pltpu.VMEM((width, length), LOW),
-                pltpu.VMEM((width, length), LOW),
-                pltpu.VMEM((steps, width, SIDE), LOW),
-                pltpu.VMEM((steps, width, SIDE), LOW),
-                pltpu.VMEM((length, SIDE), LOW),
-                pltpu.VMEM((length, SIDE), LOW),
-                pltpu.VMEM(token, WIDE),
-                pltpu.VMEM(token, WIDE),
-            ],
+            grid=(hidden // SIDE,),
+            in_specs=[fixed((width, length)), fixed((width, length)), column, column],
+            out_specs=[half] * 4,
         ),
-        out_shape=[jax.ShapeDtypeStruct(token, LOW)] * 2
-        + [jax.ShapeDtypeStruct((width // 2, hidden), LOW)] * 4,
+        out_shape=[jax.ShapeDtypeStruct((width // 2, hidden), LOW)] * 4,
         compiler_params=params(),
         cost_estimate=LONG,
-        name="feed",
-    )(table, normed, grad, *pieces)
+        name="feed_weights",
+    )(table, normed_flip, grad_flip, act, pre)
 
 
 def middle_back_kernel(
@@ -470,6 +520,8 @@
     out_send,
     sums,
     out_sum,
+    low,
+    gathered,
 ):
     step = pl.program_id(0)
     rows = out_whole.shape[0] // BLOCKS
@@ -477,23 +529,26 @@
     @pl.when(step == 0)
     def _():
         out_sum[...] = jnp.zeros_like(out_sum)
-        sums[...] = jnp.zeros_like(sums)
-
-    pull = pulled[...].astype(WIDE) + far[...].astype(WIDE)
-    hat, rate = hat_of(middle[...])
-    whole = grad[...].astype(WIDE) + norm_back(pull, hat, rate, vectors[2:3, :])
-    middle_grad[...] = whole
-    sums[0:1, :] += jnp.sum(pull * hat, axis=0, keepdims=True)
-    sums[1:2, :] += jnp.sum(pull, axis=0, keepdims=True)
-    low = whole.astype(LOW)
-    att_grad[...] = nn(low, out_whole[...]).astype(LOW)
-    out_sum[...] += tn(low, att[...])
+        gathered[...] = jnp.zeros_like(gathered)
+
+    for at in tiles(middle.shape[0]):
+        pull = pulled[at, :].astype(WIDE) + far[at, :].astype(WIDE)
+        hat, rate = hat_of(middle[at, :])
+        whole = grad[at, :].astype(WIDE) + norm_back(pull, hat, rate, vectors[2:3, :])
+        middle_grad[at, :] = whole
+        low[at, :] = whole.astype(LOW)
+        gathered[:8, :] += fold_rows(pull * hat)
+        gathered[8:, :] += fold_rows(pull)
+    att_grad[...] = nn(low[...], out_whole[...]).astype(LOW)
+    out_sum[...] += tn(low[...], att[...])
 
     @pl.when(step == pl.num_programs(0) - 1)
     def _():
         for j in range(BLOCKS):
             block = out_sum[j * rows : (j + 1) * rows, :].astype(LOW)
             put(table, RIGHT + j, rows, out_keep, out_send, block)
+        sums[0:1, :] = jnp.sum(gathered[:8, :], axis=0, keepdims=True)
+        sums[1:2, :] = jnp.sum(gathered[8:, :], axis=0, keepdims=True)
 
 
 def middle_back(table, pulled, far, middle, grad, vectors, out_whole, att):
@@ -520,7 +575,11 @@
                 kept((width // 2, inner), (0, 1)),
                 kept((8, width)),
             ],
-            scratch_shapes=[pltpu.VMEM((width, inner), WIDE)],
+            scratch_shapes=[
+                pltpu.VMEM((width, inner), WIDE),
+                pltpu.VMEM((ROWS, width), LOW),
+                pltpu.VMEM((16, width), WIDE),
+            ],
         ),
         out_shape=[
             jax.ShapeDtypeStruct((length, width), WIDE),
@@ -538,22 +597,16 @@
 def weight_back_kernel(
     table,
     proj_grad,
-    normed,
+    normed_flip,
     held_keep,
     held_send,
     left_keep,
     left_send,
     right_keep,
     right_send,
-    normed_flip,
 ):
     step = pl.program_id(0)
-    rows = normed.shape[1] // BLOCKS
-
-    @pl.when(step == 0)
-    def _():
-        normed_flip[...] = normed[...].T
-
+    rows = normed_flip.shape[0] // BLOCKS
     weight = nn(normed_flip[...], proj_grad[0]).astype(LOW)
 
     @pl.when(step < 2)
@@ -568,8 +621,8 @@
             put(table, RIGHT + j, rows, right_keep, right_send, block)
 
 
-def weight_back(table, proj_grad, normed, held_keep, held_send):
-    length, width = normed.shape
+def weight_back(table, proj_grad, normed_flip, held_keep, held_send):
+    width, length = normed_flip.shape
     inner = proj_grad.shape[2]
     early = pl.BlockSpec((width // 2, inner), lambda i, *_: (0, jnp.minimum(i, 1)))
     late = kept((width // 2, inner))
@@ -580,19 +633,18 @@
             grid=(3,),
             in_specs=[
                 pl.BlockSpec((1, length, inner), lambda i, *_: (i, 0, 0)),
-                fixed((length, width)),
+                fixed((width, length)),
                 pl.BlockSpec(memory_space=pl.ANY),
                 pl.BlockSpec(memory_space=pl.ANY),
             ],
             out_specs=[early, early, late, late],
-            scratch_shapes=[pltpu.VMEM((width, length), LOW)],
         ),
         out_shape=[jax.ShapeDtypeStruct((width // 2, 2 * inner), LOW)] * 4,
         input_output_aliases={3: 2, 4: 3},
         compiler_params=params(),
         cost_estimate=LONG,
         name="weight_back",
-    )(table, proj_grad, normed, held_keep, held_send)
+    )(table, proj_grad, normed_flip, held_keep, held_send)
 
 
 def token_back_kernel(proj_grad, whole, pulled):
@@ -621,18 +673,24 @@
     )(proj_grad, whole)
 
 
-def exit_kernel(core, pulled, far, tokens, middle_grad, vectors, result, sums):
+def exit_kernel(core, pulled, far, tokens, middle_grad, vectors, result, sums, gathered):
     step = pl.program_id(0)
 
     @pl.when(step == 0)
     def _():
-        sums[...] = jnp.zeros_like(sums)
-
-    pull = pulled[...].astype(WIDE) + far[...].astype(WIDE)
-    hat, rate = hat_of(tokens[...])
-    sums[0:1, :] += jnp.sum(pull * hat, axis=0, keepdims=True)
-    sums[1:2, :] += jnp.sum(pull, axis=0, keepdims=True)
-    result[...] = middle_grad[...] + norm_back(pull, hat, rate, vectors[0:1, :])
+        gathered[...] = jnp.zeros_like(gathered)
+
+    for at in tiles(tokens.shape[0]):
+        pull = pulled[at, :].astype(WIDE) + far[at, :].astype(WIDE)
+        hat, rate = hat_of(tokens[at, :])
+        gathered[:8, :] += fold_rows(pull * hat)
+        gathered[8:, :] += fold_rows(pull)
+        result[at, :] = middle_grad[at, :] + norm_back(pull, hat, rate, vectors[0:1, :])
+
+    @pl.when(step == pl.num_programs(0) - 1)
+    def _():
+        sums[0:1, :] = jnp.sum(gathered[:8, :], axis=0, keepdims=True)
+        sums[1:2, :] = jnp.sum(gathered[8:, :], axis=0, keepdims=True)
 
 
 def leave_layer(core, pulled, far, tokens, middle_grad, vectors):
@@ -654,6 +712,7 @@
                 pl.BlockSpec((ROWS, width), lambda i, *_: (jnp.maximum(i - part, 0), 0)),
                 kept((8, width)),
             ],
+            scratch_shapes=[pltpu.VMEM((16, width), WIDE)],
         ),
         out_shape=[
             jax.ShapeDtypeStruct((length // 2, width), WIDE),
@@ -693,7 +752,7 @@
     return pl.pallas_call(
         kernel,
         out_shape=shapes,
-        compiler_params=pltpu.CompilerParams(vmem_limit_bytes=60 * 1024 * 1024),
+        compiler_params=pltpu.CompilerParams(vmem_limit_bytes=24 * 1024 * 1024),
         cost_estimate=LONG,
         name=name,
     )(*args)
@@ -908,14 +967,15 @@
     third = beside(*third, size)
     qkv = join(*second_stage(*qkv, size), size)
     grad = in_order(cotangent, core)
+    grad_flip = grad.T
     seg_col = jnp.broadcast_to(segment_ids[:, None], (length, LANES))
     seg_row = jnp.broadcast_to(segment_ids[None, :], (8, length))
-    up_out = collect(after(second, qkv, grad, seg_col, seg_row), SIDE * (-(-second[0].shape[1] // (2 * SIDE))))
+    up_out = collect(after(second, qkv, grad, grad_flip, seg_col, seg_row), SIDE * (-(-second[0].shape[1] // (2 * SIDE))))
     third = far_rows(after(third, up_out), size)
     qkv = third_stage(*qkv, size)
     up_out = second_stage(*up_out, size)
 
-    normed_one, proj, qkv_whole, vectors = enter(table, tokens, *qkv)
+    one_flip, proj, qkv_whole, vectors = enter(table, tokens, *qkv)
     up_out = join(*after(up_out, proj), size)
     proj = after(proj, up_out)
     up_out = third_stage(*up_out, size)
@@ -924,19 +984,23 @@
     att = after(att, down, up_out)
     down = second_stage(*down, size)
     part, out_whole = leave(table, att, *up_out[2:])
-    far = after(swap_cores(part), down)
-    middle, normed_two = second_norm(tokens, part, far, vectors)
-    branch, pulled, *parts = feed(table, normed_two, grad, *up_out, *down)
+    far = swap_cores(part)
+    middle, two_flip, act, slope, up_whole = feed_first(
+        table, tokens, part, far, vectors, hidden, *up_out
+    )
+    branch, pulled, pre = feed_tokens(table, grad, act, slope, up_whole, *after(down, act))
+    parts = feed_weights(table, two_flip, grad_flip, act, pre)
+    far = after(swap_cores(pulled), parts)
     parts = first_send(*parts, size)
 
     middle_grad, att_grad, *held, sums_two = middle_back(
-        table, pulled, swap_cores(pulled), middle, grad, vectors, out_whole, att
+        table, pulled, far, middle, grad, vectors, out_whole, att
     )
     proj_grad = attend_back(proj, att, att_grad, lse, seg_col, seg_row)
     parts = fold_half(*after(parts, proj_grad), size)
     proj_grad = after(proj_grad, parts)
     parts = second_send(*parts, size)
-    tail = weight_back(table, proj_grad, normed_one, *held)
+    tail = weight_back(table, proj_grad, one_flip, *held)
     parts = fold_quarter(*after(parts, tail), size)
     tail = first_send(*tail, size)
     proj_grad = after(proj_grad, parts)

time: 255 us -> 230 us (0.902)
  Pallas kernels: 135 us -> 109 us
    pallas_call x2 -> x3, Pallas kernels: 36.7 us -> 31.5 us  [the longest x1 11.1 us: feed_tokens(): pl.pallas_call(feed_tokens_kernel, grid_spec=pltpu.PrefetchScalarGridSpec...]
    pallas_call x10, Pallas kernels: 24.3 us -> 20.2 us  [vmem_call(): pl.pallas_call(kernel, out_shape=shapes, compiler_params=pltpu.CompilerPa...]
    pallas_call x1, Pallas kernels: 15.4 us -> 11.5 us  [attend_back(): pl.pallas_call(attend_back_kernel, grid=(pairs,), in_specs=[part(0), part...]
  transfers between devices with their start and end apart: 45 -> 45, of which waited for: 15 -> 18; matrix products, arithmetic and copies ran while one was open for 8% -> 9% of each run, Pallas kernels for 35% -> 40%
where the time goes in v2:
time: 230 us; the launch traced here: 229 us
  Pallas kernels  109 us (47%)
  starting transfers between devices  50.5 us (22%)
  waiting for transfers between devices  44 us (19%)
  other arithmetic  15.3 us (7%)
  local copies, waits for them, and re-layouts  9.56 us (4%)
    ppermute x39, starting transfers between devices, hop(): return lax.ppermute(values, 'fsdp', [(i, i ^ bits) for i in range(size)])  49.9 us
    ppermute x39, waiting for transfers between devices, hop(): return lax.ppermute(values, 'fsdp', [(i, i ^ bits) for i in range(size)])  43.4 us
    pallas_call x10, Pallas kernels, vmem_call(): pl.pallas_call(kernel, out_shape=shapes, compiler_params=pltpu.CompilerPa...  20.2 us
    pallas_call x1, Pallas kernels, attend(): pl.pallas_call(attend_kernel, grid=(pairs,), in_specs=[part(0), part(1),...  13.1 us
    pallas_call x1, Pallas kernels, attend_back(): pl.pallas_call(attend_back_kernel, grid=(pairs,), in_specs=[part(0), part...  11.5 us
    pallas_call x1, Pallas kernels, feed_tokens(): pl.pallas_call(feed_tokens_kernel, grid_spec=pltpu.PrefetchScalarGridSpec...  11.1 us
    pallas_call x1, Pallas kernels, feed_weights(): pl.pallas_call(feed_weights_kernel, grid_spec=pltpu.PrefetchScalarGridSpe...  10.8 us
    pallas_call x1, Pallas kernels, feed_first(): pl.pallas_call(feed_first_kernel, grid_spec=pltpu.PrefetchScalarGridSpec(...  9.59 us
  transfers between devices with their start and end apart: 45, of which 18 were waited for; matrix products, arithmetic and copies ran while one was open for 9% of the time, Pallas kernels for 40%

profile of v2, /device:TPU:0, one launch (start us, length us, event | category | flops | bytes accessed | tf_op | source)
XLA Modules:
  0.0 229.1 jit_solution(14121276610620504056)
XLA Ops:
  5.3 2.8 %collective-permute-start.1 = (bf16[48,1280]{1,0:T(8,128)(2,1)S(1)}, bf16[48,1280]{1,0:T(8,128)(2,1)S(1)}, u32[]{:S(2)}, u32[]{:S(2)}) collective-permute-start(bf16[48,1280]{1,0:T(8,128)(2,1)S(1)} %concatenate.29.refs_0_), channel_id=1, source_target_pairs={{0,8},{2,10},{4,12},{6,14},{8,0},{10,2},{12,4},{14,6},{16,24},{18,... | collective-permute-start | bytes 368648 | tf_op jit(solution)/shard_map/ppermute | solution.py:732
  8.1 2.6 %collective-permute-start.2 = (bf16[48,1280]{1,0:T(8,128)(2,1)S(1)}, bf16[48,1280]{1,0:T(8,128)(2,1)S(1)}, u32[]{:S(2)}, u32[]{:S(2)}) collective-permute-start(bf16[48,1280]{1,0:T(8,128)(2,1)S(1)} %concatenate.29.refs_0_), channel_id=1, source_target_pairs={{0,16},{2,18},{4,20},{6,22},{8,24},{10,26},{12,28},{14,30},{16,0},... | collective-permute-start | bytes 368648 | tf_op jit(solution)/shard_map/ppermute | solution.py:732
  26.2 3.2 %maximum_select_fusion.1.grad = bf16[1024,768]{1,0:T(8,128)(2,1)} fusion(bf16[512,768]{1,0:T(8,128)(2,1)} %collective-permute-done.11, bf16[512,768]{1,0:T(8,128)(2,1)S(1)} %copy-done.30, pred[]{:T(512)S(6)} %eq.4), kind=kLoop, calls=%fused_computation.1 | loop fusion | flops 7077888 | bytes 3145729 | tf_op jit(solution)/shard_map/jit(_where)/select_n | solution.py:835
  41.2 6.7 %collective-permute-done.9.refs_2_ = bf16[48,1920]{1,0:T(8,128)(2,1)} collective-permute-done((bf16[48,1920]{1,0:T(8,128)(2,1)}, bf16[48,1920]{1,0:T(8,128)(2,1)}, u32[]{:S(2)}, u32[]{:S(2)}) %collective-permute-start.9) | collective-permute-done | bytes 184352 | tf_op jit(solution)/shard_map/ppermute | solution.py:732
  50.8 3.4 %collective-permute-start.17 = (bf16[96,1536]{1,0:T(8,128)(2,1)}, bf16[96,1536]{1,0:T(8,128)(2,1)}, u32[]{:S(2)}, u32[]{:S(2)}) collective-permute-start(bf16[96,1536]{1,0:T(8,128)(2,1)} %beside.1.refs_0_), channel_id=1, source_target_pairs={{0,16},{2,18},{4,20},{6,22},{8,24},{10,26},{12,28},{14,30},{16,0},... | collective-permute-start | bytes 884744 | tf_op jit(solution)/shard_map/ppermute | solution.py:732
  56.5 6.3 %enter.1 = (bf16[768,1024]{1,0:T(8,128)(2,1)S(1)}, bf16[1024,1152]{1,0:T(8,128)(2,1)S(1)}, bf16[768,1152]{1,0:T(8,128)(2,1)S(1)}, f32[8,768]{1,0:T(8,128)S(1)}) custom-call(s32[64]{0:T(128)S(1)} %pad_add_fusion.table, f32[1024,768]{1,0:T(8,128)S(1)} %maximum_select_fusion.tokens, bf16[384,640]{1,0:T(8,128)(2,1)} %get-tuple-element.123.wa, ...), custom_call_target="tpu_custom_call" | custom-call | flops 9999999827968 | bytes 1000000000 | tf_op jit(solution)/shard_map/enter/pallas_call | solution.py:130
  64.9 2.5 %join.3 = (bf16[384,1024]{1,0:T(8,128)(2,1)}, bf16[384,896]{1,0:T(8,128)(2,1)}) custom-call(bf16[192,1024]{1,0:T(8,128)(2,1)} %get-tuple-element.133.one, bf16[192,1024]{1,0:T(8,128)(2,1)} %collective-permute-done.12.one_far, bf16[192,896]{1,0:T(8,128)(2,1)} %get-tuple-element.135.two, bf16[192,896]{1,0:T(8,128)(2,1)} %collective-permute-done.13.two_far), custom_call_target="tpu_custom_call" | custom-call | flops 9999999827968 | bytes 1000000000 | tf_op jit(solution)/shard_map/join/pallas_call | solution.py:752
  69.6 13.1 %attend.1 = (bf16[1024,384]{1,0:T(8,128)(2,1)S(1)}, f32[24,1024]{1,0:T(8,128)S(1)}) custom-call(bf16[1024,1152]{1,0:T(8,128)(2,1)S(1)} %get-tuple-element.139.queries.keys.values, bf16[1024,1152]{1,0:T(8,128)(2,1)S(1)} %get-tuple-element.139.queries.keys.values, bf16[1024,1152]{1,0:T(8,128)(2,1)S(1)} %get-tuple-element.139.queries.keys.values, ...), custom_call_target="tpu_custom_call" | custom-call | flops 9999999827968 | bytes 1000000000 | tf_op jit(solution)/shard_map/attend/pallas_call | solution.py:209
  85.3 3.6 %leave.1 = (bf16[1024,768]{1,0:T(8,128)(2,1)S(1)}, bf16[768,384]{1,0:T(8,128)(2,1)S(1)}) custom-call(s32[64]{0:T(128)S(1)} %pad_add_fusion.table, bf16[1024,384]{1,0:T(8,128)(2,1)S(1)} %get-tuple-element.148.att.out, bf16[384,896]{1,0:T(8,128)(2,1)} %get-tuple-element.138.near.up_b, bf16[384,896]{1,0:T(8,128)(2,1)} %collective-permute-done.20.far.up_b2), custom_call_target="tpu_custom_call" | custom-call | flops 9999999827968 | bytes 1000000000 | tf_op jit(solution)/shard_map/leave/pallas_call | solution.py:321
  95.3 9.6 %feed_first.1 = (f32[1024,768]{1,0:T(8,128)S(1)}, bf16[768,1024]{1,0:T(8,128)(2,1)S(1)}, bf16[1024,1536]{1,0:T(8,128)(2,1)S(1)}, bf16[1024,1536]{1,0:T(8,128)(2,1)S(1)}, bf16[768,1536]{1,0:T(8,128)(2,1)S(1)}) custom-call(s32[64]{0:T(128)S(1)} %copy-done.12, f32[1024,768]{1,0:T(8,128)S(1)} %copy-done.2, bf16[1024,768]{1,0:T(8,128)(2,1)S(1)} %get-tuple-element.149.part, ...), custom_call_target="tpu_custom_call" | custom-call | flops 9999999827968 | bytes 1000000000 | tf_op jit(solution)/shard_map/feed_first/pallas_call | solution.py:394
  104.9 2.6 %collective-permute-done.22.down_a2 = bf16[384,768]{1,0:T(8,128)(2,1)} collective-permute-done((bf16[384,768]{1,0:T(8,128)(2,1)}, bf16[384,768]{1,0:T(8,128)(2,1)}, u32[]{:S(2)}, u32[]{:S(2)}) %collective-permute-start.22) | collective-permute-done | bytes 589856 | tf_op jit(solution)/shard_map/ppermute | solution.py:732
  108.5 11.1 %feed_tokens.1 = (bf16[1024,768]{1,0:T(8,128)(2,1)S(1)}, bf16[1024,768]{1,0:T(8,128)(2,1)}, bf16[1024,1536]{1,0:T(8,128)(2,1)S(1)}) custom-call(s32[64]{0:T(128)S(1)} %copy-done.12, bf16[1024,768]{1,0:T(8,128)(2,1)S(1)} %copy-done, bf16[1024,1536]{1,0:T(8,128)(2,1)S(1)} %get-tuple-element.153.act, bf16[1024,1536]{1,0:T(8,128)(2,1)S(1)} %get-tuple-element.154.slope, ...), custom_call_target="tpu_custom_call" | custom-call | flops 9999999827968 | bytes 1000000000 | tf_op jit(solution)/shard_map/feed_tokens/pallas_call | solution.py:455
  119.6 10.8 %feed_weights.1 = (bf16[384,1536]{1,0:T(8,128)(2,1)S(1)}, bf16[384,1536]{1,0:T(8,128)(2,1)}, bf16[384,1536]{1,0:T(8,128)(2,1)S(1)}, bf16[384,1536]{1,0:T(8,128)(2,1)}) custom-call(s32[64]{0:T(128)S(1)} %copy-done.12, bf16[768,1024]{1,0:T(8,128)(2,1)S(1)} %get-tuple-element.152.normed_flip, bf16[768,1024]{1,0:T(8,128)(2,1)S(1)} %copy-done.4, ...), custom_call_target="tpu_custom_call" | custom-call | flops 9999999827968 | bytes 1000000000 | tf_op jit(solution)/shard_map/feed_weights/pallas_call | solution.py:493
  132.3 7.8 %middle_back.1 = (f32[1024,768]{1,0:T(8,128)S(1)}, bf16[1024,384]{1,0:T(8,128)(2,1)S(1)}, bf16[384,768]{1,0:T(8,128)(2,1)S(1)}, bf16[384,768]{1,0:T(8,128)(2,1)}, f32[8,768]{1,0:T(8,128)S(1)}) custom-call(s32[64]{0:T(128)S(1)} %copy-done.12, bf16[1024,768]{1,0:T(8,128)(2,1)} %get-tuple-element.165.pulled, bf16[1024,768]{1,0:T(8,128)(2,1)} %collective-permute-done.26.far, ...), custom_call_target="tpu_custom_call" | custom-call | flops 9999999827968 | bytes 1000000000 | tf_op jit(solution)/shard_map/middle_back/pallas_call | solution.py:557
  140.2 11.5 %attend_back.1.proj_grad = bf16[3,1024,384]{2,1,0:T(8,128)(2,1)S(1)} custom-call(bf16[1024,1152]{1,0:T(8,128)(2,1)S(1)} %copy-done.18, bf16[1024,1152]{1,0:T(8,128)(2,1)S(1)} %copy-done.18, bf16[1024,1152]{1,0:T(8,128)(2,1)S(1)} %copy-done.18, bf16[1024,384]{1,0:T(8,128)(2,1)S(1)} %copy-done.24, bf16[1024,384]{1,0:T(8,128)(2,1)S(1)} %get-tuple-element.168.grad, ...), custom_call_target="tpu_custom_call" | custom-call | flops 9999999827968 | bytes 1000000000 | tf_op jit(solution)/shard_map/attend_back/pallas_call | solution.py:278
  151.7 7.4 %collective-permute-done.24.one_far = bf16[384,1536]{1,0:T(8,128)(2,1)} collective-permute-done((bf16[384,1536]{1,0:T(8,128)(2,1)}, bf16[384,1536]{1,0:T(8,128)(2,1)}, u32[]{:S(2)}, u32[]{:S(2)}) %collective-permute-start.24) | collective-permute-done | bytes 1179680 | tf_op jit(solution)/shard_map/ppermute | solution.py:732
  159.5 3.0 %fold_half.2 = (bf16[192,1536]{1,0:T(8,128)(2,1)S(1)}, bf16[192,1536]{1,0:T(8,128)(2,1)}, bf16[192,1536]{1,0:T(8,128)(2,1)S(1)}, bf16[192,1536]{1,0:T(8,128)(2,1)}) custom-call(bf16[384,1536]{1,0:T(8,128)(2,1)S(1)} %get-tuple-element.170.one, bf16[384,1536]{1,0:T(8,128)(2,1)} %collective-permute-done.24.one_far, ...), custom_call_target="tpu_custom_call" | custom-call | flops 9999999827968 | bytes 1000000000 | tf_op jit(solution)/shard_map/fold_half/pallas_call | solution.py:752
  164.6 5.3 %weight_back.1 = (bf16[384,768]{1,0:T(8,128)(2,1)S(1)}, bf16[384,768]{1,0:T(8,128)(2,1)}, bf16[384,768]{1,0:T(8,128)(2,1)S(1)}, bf16[384,768]{1,0:T(8,128)(2,1)}) custom-call(s32[64]{0:T(128)S(1)} %copy-done.12, bf16[3,1024,384]{2,1,0:T(8,128)(2,1)S(1)} %attend_back.1.proj_grad, ...), custom_call_target="tpu_custom_call", output_to_operand_aliasing={{2}: (3, {}), {3}: (4, {})} | custom-call | flops 9999999827968 | bytes 1000000000 | tf_op jit(solution)/shard_map/weight_back/pallas_call | solution.py:629
  173.3 5.8 %collective-permute-done.27.one_far = bf16[192,1536]{1,0:T(8,128)(2,1)} collective-permute-done((bf16[192,1536]{1,0:T(8,128)(2,1)}, bf16[192,1536]{1,0:T(8,128)(2,1)}, u32[]{:S(2)}, u32[]{:S(2)}) %collective-permute-start.27) | collective-permute-done | bytes 589856 | tf_op jit(solution)/shard_map/ppermute | solution.py:732
  182.6 3.3 %collective-permute-start.30 = (bf16[48,3072]{1,0:T(8,128)(2,1)}, bf16[48,3072]{1,0:T(8,128)(2,1)}, u32[]{:S(2)}, u32[]{:S(2)}) collective-permute-start(bf16[48,3072]{1,0:T(8,128)(2,1)} %get-tuple-element.192), channel_id=1, source_target_pairs={{0,16},{2,18},{4,20},{6,22},{8,24},{10,26},{12,28},{14,30},{16,0},... | collective-permute-start | bytes 884744 | tf_op jit(solution)/shard_map/ppermute | solution.py:732
  187.0 4.2 %token_back.1.pulled = bf16[1024,768]{1,0:T(8,128)(2,1)} custom-call(bf16[3,1024,384]{2,1,0:T(8,128)(2,1)S(1)} %attend_back.1.proj_grad, bf16[768,1152]{1,0:T(8,128)(2,1)S(1)} %copy-done.20), custom_call_target="tpu_custom_call" | custom-call | flops 9999999827968 | bytes 1000000000 | tf_op jit(solution)/shard_map/token_back/pallas_call | solution.py:661
  195.8 5.2 %leave_layer.1 = (f32[512,768]{1,0:T(8,128)}, f32[8,768]{1,0:T(8,128)S(1)}) custom-call(s32[1]{0:T(128)} %bitcast.9.core, bf16[1024,768]{1,0:T(8,128)(2,1)} %token_back.1.pulled, bf16[1024,768]{1,0:T(8,128)(2,1)} %collective-permute-done.32.far, f32[1024,768]{1,0:T(8,128)S(1)} %copy-done.3, f32[1024,768]{1,0:T(8,128)S(1)} %get-tuple-element.206.middle_grad, ...), custom_call_target="tpu_custom_call" | custom-call | flops 9999999827968 | bytes 1000000000 | tf_op jit(solution)/shard_map/leave_layer/pallas_call | solution.py:705
  206.6 3.7 %collective-permute-start.38 = (bf16[48,1536]{1,0:T(8,128)(2,1)S(1)}, bf16[48,1536]{1,0:T(8,128)(2,1)S(1)}, u32[]{:S(2)}, u32[]{:S(2)}) collective-permute-start(bf16[48,1536]{1,0:T(8,128)(2,1)S(1)} %get-tuple-element.214), channel_id=1, source_target_pairs={{0,8},{2,10},{4,12},{6,14},{8,0},{10,2},{12,4},{14,6},{16,24},{18,... | collective-permute-start | bytes 442376 | tf_op jit(solution)/shard_map/ppermute | solution.py:732
  222.5 3.1 %collective-permute-done.44 = f32[4,768]{1,0:T(4,128)S(1)} collective-permute-done((f32[4,768]{1,0:T(4,128)S(1)}, f32[4,768]{1,0:T(4,128)S(1)}, u32[]{:S(2)}, u32[]{:S(2)}) %collective-permute-start.44) | collective-permute-done | bytes 12320 | tf_op jit(solution)/shard_map/ppermute | solution.py:732
  (195 shorter events, 89.5 us)
Async XLA Ops:
  0.7 13.5 %collective-permute-start = (f32[512,768]{1,0:T(8,128)}, f32[512,768]{1,0:T(8,128)}, u32[]{:S(2)}, u32[]{:S(2)}) collective-permute-start(f32[512,768]{1,0:T(8,128)} %param.11), channel_id=1, source_target_pairs={{0,1},{1,0},{2,3},{3,2},{4,5},{5,4},{6,7},{7,6},{8,9},{9,8},{10,11... | collective-permute-start | bytes 4718600 | tf_op jit(solution)/shard_map/ppermute | solution.py:728
  10.7 15.4 %collective-permute-start.11 = (bf16[512,768]{1,0:T(8,128)(2,1)}, bf16[512,768]{1,0:T(8,128)(2,1)}, u32[]{:S(2)}, u32[]{:S(2)}) collective-permute-start(bf16[512,768]{1,0:T(8,128)(2,1)} %param.21), channel_id=1, source_target_pairs={{0,1},{1,0},{2,3},{3,2},{4,5},{5,4},{6,7},{7,6},{8,9},{9,8},{10,11... | collective-permute-start | bytes 2359304 | tf_op jit(solution)/shard_map/ppermute | solution.py:728
  33.2 14.6 %collective-permute-start.9 = (bf16[48,1920]{1,0:T(8,128)(2,1)}, bf16[48,1920]{1,0:T(8,128)(2,1)}, u32[]{:S(2)}, u32[]{:S(2)}) collective-permute-start(bf16[48,1920]{1,0:T(8,128)(2,1)} %pad_maximum_fusion.1.refs_0_), channel_id=1, source_target_pairs={{0,16},{2,18},{4,20},{6,22},{8,24},{10,26},{12,28},{14,30},{16,0},... | collective-permute-start | bytes 552968 | tf_op jit(solution)/shard_map/ppermute | solution.py:732
  36.1 18.7 %collective-permute-start.6 = (bf16[384,640]{1,0:T(8,128)(2,1)}, bf16[384,640]{1,0:T(8,128)(2,1)}, u32[]{:S(2)}, u32[]{:S(2)}) collective-permute-start(bf16[384,640]{1,0:T(8,128)(2,1)} %get-tuple-element.123.wa), channel_id=1, source_target_pairs={{0,2},{2,0},{4,6},{6,4},{8,10},{10,8},{12,14},{14,12},{16,18},{18,... | collective-permute-start | bytes 1474568 | tf_op jit(solution)/shard_map/ppermute | solution.py:732
  36.6 19.4 %collective-permute-start.7 = (bf16[384,640]{1,0:T(8,128)(2,1)}, bf16[384,640]{1,0:T(8,128)(2,1)}, u32[]{:S(2)}, u32[]{:S(2)}) collective-permute-start(bf16[384,640]{1,0:T(8,128)(2,1)} %get-tuple-element.124.wb), channel_id=1, source_target_pairs={{0,4},{2,6},{4,0},{6,2},{8,12},{10,14},{12,8},{14,10},{16,20},{18,... | collective-permute-start | bytes 1474568 | tf_op jit(solution)/shard_map/ppermute | solution.py:732
  50.4 32.3 %collective-permute-start.16 = (bf16[96,1536]{1,0:T(8,128)(2,1)}, bf16[96,1536]{1,0:T(8,128)(2,1)}, u32[]{:S(2)}, u32[]{:S(2)}) collective-permute-start(bf16[96,1536]{1,0:T(8,128)(2,1)} %beside.1.refs_0_), channel_id=1, source_target_pairs={{0,8},{2,10},{4,12},{6,14},{8,0},{10,2},{12,4},{14,6},{16,24},{18,... | collective-permute-start | bytes 884744 | tf_op jit(solution)/shard_map/ppermute | solution.py:732
  50.8 31.9 %collective-permute-start.17 = (bf16[96,1536]{1,0:T(8,128)(2,1)}, bf16[96,1536]{1,0:T(8,128)(2,1)}, u32[]{:S(2)}, u32[]{:S(2)}) collective-permute-start(bf16[96,1536]{1,0:T(8,128)(2,1)} %beside.1.refs_0_), channel_id=1, source_target_pairs={{0,16},{2,18},{4,20},{6,22},{8,24},{10,26},{12,28},{14,30},{16,0},... | collective-permute-start | bytes 884744 | tf_op jit(solution)/shard_map/ppermute | solution.py:732
  54.2 28.6 %collective-permute-start.18 = (bf16[96,1536]{1,0:T(8,128)(2,1)}, bf16[96,1536]{1,0:T(8,128)(2,1)}, u32[]{:S(2)}, u32[]{:S(2)}) collective-permute-start(bf16[96,1536]{1,0:T(8,128)(2,1)} %beside.1.refs_0_), channel_id=1, source_target_pairs={{0,24},{2,26},{4,28},{6,30},{8,16},{10,18},{12,20},{14,22},{16,8},... | collective-permute-start | bytes 884744 | tf_op jit(solution)/shard_map/ppermute | solution.py:732
  67.4 17.8 %collective-permute-start.19 = (bf16[384,1024]{1,0:T(8,128)(2,1)}, bf16[384,1024]{1,0:T(8,128)(2,1)}, u32[]{:S(2)}, u32[]{:S(2)}) collective-permute-start(bf16[384,1024]{1,0:T(8,128)(2,1)} %get-tuple-element.137.up_a), channel_id=1, source_target_pairs={{0,2},{2,0},{4,6},{6,4},{8,10},{10,8},{12,14},{14,12},{16,18},{18,... | collective-permute-start | bytes 2359304 | tf_op jit(solution)/shard_map/ppermute | solution.py:732
  68.9 15.4 %collective-permute-start.20 = (bf16[384,896]{1,0:T(8,128)(2,1)}, bf16[384,896]{1,0:T(8,128)(2,1)}, u32[]{:S(2)}, u32[]{:S(2)}) collective-permute-start(bf16[384,896]{1,0:T(8,128)(2,1)} %get-tuple-element.138.near.up_b), channel_id=1, source_target_pairs={{0,4},{2,6},{4,0},{6,2},{8,12},{10,14},{12,8},{14,10},{16,20},{18,... | collective-permute-start | bytes 2064392 | tf_op jit(solution)/shard_map/ppermute | solution.py:732
  91.4 16.1 %collective-permute-start.22 = (bf16[384,768]{1,0:T(8,128)(2,1)}, bf16[384,768]{1,0:T(8,128)(2,1)}, u32[]{:S(2)}, u32[]{:S(2)}) collective-permute-start(bf16[384,768]{1,0:T(8,128)(2,1)} %copy-done.13), channel_id=1, source_target_pairs={{0,4},{2,6},{4,0},{6,2},{8,12},{10,14},{12,8},{14,10},{16,20},{18,... | collective-permute-start | bytes 1769480 | tf_op jit(solution)/shard_map/ppermute | solution.py:732
  92.7 15.8 %collective-permute-start.23 = (bf16[384,768]{1,0:T(8,128)(2,1)}, bf16[384,768]{1,0:T(8,128)(2,1)}, u32[]{:S(2)}, u32[]{:S(2)}) collective-permute-start(bf16[384,768]{1,0:T(8,128)(2,1)} %copy-done.15), channel_id=1, source_target_pairs={{0,2},{2,0},{4,6},{6,4},{8,10},{10,8},{12,14},{14,12},{16,18},{18,... | collective-permute-start | bytes 1769480 | tf_op jit(solution)/shard_map/ppermute | solution.py:732
  130.4 28.7 %collective-permute-start.24 = (bf16[384,1536]{1,0:T(8,128)(2,1)}, bf16[384,1536]{1,0:T(8,128)(2,1)}, u32[]{:S(2)}, u32[]{:S(2)}) collective-permute-start(bf16[384,1536]{1,0:T(8,128)(2,1)} %get-tuple-element.162), channel_id=1, source_target_pairs={{0,2},{2,0},{4,6},{6,4},{8,10},{10,8},{12,14},{14,12},{16,18},{18,... | collective-permute-start | bytes 3538952 | tf_op jit(solution)/shard_map/ppermute | solution.py:732
  131.1 28.4 %collective-permute-start.25 = (bf16[384,1536]{1,0:T(8,128)(2,1)}, bf16[384,1536]{1,0:T(8,128)(2,1)}, u32[]{:S(2)}, u32[]{:S(2)}) collective-permute-start(bf16[384,1536]{1,0:T(8,128)(2,1)} %get-tuple-element.164), channel_id=1, source_target_pairs={{0,4},{2,6},{4,0},{6,2},{8,12},{10,14},{12,8},{14,10},{16,20},{18,... | collective-permute-start | bytes 3538952 | tf_op jit(solution)/shard_map/ppermute | solution.py:732
  162.5 16.6 %collective-permute-start.27 = (bf16[192,1536]{1,0:T(8,128)(2,1)}, bf16[192,1536]{1,0:T(8,128)(2,1)}, u32[]{:S(2)}, u32[]{:S(2)}) collective-permute-start(bf16[192,1536]{1,0:T(8,128)(2,1)} %get-tuple-element.175), channel_id=1, source_target_pairs={{0,4},{2,6},{4,0},{6,2},{8,12},{10,14},{12,8},{14,10},{16,20},{18,... | collective-permute-start | bytes 1769480 | tf_op jit(solution)/shard_map/ppermute | solution.py:732
  163.7 16.6 %collective-permute-start.28 = (bf16[192,1536]{1,0:T(8,128)(2,1)}, bf16[192,1536]{1,0:T(8,128)(2,1)}, u32[]{:S(2)}, u32[]{:S(2)}) collective-permute-start(bf16[192,1536]{1,0:T(8,128)(2,1)} %get-tuple-element.177), channel_id=1, source_target_pairs={{0,2},{2,0},{4,6},{6,4},{8,10},{10,8},{12,14},{14,12},{16,18},{18,... | collective-permute-start | bytes 1769480 | tf_op jit(solution)/shard_map/ppermute | solution.py:732
  170.7 20.5 %collective-permute-start.33 = (bf16[384,768]{1,0:T(8,128)(2,1)}, bf16[384,768]{1,0:T(8,128)(2,1)}, u32[]{:S(2)}, u32[]{:S(2)}) collective-permute-start(bf16[384,768]{1,0:T(8,128)(2,1)} %get-tuple-element.183), channel_id=1, source_target_pairs={{0,2},{2,0},{4,6},{6,4},{8,10},{10,8},{12,14},{14,12},{16,18},{18,... | collective-permute-start | bytes 1769480 | tf_op jit(solution)/shard_map/ppermute | solution.py:732
  171.8 19.4 %collective-permute-start.34 = (bf16[384,768]{1,0:T(8,128)(2,1)}, bf16[384,768]{1,0:T(8,128)(2,1)}, u32[]{:S(2)}, u32[]{:S(2)}) collective-permute-start(bf16[384,768]{1,0:T(8,128)(2,1)} %get-tuple-element.185), channel_id=1, source_target_pairs={{0,4},{2,6},{4,0},{6,2},{8,12},{10,14},{12,8},{14,10},{16,20},{18,... | collective-permute-start | bytes 1769480 | tf_op jit(solution)/shard_map/ppermute | solution.py:732
  182.6 22.9 %collective-permute-start.29 = (bf16[48,3072]{1,0:T(8,128)(2,1)}, bf16[48,3072]{1,0:T(8,128)(2,1)}, u32[]{:S(2)}, u32[]{:S(2)}) collective-permute-start(bf16[48,3072]{1,0:T(8,128)(2,1)} %get-tuple-element.191), channel_id=1, source_target_pairs={{0,8},{2,10},{4,12},{6,14},{8,0},{10,2},{12,4},{14,6},{16,24},{18,... | collective-permute-start | bytes 884744 | tf_op jit(solution)/shard_map/ppermute | solution.py:732
  182.6 22.9 %collective-permute-start.30 = (bf16[48,3072]{1,0:T(8,128)(2,1)}, bf16[48,3072]{1,0:T(8,128)(2,1)}, u32[]{:S(2)}, u32[]{:S(2)}) collective-permute-start(bf16[48,3072]{1,0:T(8,128)(2,1)} %get-tuple-element.192), channel_id=1, source_target_pairs={{0,16},{2,18},{4,20},{6,22},{8,24},{10,26},{12,28},{14,30},{16,0},... | collective-permute-start | bytes 884744 | tf_op jit(solution)/shard_map/ppermute | solution.py:732
  185.9 19.6 %collective-permute-start.31 = (bf16[48,3072]{1,0:T(8,128)(2,1)}, bf16[48,3072]{1,0:T(8,128)(2,1)}, u32[]{:S(2)}, u32[]{:S(2)}) collective-permute-start(bf16[48,3072]{1,0:T(8,128)(2,1)} %get-tuple-element.193), channel_id=1, source_target_pairs={{0,24},{2,26},{4,28},{6,30},{8,16},{10,18},{12,20},{14,22},{16,8},... | collective-permute-start | bytes 884744 | tf_op jit(solution)/shard_map/ppermute | solution.py:732
  206.6 19.5 %collective-permute-start.38 = (bf16[48,1536]{1,0:T(8,128)(2,1)S(1)}, bf16[48,1536]{1,0:T(8,128)(2,1)S(1)}, u32[]{:S(2)}, u32[]{:S(2)}) collective-permute-start(bf16[48,1536]{1,0:T(8,128)(2,1)S(1)} %get-tuple-element.214), channel_id=1, source_target_pairs={{0,8},{2,10},{4,12},{6,14},{8,0},{10,2},{12,4},{14,6},{16,24},{18,... | collective-permute-start | bytes 442376 | tf_op jit(solution)/shard_map/ppermute | solution.py:732
  210.3 15.8 %collective-permute-start.39 = (bf16[48,1536]{1,0:T(8,128)(2,1)S(1)}, bf16[48,1536]{1,0:T(8,128)(2,1)S(1)}, u32[]{:S(2)}, u32[]{:S(2)}) collective-permute-start(bf16[48,1536]{1,0:T(8,128)(2,1)S(1)} %get-tuple-element.215), channel_id=1, source_target_pairs={{0,16},{2,18},{4,20},{6,22},{8,24},{10,26},{12,28},{14,30},{16,0},... | collective-permute-start | bytes 442376 | tf_op jit(solution)/shard_map/ppermute | solution.py:732
  211.3 14.9 %collective-permute-start.40 = (bf16[48,1536]{1,0:T(8,128)(2,1)S(1)}, bf16[48,1536]{1,0:T(8,128)(2,1)S(1)}, u32[]{:S(2)}, u32[]{:S(2)}) collective-permute-start(bf16[48,1536]{1,0:T(8,128)(2,1)S(1)} %get-tuple-element.216), channel_id=1, source_target_pairs={{0,24},{2,26},{4,28},{6,30},{8,16},{10,18},{12,20},{14,22},{16,8},... | collective-permute-start | bytes 442376 | tf_op jit(solution)/shard_map/ppermute | solution.py:732
  (55 other events, 549.1 us)

commit v3 on v2

--- a/solution.py
+++ b/solution.py
@@ -42,9 +42,9 @@
     )
 
 
-def fixed(shape, index=None):
-    place = index or (0,) * len(shape)
-    return pl.BlockSpec(shape, lambda i, *_: place, pipeline_mode=pl.Buffered(1))
+def fixed(shape):
+    del shape
+    return pl.BlockSpec(memory_space=pltpu.VMEM)
 
 
 def kept(shape, index=None):
@@ -82,28 +82,38 @@
     )
 
 
-def take(table, entry, rows, near, far, lanes=slice(None)):
+def take(table, entry, rows, pieces, lanes=slice(None)):
+    each = BLOCKS // len(pieces)
     place = table[entry]
-    at = pl.ds(pl.multiple_of((place % (BLOCKS // 2)) * rows, 16), rows)
-    return jnp.where(place < BLOCKS // 2, near[at, lanes], far[at, lanes])
-
-
-def put(table, entry, rows, keep, send, values):
-    place = table[entry]
-    at = pl.ds(pl.multiple_of((place % (BLOCKS // 2)) * rows, 16), rows)
-
-    @pl.when(place < BLOCKS // 2)
-    def _():
-        keep[at, :] = values
-
-    @pl.when(place >= BLOCKS // 2)
-    def _():
-        send[at, :] = values
-
-
-def enter_kernel(table, tokens, wa, wa2, wb, wb2, flip, proj, whole, vectors, loose, normed):
+    at = pl.ds(pl.multiple_of((place % each) * rows, 16), rows)
+    block = pieces[0][at, lanes]
+    for k in range(1, len(pieces)):
+        block = jnp.where(place >= k * each, pieces[k][at, lanes], block)
+    return block
+
+
+def put(table, entry, bit, rows, keep, send, whole):
+    for j in range(BLOCKS):
+        if j & bit:
+            continue
+        blocks = [whole[k * rows : (k + 1) * rows] for k in (j, j | bit)]
+        place = table[entry + j]
+        stays = place < BLOCKS // 2
+        at = pl.ds(pl.multiple_of((place % (BLOCKS // 2)) * rows, 16), rows)
+        keep[at, :] = jnp.where(stays, blocks[0], blocks[1])
+        send[at, :] = jnp.where(stays, blocks[1], blocks[0])
+
+
+def side_bits(size):
+    return (1, 2) if size == BLOCKS else (BLOCKS // 2, BLOCKS // 2)
+
+
+def enter_kernel(
+    share, table, tokens, wa, wb, wc, wd, we, wf, wg, wh, flip, proj, whole, vectors, loose, normed
+):
     step = pl.program_id(0)
-    rows = wa.shape[0] // (BLOCKS // 2)
+    lefts, rights = (wa, wb, wc, wd), (we, wf, wg, wh)
+    rows = wa.shape[0] // (BLOCKS // 4)
     cut = wa.shape[1]
     rest = whole.shape[1] - cut
 
@@ -111,11 +121,17 @@
     def _():
         for j in range(BLOCKS):
             to = slice(j * rows, (j + 1) * rows)
-            whole[to, :cut] = take(table, LEFT + j, rows, wa, wa2)
-            late = take(table, RIGHT + j, rows, wb, wb2)
+            whole[to, :cut] = take(table, LEFT + j, rows, lefts)
+            late = take(table, RIGHT + j, rows, rights)
             whole[to, cut:] = late[:, :rest]
             loose[to, :] = late[:, rest:].astype(WIDE)
-        vectors[...] = loose[...].T[:8]
+        total = jnp.zeros(vectors.shape, WIDE)
+        beyond = jnp.zeros((4, vectors.shape[1] - LANES), WIDE)
+        for start in range(0, vectors.shape[1], share):
+            piece = jnp.concatenate([loose[start : start + 4, :], beyond], axis=1)
+            piece = jnp.concatenate([piece, jnp.zeros_like(piece)], axis=0)
+            total = total + pltpu.roll(piece, start, 1)
+        vectors[...] = total
 
     for at in tiles(tokens.shape[0]):
         hat, _ = hat_of(tokens[at, :])
@@ -124,11 +140,11 @@
     flip[...] = normed[...].T
 
 
-def enter(table, tokens, *pieces):
+def enter(share, table, tokens, *pieces):
     length, width = tokens.shape
-    total = pieces[0].shape[1] + pieces[2].shape[1] - LANES
+    total = pieces[0].shape[1] + pieces[4].shape[1] - LANES
     return pl.pallas_call(
-        enter_kernel,
+        functools.partial(enter_kernel, share),
         grid_spec=pltpu.PrefetchScalarGridSpec(
             num_scalar_prefetch=1,
             grid=(length // ROWS,),
@@ -174,7 +190,9 @@
     return jnp.concatenate([empty, flipped[HD:]], axis=0)
 
 
-def attend_kernel(queries, keys, values, seg_col, seg_row, out, lse, bias):
+def attend_kernel(queries, keys, values, seg_col, seg_row, *refs):
+    out, lse, bias = refs[-3:]
+
     @pl.when(pl.program_id(0) == 0)
     def _():
         build_bias(bias, seg_col, seg_row)
@@ -199,35 +217,37 @@
         out[lanes, :] = jnp.concatenate(pieces, axis=0).T.astype(LOW)
 
 
-def attend(proj, seg_col, seg_row):
+def attend(proj, seg_col, seg_row, begin, end, held=()):
     length = proj.shape[0]
     pairs = proj.shape[1] // (3 * LANES)
 
     def part(k):
-        return pl.BlockSpec((length, LANES), lambda i: (0, k * pairs + i))
+        return pl.BlockSpec((length, LANES), lambda i: (0, k * pairs + begin + i))
 
     return pl.pallas_call(
         attend_kernel,
-        grid=(pairs,),
-        in_specs=[part(0), part(1), part(2), fixed(seg_col.shape), fixed(seg_row.shape)],
+        grid=(end - begin,),
+        in_specs=[part(0), part(1), part(2), fixed(seg_col.shape), fixed(seg_row.shape)]
+        + [pl.BlockSpec(memory_space=pl.ANY) for _ in held],
         out_specs=[
-            pl.BlockSpec((length, LANES), lambda i: (0, i)),
-            pl.BlockSpec((8, length), lambda i: (i, 0)),
+            pl.BlockSpec((length, LANES), lambda i: (0, begin + i)),
+            pl.BlockSpec((8, length), lambda i: (begin + i, 0)),
         ],
         out_shape=[
             jax.ShapeDtypeStruct((length, pairs * LANES), LOW),
             jax.ShapeDtypeStruct((8 * pairs, length), WIDE),
         ],
+        input_output_aliases={5 + k: k for k in range(len(held))},
         scratch_shapes=[pltpu.VMEM((length, length), WIDE)],
         compiler_params=params(),
         cost_estimate=LONG,
         name="attend",
-    )(proj, proj, proj, seg_col, seg_row)
-
-
-def attend_back_kernel(
-    queries, keys, values, out, grad, lse, seg_col, seg_row, result, bias, soft, pull
-):
+    )(proj, proj, proj, seg_col, seg_row, *held)
+
+
+def attend_back_kernel(queries, keys, values, out, grad, lse, seg_col, seg_row, *refs):
+    result, bias, soft, pull = refs[-4:]
+
     @pl.when(pl.program_id(0) == 0)
     def _():
         build_bias(bias, seg_col, seg_row)
@@ -268,28 +288,30 @@
         result[0, at] = (jnp.concatenate(pieces, axis=0) * scale).T.astype(LOW)
 
 
-def attend_back(proj, out, grad, lse, seg_col, seg_row):
+def attend_back(proj, out, grad, lse, seg_col, seg_row, begin, end, held=()):
     length = proj.shape[0]
     pairs = proj.shape[1] // (3 * LANES)
 
     def part(k):
-        return pl.BlockSpec((length, LANES), lambda i: (0, k * pairs + i))
+        return pl.BlockSpec((length, LANES), lambda i: (0, k * pairs + begin + i))
 
     return pl.pallas_call(
         attend_back_kernel,
-        grid=(pairs,),
+        grid=(end - begin,),
         in_specs=[
             part(0),
             part(1),
             part(2),
             part(0),
             part(0),
-            pl.BlockSpec((8, length), lambda i: (i, 0)),
+            pl.BlockSpec((8, length), lambda i: (begin + i, 0)),
             fixed(seg_col.shape),
             fixed(seg_row.shape),
-        ],
-        out_specs=pl.BlockSpec((3, length, LANES), lambda i: (0, 0, i)),
+        ]
+        + [pl.BlockSpec(memory_space=pl.ANY) for _ in held],
+        out_specs=pl.BlockSpec((3, length, LANES), lambda i: (0, 0, begin + i)),
         out_shape=jax.ShapeDtypeStruct((3, length, pairs * LANES), LOW),
+        input_output_aliases={8 + k: k for k in range(len(held))},
         scratch_shapes=[
             pltpu.VMEM((length, length), WIDE),
             pltpu.VMEM((2, length, length), LOW),
@@ -298,32 +320,32 @@
         compiler_params=params(),
         cost_estimate=LONG,
         name="attend_back",
-    )(proj, proj, proj, out, grad, lse, seg_col, seg_row)
-
-
-def leave_kernel(table, att, near, far, part, whole):
-    rows = near.shape[0] // (BLOCKS // 2)
-    lanes = slice(near.shape[1] - whole.shape[1], None)
+    )(proj, proj, proj, out, grad, lse, seg_col, seg_row, *held)
+
+
+def leave_kernel(table, att, wa, wb, wc, wd, part, whole):
+    rows = wa.shape[0] // (BLOCKS // 4)
+    lanes = slice(wa.shape[1] - whole.shape[1], None)
 
     @pl.when(pl.program_id(0) == 0)
     def _():
         for j in range(BLOCKS):
             whole[j * rows : (j + 1) * rows, :] = take(
-                table, BLOCKS + j, rows, near, far, lanes
+                table, RIGHT + j, rows, (wa, wb, wc, wd), lanes
             )
 
     part[...] = nt(att[...], whole[...]).astype(LOW)
 
 
-def leave(table, att, near, far):
+def leave(table, att, *pieces):
     length, inner = att.shape
-    width = near.shape[0] * 2
+    width = pieces[0].shape[0] * 4
     return pl.pallas_call(
         leave_kernel,
         grid_spec=pltpu.PrefetchScalarGridSpec(
             num_scalar_prefetch=1,
             grid=(length // ROWS,),
-            in_specs=[by_row(inner), fixed(near.shape), fixed(far.shape)],
+            in_specs=[by_row(inner)] + [fixed(piece.shape) for piece in pieces],
             out_specs=[by_row(width), kept((width, inner))],
         ),
         out_shape=[
@@ -333,20 +355,20 @@
         compiler_params=params(),
         cost_estimate=LONG,
         name="leave",
-    )(table, att, near, far)
+    )(table, att, *pieces)
 
 
 SIDE = 256
 
 
-def unpack(table, whole, left, right, near_a, far_a, near_b, far_b):
-    rows = near_a.shape[0] // (BLOCKS // 2)
-    cut = min(near_a.shape[1], whole.shape[1])
+def unpack(table, whole, left, right, lefts, rights):
+    rows = whole.shape[0] // BLOCKS
+    cut = min(lefts[0].shape[1], whole.shape[1])
     for j in range(BLOCKS):
         to = slice(j * rows, (j + 1) * rows)
-        whole[to, :cut] = take(table, left + j, rows, near_a, far_a)
+        whole[to, :cut] = take(table, left + j, rows, lefts)
         lanes = slice(0, whole.shape[1] - cut)
-        whole[to, cut:] = take(table, right + j, rows, near_b, far_b, lanes)
+        whole[to, cut:] = take(table, right + j, rows, rights, lanes)
 
 
 def feed_first_kernel(
@@ -355,10 +377,14 @@
     part,
     far,
     vectors,
-    up_a,
-    up_a2,
-    up_b,
-    up_b2,
+    wa,
+    wb,
+    wc,
+    wd,
+    we,
+    wf,
+    wg,
+    wh,
     middle,
     flip,
     act,
@@ -368,7 +394,7 @@
 ):
     @pl.when(pl.program_id(0) == 0)
     def _():
-        unpack(table, whole, LEFT, RIGHT, up_a, up_a2, up_b, up_b2)
+        unpack(table, whole, LEFT, RIGHT, (wa, wb, wc, wd), (we, wf, wg, wh))
 
     for at in tiles(tokens.shape[0]):
         values = tokens[at, :] + (part[at, :].astype(WIDE) + far[at, :].astype(WIDE))
@@ -437,7 +463,9 @@
 ):
     @pl.when(pl.program_id(0) == 0)
     def _():
-        unpack(table, whole, DOWN_LEFT, DOWN_RIGHT, down_a, down_a2, down_b, down_b2)
+        unpack(
+            table, whole, DOWN_LEFT, DOWN_RIGHT, (down_a, down_a2), (down_b, down_b2)
+        )
 
     for start in range(0, whole.shape[1], SIDE):
         lanes = slice(start, start + SIDE)
@@ -473,39 +501,45 @@
     )(table, grad, act, slope, up, *pieces)
 
 
-def feed_weights_kernel(
-    table, normed_flip, grad_flip, act, pre, up_keep, up_send, down_keep, down_send
-):
-    rows = normed_flip.shape[0] // BLOCKS
-    lifted = nn(normed_flip[...], pre[...]).astype(LOW)
-    lowered = nn(grad_flip[...], act[...]).astype(LOW)
-    for j in range(BLOCKS):
-        block = slice(j * rows, (j + 1) * rows)
-        put(table, LEFT + j, rows, up_keep, up_send, lifted[block])
-        put(table, RIGHT + j, rows, down_keep, down_send, lowered[block])
-
-
-def feed_weights(table, normed_flip, grad_flip, act, pre):
-    width, length = normed_flip.shape
-    hidden = act.shape[1]
-    column = pl.BlockSpec((length, SIDE), lambda i, *_: (0, i))
-    half = pl.BlockSpec((width // 2, SIDE), lambda i, *_: (0, i))
+def feed_weight_kernel(bits, table, flip, side, left_keep, left_send, right_keep, right_send):
+    step = pl.program_id(0)
+    rows = flip.shape[0] // BLOCKS
+    middle = pl.num_programs(0) // 2
+
+    @pl.when(step < middle)
+    def _():
+        whole = nn(flip[...], side[...]).astype(LOW)
+        put(table, LEFT, bits[0], rows, left_keep, left_send, whole)
+
+    @pl.when(step >= middle)
+    def _():
+        whole = nn(flip[...], side[...]).astype(LOW)
+        put(table, RIGHT, bits[1], rows, right_keep, right_send, whole)
+
+
+def feed_weight(size, table, flip, side):
+    width, length = flip.shape
+    hidden = side.shape[1]
+    middle = hidden // SIDE // 2
+    left = pl.BlockSpec((width // 2, SIDE), lambda i, *_: (0, jnp.minimum(i, middle - 1)))
+    right = pl.BlockSpec((width // 2, SIDE), lambda i, *_: (0, jnp.maximum(i - middle, 0)))
     return pl.pallas_call(
-        feed_weights_kernel,
+        functools.partial(feed_weight_kernel, side_bits(size)),
         grid_spec=pltpu.PrefetchScalarGridSpec(
             num_scalar_prefetch=1,
             grid=(hidden // SIDE,),
-            in_specs=[fixed((width, length)), fixed((width, length)), column, column],
-            out_specs=[half] * 4,
+            in_specs=[fixed((width, length)), pl.BlockSpec((length, SIDE), lambda i, *_: (0, i))],
+            out_specs=[left, left, right, right],
         ),
-        out_shape=[jax.ShapeDtypeStruct((width // 2, hidden), LOW)] * 4,
+        out_shape=[jax.ShapeDtypeStruct((width // 2, hidden // 2), LOW)] * 4,
         compiler_params=params(),
         cost_estimate=LONG,
-        name="feed_weights",
-    )(table, normed_flip, grad_flip, act, pre)
+        name="feed_weight",
+    )(table, flip, side)
 
 
 def middle_back_kernel(
+    bits,
     table,
     pulled,
     far,
@@ -531,31 +565,32 @@
         out_sum[...] = jnp.zeros_like(out_sum)
         gathered[...] = jnp.zeros_like(gathered)
 
+    gains, shifts = gathered[:8, :], gathered[8:, :]
     for at in tiles(middle.shape[0]):
         pull = pulled[at, :].astype(WIDE) + far[at, :].astype(WIDE)
         hat, rate = hat_of(middle[at, :])
         whole = grad[at, :].astype(WIDE) + norm_back(pull, hat, rate, vectors[2:3, :])
         middle_grad[at, :] = whole
         low[at, :] = whole.astype(LOW)
-        gathered[:8, :] += fold_rows(pull * hat)
-        gathered[8:, :] += fold_rows(pull)
+        gains += fold_rows(pull * hat)
+        shifts += fold_rows(pull)
+    gathered[:8, :] = gains
+    gathered[8:, :] = shifts
     att_grad[...] = nn(low[...], out_whole[...]).astype(LOW)
     out_sum[...] += tn(low[...], att[...])
 
     @pl.when(step == pl.num_programs(0) - 1)
     def _():
-        for j in range(BLOCKS):
-            block = out_sum[j * rows : (j + 1) * rows, :].astype(LOW)
-            put(table, RIGHT + j, rows, out_keep, out_send, block)
+        put(table, RIGHT, bits[1], rows, out_keep, out_send, out_sum[...].astype(LOW))
         sums[0:1, :] = jnp.sum(gathered[:8, :], axis=0, keepdims=True)
         sums[1:2, :] = jnp.sum(gathered[8:, :], axis=0, keepdims=True)
 
 
-def middle_back(table, pulled, far, middle, grad, vectors, out_whole, att):
+def middle_back(size, table, pulled, far, middle, grad, vectors, out_whole, att):
     length, width = middle.shape
     inner = att.shape[1]
     return pl.pallas_call(
-        middle_back_kernel,
+        functools.partial(middle_back_kernel, side_bits(size)),
         grid_spec=pltpu.PrefetchScalarGridSpec(
             num_scalar_prefetch=1,
             grid=(length // ROWS,),
@@ -595,6 +630,7 @@
 
 
 def weight_back_kernel(
+    bits,
     table,
     proj_grad,
     normed_flip,
@@ -607,27 +643,25 @@
 ):
     step = pl.program_id(0)
     rows = normed_flip.shape[0] // BLOCKS
-    weight = nn(normed_flip[...], proj_grad[0]).astype(LOW)
 
     @pl.when(step < 2)
     def _():
-        for j in range(BLOCKS):
-            put(table, LEFT + j, rows, left_keep, left_send, weight[j * rows : (j + 1) * rows])
+        weight = nn(normed_flip[...], proj_grad[0]).astype(LOW)
+        put(table, LEFT, bits[0], rows, left_keep, left_send, weight)
 
     @pl.when(step == 2)
     def _():
-        for j in range(BLOCKS):
-            block = weight[j * rows : (j + 1) * rows]
-            put(table, RIGHT + j, rows, right_keep, right_send, block)
-
-
-def weight_back(table, proj_grad, normed_flip, held_keep, held_send):
+        weight = nn(normed_flip[...], proj_grad[0]).astype(LOW)
+        put(table, RIGHT, bits[1], rows, right_keep, right_send, weight)
+
+
+def weight_back(size, table, proj_grad, normed_flip, held_keep, held_send):
     width, length = normed_flip.shape
     inner = proj_grad.shape[2]
     early = pl.BlockSpec((width // 2, inner), lambda i, *_: (0, jnp.minimum(i, 1)))
     late = kept((width // 2, inner))
     return pl.pallas_call(
-        weight_back_kernel,
+        functools.partial(weight_back_kernel, side_bits(size)),
         grid_spec=pltpu.PrefetchScalarGridSpec(
             num_scalar_prefetch=1,
             grid=(3,),
@@ -680,12 +714,15 @@
     def _():
         gathered[...] = jnp.zeros_like(gathered)
 
+    gains, shifts = gathered[:8, :], gathered[8:, :]
     for at in tiles(tokens.shape[0]):
         pull = pulled[at, :].astype(WIDE) + far[at, :].astype(WIDE)
         hat, rate = hat_of(tokens[at, :])
-        gathered[:8, :] += fold_rows(pull * hat)
-        gathered[8:, :] += fold_rows(pull)
+        gains += fold_rows(pull * hat)
+        shifts += fold_rows(pull)
         result[at, :] = middle_grad[at, :] + norm_back(pull, hat, rate, vectors[0:1, :])
+    gathered[:8, :] = gains
+    gathered[8:, :] = shifts
 
     @pl.when(step == pl.num_programs(0) - 1)
     def _():
@@ -777,21 +814,6 @@
     )
 
 
-def join(left, left_far, right, right_far, size):
-    if size != BLOCKS:
-        return jnp.concatenate([left, left_far], 0), jnp.concatenate([right, right_far], 0)
-
-    def kernel(one, one_far, two, two_far, one_out, two_out):
-        rows = one.shape[0]
-        one_out[:rows, :] = one[...]
-        one_out[rows:, :] = one_far[...]
-        two_out[:rows, :] = two[...]
-        two_out[rows:, :] = two_far[...]
-
-    shapes = [jax.ShapeDtypeStruct((2 * v.shape[0], v.shape[1]), LOW) for v in (left, right)]
-    return vmem_call(kernel, shapes, (left, left_far, right, right_far), "join")
-
-
 def far_rows(values, size):
     if size != BLOCKS:
         whole = lax.all_gather(values, "fsdp", axis=0, tiled=True)
@@ -839,36 +861,58 @@
     )
 
 
-def second_stage(left, right, size):
+def quarters(whole):
+    rows = whole.shape[0] // 4
+    return [whole[k * rows : (k + 1) * rows] for k in range(4)]
+
+
+def spread(left, right, size):
+    if size != BLOCKS:
+        return quarters(left) + quarters(right)
+    left_next, right_next = hop(left, 2, size), hop(right, 1, size)
+    return [
+        left,
+        left_next,
+        hop(left, 1, size),
+        hop(left_next, 1, size),
+        right,
+        right_next,
+        hop(right, 2, size),
+        hop(right_next, 2, size),
+    ]
+
+
+def last_stage(left, right, size):
     if size != BLOCKS:
         return halves(left) + halves(right)
     return left, hop(left, 2, size), right, hop(right, 1, size)
 
 
-def third_stage(left, right, size):
-    if size != BLOCKS:
-        return halves(left) + halves(right)
-    return left, hop(left, 1, size), right, hop(right, 2, size)
-
-
-def fold_half(left, left_far, right, right_far, size):
-    if size != BLOCKS:
-        return left, left_far, right, right_far
-
-    def kernel(one, one_far, two, two_far, one_low, one_high, two_low, two_high):
-        rows = one_low.shape[0]
-        for a, b, low, high in (
-            (one, one_far, one_low, one_high),
-            (two, two_far, two_low, two_high),
-        ):
-            low[...] = (a[:rows, :].astype(WIDE) + b[:rows, :].astype(WIDE)).astype(LOW)
-            high[...] = (a[rows:, :].astype(WIDE) + b[rows:, :].astype(WIDE)).astype(LOW)
-
-    shapes = [
-        jax.ShapeDtypeStruct((v.shape[0] // 2, v.shape[1]), LOW)
-        for v in (left, left, right, right)
-    ]
-    return vmem_call(kernel, shapes, (left, left_far, right, right_far), "fold_half")
+def fold_half(groups, size):
+    if size != BLOCKS:
+        return [jnp.concatenate(part, axis=1) for part in zip(*groups)]
+    count = len(groups)
+
+    def kernel(*refs):
+        low, high, low_two, high_two = refs[4 * count :]
+        rows = low.shape[0]
+        start = 0
+        for k in range(count):
+            one, one_far, two, two_far = refs[4 * k : 4 * k + 4]
+            for a, b, to_low, to_high in (
+                (one, one_far, low, high),
+                (two, two_far, low_two, high_two),
+            ):
+                at = slice(start, start + a.shape[1]) if count > 1 else slice(None)
+                to_low[:, at] = (a[:rows, :].astype(WIDE) + b[:rows, :].astype(WIDE)).astype(LOW)
+                to_high[:, at] = (a[rows:, :].astype(WIDE) + b[rows:, :].astype(WIDE)).astype(LOW)
+            start += one.shape[1]
+
+    rows = groups[0][0].shape[0] // 2
+    left = sum(group[0].shape[1] for group in groups)
+    right = sum(group[2].shape[1] for group in groups)
+    shapes = [jax.ShapeDtypeStruct((rows, n), LOW) for n in (left, left, right, right)]
+    return vmem_call(kernel, shapes, [v for group in groups for v in group], "fold_half")
 
 
 def fold_quarter(left, left_far, right, right_far, size):
@@ -906,7 +950,7 @@
 def third_send(parts, size):
     if size != BLOCKS:
         return parts
-    return [parts[0]] + [hop(parts[k], 4 * k, size) for k in range(1, 4)]
+    return [parts[0]] + [hop(parts[k], 4 * k, size) for k in (3, 2, 1)]
 
 
 def total_of(parts, size):
@@ -919,11 +963,19 @@
     return total
 
 
-def sum_all(values, size):
+def sum_near(values, size):
+    if size != BLOCKS:
+        return values
+    for k in range(2):
+        values = values + hop(values, 1 << k, size)
+    return values
+
+
+def sum_far(values, size):
     if size != BLOCKS:
         return lax.psum(values, "fsdp")
-    for k in range(4):
-        values = values + hop(values, 1 << k, size)
+    for other in [hop(values, 4 * k, size) for k in range(1, 4)]:
+        values = values + other
     return values
 
 
@@ -948,12 +1000,10 @@
     length = 2 * half
     table = block_places(size, me)
 
+    norms = jnp.stack([gain_one, shift_one, gain_two, shift_two], axis=0)
     first = jnp.concatenate(
-        [
-            qkv_weight.transpose(1, 0, 2).reshape(rows, 3 * width),
-            jnp.stack([gain_one, shift_one, gain_two, shift_two], axis=1),
-            jnp.zeros((rows, LANES - 4), WIDE),
-        ],
+        [qkv_weight[0], qkv_weight[1], qkv_weight[2]]
+        + [jnp.pad(norms, ((0, rows - 4), (0, LANES - rows)))],
         axis=1,
     ).astype(LOW)
     second = jnp.concatenate([up_weight, out_weight.T], axis=1).astype(LOW)
@@ -965,48 +1015,55 @@
     qkv = collect(after(first, tokens), (3 * width + LANES) // 2)
     second = far_rows(after(second, qkv), size)
     third = beside(*third, size)
-    qkv = join(*second_stage(*qkv, size), size)
+    qkv = spread(*qkv, size)
     grad = in_order(cotangent, core)
     grad_flip = grad.T
     seg_col = jnp.broadcast_to(segment_ids[:, None], (length, LANES))
     seg_row = jnp.broadcast_to(segment_ids[None, :], (8, length))
-    up_out = collect(after(second, qkv, grad, grad_flip, seg_col, seg_row), SIDE * (-(-second[0].shape[1] // (2 * SIDE))))
+    up_out = collect(after(second, qkv[1], qkv[5]), SIDE * (-(-second[0].shape[1] // (2 * SIDE))))
     third = far_rows(after(third, up_out), size)
-    qkv = third_stage(*qkv, size)
-    up_out = second_stage(*up_out, size)
-
-    one_flip, proj, qkv_whole, vectors = enter(table, tokens, *qkv)
-    up_out = join(*after(up_out, proj), size)
-    proj = after(proj, up_out)
-    up_out = third_stage(*up_out, size)
-    att, lse = attend(proj, seg_col, seg_row)
+    tokens, grad, grad_flip, seg_col, seg_row = after(
+        (tokens, grad, grad_flip, seg_col, seg_row), up_out
+    )
+    up_out = spread(*up_out, size)
+
+    one_flip, proj, qkv_whole, vectors = enter(rows, table, tokens, *qkv)
+    proj = after(proj, up_out[1], up_out[5])
+    att, lse = attend(proj, seg_col, seg_row, 0, width // LANES)
     down = collect(after(third, att), hidden // 2)
     att = after(att, down, up_out)
-    down = second_stage(*down, size)
-    part, out_whole = leave(table, att, *up_out[2:])
+    down = last_stage(*down, size)
+    part, out_whole = leave(table, att, *up_out[4:])
     far = swap_cores(part)
     middle, two_flip, act, slope, up_whole = feed_first(
         table, tokens, part, far, vectors, hidden, *up_out
     )
-    branch, pulled, pre = feed_tokens(table, grad, act, slope, up_whole, *after(down, act))
-    parts = feed_weights(table, two_flip, grad_flip, act, pre)
-    far = after(swap_cores(pulled), parts)
-    parts = first_send(*parts, size)
+    down_parts = feed_weight(size, table, grad_flip, act)
+    down = after(down, down_parts)
+    down_parts = first_send(*down_parts, size)
+    branch, pulled, pre = feed_tokens(table, grad, act, slope, up_whole, *down)
+    up_parts = feed_weight(size, table, two_flip, pre)
+    far = after(swap_cores(pulled), up_parts)
+    up_parts = first_send(*up_parts, size)
 
     middle_grad, att_grad, *held, sums_two = middle_back(
-        table, pulled, far, middle, grad, vectors, out_whole, att
+        size, table, pulled, far, middle, grad, vectors, out_whole, att
     )
-    proj_grad = attend_back(proj, att, att_grad, lse, seg_col, seg_row)
-    parts = fold_half(*after(parts, proj_grad), size)
+    pairs = width // LANES
+    early = (2 * pairs + 2) // 3
+    known = (proj, att, att_grad, lse, seg_col, seg_row)
+    proj_grad = attend_back(*known, 0, early)
+    parts = fold_half(after([down_parts, up_parts], proj_grad), size)
     proj_grad = after(proj_grad, parts)
     parts = second_send(*parts, size)
-    tail = weight_back(table, proj_grad, one_flip, *held)
-    parts = fold_quarter(*after(parts, tail), size)
+    proj_grad = attend_back(*known, early, pairs, (proj_grad,))
+    tail = weight_back(size, table, proj_grad, one_flip, *held)
+    proj_grad = after(proj_grad, tail)
     tail = first_send(*tail, size)
-    proj_grad = after(proj_grad, parts)
+    pulled = token_back(proj_grad, qkv_whole)
+    parts = fold_quarter(*after(parts, pulled), size)
+    tail = fold_half([after(tail, parts)], size)
     parts = third_send(parts, size)
-    pulled = token_back(proj_grad, qkv_whole)
-    tail = fold_half(*after(tail, pulled), size)
     far = after(swap_cores(pulled), tail)
     tail = second_send(*tail, size)
     input_grad, sums_one = leave_layer(
@@ -1022,8 +1079,11 @@
     far = swap_cores(lax.dynamic_slice_in_dim(branch, (1 - core) * half, half, 0))
     outputs = own_half(middle) + (own_half(branch).astype(WIDE) + far.astype(WIDE))
     feed_grad = total_of(parts, size)
-    sums = sum_all(jnp.concatenate([sums_one[:2], sums_two[:2]], axis=0), size)
+    sums = sum_near(jnp.concatenate([sums_one[:2], sums_two[:2]], axis=0), size)
+    sums = sum_far(after(sums, tail), size)
     tail = total_of(tail, size)
+    part = hidden // 2
+    quarters = [feed_grad[:, k * part : (k + 1) * part] for k in range(4)]
     sums = lax.dynamic_slice_in_dim(sums, me * rows, rows, 1)
     qkv_grad = jnp.stack([tail[:, k * width : (k + 1) * width] for k in range(3)], axis=0)
     return (
@@ -1031,8 +1091,8 @@
         input_grad,
         qkv_grad,
         tail[:, 3 * width :].T,
-        feed_grad[:, :hidden],
-        feed_grad[:, hidden:].T,
+        jnp.concatenate([quarters[1], quarters[3]], axis=1),
+        jnp.concatenate([quarters[0].T, quarters[2].T], axis=0),
         sums[0],
         sums[1],
         sums[2],

time: 230 us -> 224 us (0.974)
  waiting for transfers between devices: 44 us -> 34.9 us
  starting transfers between devices: 50.5 us -> 57.7 us
  Pallas kernels: 109 us -> 104 us
    ppermute x39 -> x46, waiting for transfers between devices: 43.4 us -> 33.1 us  [hop(): return lax.ppermute(values, 'fsdp', [(i, i ^ bits) for i in range(size)])]
    ppermute x39 -> x46, starting transfers between devices: 49.9 us -> 57.1 us  [hop(): return lax.ppermute(values, 'fsdp', [(i, i ^ bits) for i in range(size)])]
    pallas_call x10 -> x8, Pallas kernels: 20.2 us -> 14.8 us  [vmem_call(): pl.pallas_call(kernel, out_shape=shapes, compiler_params=pltpu.CompilerPa...]
    transpose x2 -> x1, local copies, waits for them, and re-layouts: 2.48 us -> 0.04 us  [body(): quarters[0]]
    pallas_call x6 -> x8, Pallas kernels: 54.9 us -> 55 us  [the longest x1 13 us: attend(): pl.pallas_call(attend_kernel, grid=(end - begin,), in_specs=[part(0), par...]
  transfers between devices with their start and end apart: 45 -> 52, of which waited for: 18 -> 11; matrix products, arithmetic and copies ran while one was open for 9% -> 8% of each run, Pallas kernels for 40% -> 43%
where the time goes in v3:
time: 224 us; the launch traced here: 223 us
  Pallas kernels  104 us (46%)
  starting transfers between devices  57.7 us (26%)
  waiting for transfers between devices  34.9 us (16%)
  other arithmetic  15.6 us (7%)
  local copies, waits for them, and re-layouts  9.35 us (4%)
    ppermute x46, starting transfers between devices, hop(): return lax.ppermute(values, 'fsdp', [(i, i ^ bits) for i in range(size)])  57.1 us
    ppermute x46, waiting for transfers between devices, hop(): return lax.ppermute(values, 'fsdp', [(i, i ^ bits) for i in range(size)])  33.1 us
    pallas_call x8, Pallas kernels, vmem_call(): pl.pallas_call(kernel, out_shape=shapes, compiler_params=pltpu.CompilerPa...  14.8 us
    pallas_call x1, Pallas kernels, attend(): pl.pallas_call(attend_kernel, grid=(end - begin,), in_specs=[part(0), par...  13 us
    pallas_call x2, Pallas kernels, attend_back(): pl.pallas_call(attend_back_kernel, grid=(end - begin,), in_specs=[part(0)...  11.6 us
    pallas_call x2, Pallas kernels, feed_weight(): pl.pallas_call(functools.partial(feed_weight_kernel, side_bits(size)), gr...  11.1 us
    pallas_call x1, Pallas kernels, feed_tokens(): pl.pallas_call(feed_tokens_kernel, grid_spec=pltpu.PrefetchScalarGridSpec...  10.9 us
    pallas_call x1, Pallas kernels, feed_first(): pl.pallas_call(feed_first_kernel, grid_spec=pltpu.PrefetchScalarGridSpec(...  9.74 us
  transfers between devices with their start and end apart: 52, of which 11 were waited for; matrix products, arithmetic and copies ran while one was open for 8% of the time, Pallas kernels for 43%

profile of v3, /device:TPU:0, one launch (start us, length us, event | category | flops | bytes accessed | tf_op | source)
XLA Modules:
  0.0 223.2 jit_solution(12360900635278184076)
XLA Ops:
  3.5 2.8 %collective-permute-start.2 = (bf16[48,1280]{1,0:T(8,128)(2,1)S(1)}, bf16[48,1280]{1,0:T(8,128)(2,1)S(1)}, u32[]{:S(2)}, u32[]{:S(2)}) collective-permute-start(bf16[48,1280]{1,0:T(8,128)(2,1)S(1)} %pad_maximum_fusion.4.refs_0_), channel_id=1, source_target_pairs={{0,8},{2,10},{4,12},{6,14},{8,0},{10,2},{12,4},{14,6},{16,24},{18,... | collective-permute-start | bytes 368648 | tf_op jit(solution)/shard_map/ppermute | solution.py:769
  6.3 2.6 %collective-permute-start.3 = (bf16[48,1280]{1,0:T(8,128)(2,1)S(1)}, bf16[48,1280]{1,0:T(8,128)(2,1)S(1)}, u32[]{:S(2)}, u32[]{:S(2)}) collective-permute-start(bf16[48,1280]{1,0:T(8,128)(2,1)S(1)} %pad_maximum_fusion.4.refs_0_), channel_id=1, source_target_pairs={{0,16},{2,18},{4,20},{6,22},{8,24},{10,26},{12,28},{14,30},{16,0},... | collective-permute-start | bytes 368648 | tf_op jit(solution)/shard_map/ppermute | solution.py:769
  29.1 3.3 %maximum_select_fusion.1.grad = bf16[1024,768]{1,0:T(8,128)(2,1)} fusion(bf16[512,768]{1,0:T(8,128)(2,1)} %collective-permute-done.1, bf16[512,768]{1,0:T(8,128)(2,1)} %param.21, pred[]{:T(512)S(6)} %eq.4), kind=kLoop, calls=%fused_computation.1 | loop fusion | flops 7077888 | bytes 3145729 | tf_op jit(solution)/shard_map/jit(_where)/select_n | solution.py:857
  33.0 5.5 %collective-permute-done.6.refs_2_ = bf16[48,1920]{1,0:T(8,128)(2,1)} collective-permute-done((bf16[48,1920]{1,0:T(8,128)(2,1)}, bf16[48,1920]{1,0:T(8,128)(2,1)}, u32[]{:S(2)}, u32[]{:S(2)}) %collective-permute-start.6) | collective-permute-done | bytes 184352 | tf_op jit(solution)/shard_map/ppermute | solution.py:769
  51.0 6.8 %enter.1 = (bf16[768,1024]{1,0:T(8,128)(2,1)S(1)}, bf16[1024,1152]{1,0:T(8,128)(2,1)S(1)}, bf16[768,1152]{1,0:T(8,128)(2,1)S(1)}, f32[8,768]{1,0:T(8,128)S(1)}) custom-call(s32[64]{0:T(128)S(1)} %pad_add_fusion.table, f32[1024,768]{1,0:T(8,128)S(1)} %maximum_select_fusion.tokens, bf16[192,640]{1,0:T(8,128)(2,1)} %get-tuple-element.127.wa, ...), custom_call_target="tpu_custom_call" | custom-call | flops 9999999827968 | bytes 1000000000 | tf_op jit(solution)/shard_map/enter/pallas_call | solution.py:146
  61.2 13.0 %attend.1 = (bf16[1024,384]{1,0:T(8,128)(2,1)S(1)}, f32[24,1024]{1,0:T(8,128)S(1)}) custom-call(bf16[1024,1152]{1,0:T(8,128)(2,1)S(1)} %get-tuple-element.138.queries.keys.values, bf16[1024,1152]{1,0:T(8,128)(2,1)S(1)} %get-tuple-element.138.queries.keys.values, bf16[1024,1152]{1,0:T(8,128)(2,1)S(1)} %get-tuple-element.138.queries.keys.values, ...), custom_call_target="tpu_custom_call" | custom-call | flops 9999999827968 | bytes 1000000000 | tf_op jit(solution)/shard_map/attend/pallas_call | solution.py:227
  79.3 2.6 %collective-permute-done.24.wd.wh = bf16[192,896]{1,0:T(8,128)(2,1)} collective-permute-done((bf16[192,896]{1,0:T(8,128)(2,1)}, bf16[192,896]{1,0:T(8,128)(2,1)}, u32[]{:S(2)}, u32[]{:S(2)}) %collective-permute-start.24) | collective-permute-done | bytes 344096 | tf_op jit(solution)/shard_map/ppermute | solution.py:769
  83.9 4.7 %leave.1 = (bf16[1024,768]{1,0:T(8,128)(2,1)}, bf16[768,384]{1,0:T(8,128)(2,1)S(1)}) custom-call(s32[64]{0:T(128)S(1)} %pad_add_fusion.table, bf16[1024,384]{1,0:T(8,128)(2,1)S(1)} %get-tuple-element.149.att.out, bf16[192,896]{1,0:T(8,128)(2,1)} %get-tuple-element.135.wa.we, bf16[192,896]{1,0:T(8,128)(2,1)} %collective-permute-done.15.wb.wf, ...), custom_call_target="tpu_custom_call" | custom-call | flops 9999999827968 | bytes 1000000000 | tf_op jit(solution)/shard_map/leave/pallas_call | solution.py:343
  95.1 9.7 %feed_first.1 = (f32[1024,768]{1,0:T(8,128)S(1)}, bf16[768,1024]{1,0:T(8,128)(2,1)S(1)}, bf16[1024,1536]{1,0:T(8,128)(2,1)S(1)}, bf16[1024,1536]{1,0:T(8,128)(2,1)S(1)}, bf16[768,1536]{1,0:T(8,128)(2,1)S(1)}) custom-call(s32[64]{0:T(128)S(1)} %copy-done.11, f32[1024,768]{1,0:T(8,128)S(1)} %copy-done.2, bf16[1024,768]{1,0:T(8,128)(2,1)} %get-tuple-element.150.part, ...), custom_call_target="tpu_custom_call" | custom-call | flops 9999999827968 | bytes 1000000000 | tf_op jit(solution)/shard_map/feed_first/pallas_call | solution.py:420
  104.9 5.4 %feed_weight.2 = (bf16[384,768]{1,0:T(8,128)(2,1)S(1)}, bf16[384,768]{1,0:T(8,128)(2,1)}, bf16[384,768]{1,0:T(8,128)(2,1)S(1)}, bf16[384,768]{1,0:T(8,128)(2,1)}) custom-call(s32[64]{0:T(128)S(1)} %copy-done.11, bf16[768,1024]{1,0:T(8,128)(2,1)S(1)} %copy.24.flip, bf16[1024,1536]{1,0:T(8,128)(2,1)S(1)} %get-tuple-element.154.side.act), custom_call_target="tpu_custom_call" | custom-call | flops 9999999827968 | bytes 1000000000 | tf_op jit(solution)/shard_map/feed_weight/pallas_call | solution.py:526
  111.5 10.9 %feed_tokens.1 = (bf16[1024,768]{1,0:T(8,128)(2,1)S(1)}, bf16[1024,768]{1,0:T(8,128)(2,1)}, bf16[1024,1536]{1,0:T(8,128)(2,1)S(1)}) custom-call(s32[64]{0:T(128)S(1)} %copy-done.11, bf16[1024,768]{1,0:T(8,128)(2,1)S(1)} %copy-done, bf16[1024,1536]{1,0:T(8,128)(2,1)S(1)} %get-tuple-element.154.side.act, bf16[1024,1536]{1,0:T(8,128)(2,1)S(1)} %get-tuple-element.161.slope, ...), custom_call_target="tpu_custom_call" | custom-call | flops 9999999827968 | bytes 1000000000 | tf_op jit(solution)/shard_map/feed_tokens/pallas_call | solution.py:483
  122.4 5.7 %feed_weight.3 = (bf16[384,768]{1,0:T(8,128)(2,1)S(1)}, bf16[384,768]{1,0:T(8,128)(2,1)}, bf16[384,768]{1,0:T(8,128)(2,1)S(1)}, bf16[384,768]{1,0:T(8,128)(2,1)}) custom-call(s32[64]{0:T(128)S(1)} %copy-done.11, bf16[768,1024]{1,0:T(8,128)(2,1)S(1)} %get-tuple-element.159.flip, bf16[1024,1536]{1,0:T(8,128)(2,1)S(1)} %get-tuple-element.167.side), custom_call_target="tpu_custom_call" | custom-call | flops 9999999827968 | bytes 1000000000 | tf_op jit(solution)/shard_map/feed_weight/pallas_call | solution.py:526
  131.0 7.7 %middle_back.1 = (f32[1024,768]{1,0:T(8,128)S(1)}, bf16[1024,384]{1,0:T(8,128)(2,1)S(1)}, bf16[384,768]{1,0:T(8,128)(2,1)S(1)}, bf16[384,768]{1,0:T(8,128)(2,1)}, f32[8,768]{1,0:T(8,128)S(1)}) custom-call(s32[64]{0:T(128)S(1)} %copy-done.11, bf16[1024,768]{1,0:T(8,128)(2,1)} %get-tuple-element.172.pulled, bf16[1024,768]{1,0:T(8,128)(2,1)} %collective-permute-done.32.far, ...), custom_call_target="tpu_custom_call" | custom-call | flops 9999999827968 | bytes 1000000000 | tf_op jit(solution)/shard_map/middle_back/pallas_call | solution.py:592
  138.7 7.8 %attend_back.2.refs_0_ = bf16[3,1024,384]{2,1,0:T(8,128)(2,1)S(1)} custom-call(bf16[1024,1152]{1,0:T(8,128)(2,1)S(1)} %copy-done.17, bf16[1024,1152]{1,0:T(8,128)(2,1)S(1)} %copy-done.17, bf16[1024,1152]{1,0:T(8,128)(2,1)S(1)} %copy-done.17, bf16[1024,384]{1,0:T(8,128)(2,1)S(1)} %copy-done.24, bf16[1024,384]{1,0:T(8,128)(2,1)S(1)} %get-tuple-element.175.grad, ...), custom_call_target="tpu_custom_call" | custom-call | flops 9999999827968 | bytes 1000000000 | tf_op jit(solution)/shard_map/attend_back/pallas_call | solution.py:298
  146.7 3.0 %fold_half.2 = (bf16[192,1536]{1,0:T(8,128)(2,1)S(1)}, bf16[192,1536]{1,0:T(8,128)(2,1)}, bf16[192,1536]{1,0:T(8,128)(2,1)S(1)}, bf16[192,1536]{1,0:T(8,128)(2,1)}) custom-call(bf16[384,768]{1,0:T(8,128)(2,1)S(1)} %get-tuple-element.177.refs_0_, bf16[384,768]{1,0:T(8,128)(2,1)} %collective-permute-done.26.refs_1_, ...), custom_call_target="tpu_custom_call" | custom-call | flops 9999999827968 | bytes 1000000000 | tf_op jit(solution)/shard_map/fold_half/pallas_call | solution.py:789
  150.9 3.8 %attend_back.3.proj_grad = bf16[3,1024,384]{2,1,0:T(8,128)(2,1)S(1)} custom-call(bf16[1024,1152]{1,0:T(8,128)(2,1)S(1)} %copy-done.18, bf16[1024,1152]{1,0:T(8,128)(2,1)S(1)} %copy-done.18, bf16[1024,1152]{1,0:T(8,128)(2,1)S(1)} %copy-done.18, bf16[1024,384]{1,0:T(8,128)(2,1)S(1)} %copy-done.25, ...), custom_call_target="tpu_custom_call", output_to_operand_aliasing={{}: (8, {})} | custom-call | flops 9999999827968 | bytes 1000000000 | tf_op jit(solution)/shard_map/attend_back/pallas_call | solution.py:298
  154.7 4.7 %weight_back.1 = (bf16[384,768]{1,0:T(8,128)(2,1)S(1)}, bf16[384,768]{1,0:T(8,128)(2,1)}, bf16[384,768]{1,0:T(8,128)(2,1)S(1)}, bf16[384,768]{1,0:T(8,128)(2,1)}) custom-call(s32[64]{0:T(128)S(1)} %copy-done.11, bf16[3,1024,384]{2,1,0:T(8,128)(2,1)S(1)} %attend_back.3.proj_grad, ...), custom_call_target="tpu_custom_call", output_to_operand_aliasing={{2}: (3, {}), {3}: (4, {})} | custom-call | flops 9999999827968 | bytes 1000000000 | tf_op jit(solution)/shard_map/weight_back/pallas_call | solution.py:663
  162.3 4.2 %token_back.1.pulled = bf16[1024,768]{1,0:T(8,128)(2,1)} custom-call(bf16[3,1024,384]{2,1,0:T(8,128)(2,1)S(1)} %attend_back.3.proj_grad, bf16[768,1152]{1,0:T(8,128)(2,1)S(1)} %copy-done.20), custom_call_target="tpu_custom_call" | custom-call | flops 9999999827968 | bytes 1000000000 | tf_op jit(solution)/shard_map/token_back/pallas_call | solution.py:695
  171.6 6.6 %collective-permute-done.39.refs_1_ = bf16[384,768]{1,0:T(8,128)(2,1)} collective-permute-done((bf16[384,768]{1,0:T(8,128)(2,1)}, bf16[384,768]{1,0:T(8,128)(2,1)}, u32[]{:S(2)}, u32[]{:S(2)}) %collective-permute-start.39) | collective-permute-done | bytes 589856 | tf_op jit(solution)/shard_map/ppermute | solution.py:769
  183.5 5.1 %leave_layer.1 = (f32[512,768]{1,0:T(8,128)}, f32[8,768]{1,0:T(8,128)S(1)}) custom-call(s32[1]{0:T(128)} %bitcast.11.core, bf16[1024,768]{1,0:T(8,128)(2,1)} %token_back.1.pulled, bf16[1024,768]{1,0:T(8,128)(2,1)} %collective-permute-done.38.far, f32[1024,768]{1,0:T(8,128)S(1)} %copy-done.3, f32[1024,768]{1,0:T(8,128)S(1)} %get-tuple-element.217.middle_grad, ...), custom_call_target="tpu_custom_call" | custom-call | flops 9999999827968 | bytes 1000000000 | tf_op jit(solution)/shard_map/leave_layer/pallas_call | solution.py:742
  195.4 9.7 %collective-permute-done.36 = bf16[48,3072]{1,0:T(8,128)(2,1)} collective-permute-done((bf16[48,3072]{1,0:T(8,128)(2,1)}, bf16[48,3072]{1,0:T(8,128)(2,1)}, u32[]{:S(2)}, u32[]{:S(2)}) %collective-permute-start.36) | collective-permute-done | bytes 294944 | tf_op jit(solution)/shard_map/ppermute | solution.py:769
  210.6 2.4 %collective-permute-done.48 = f32[4,768]{1,0:T(4,128)S(1)} collective-permute-done((f32[4,768]{1,0:T(4,128)S(1)}, f32[4,768]{1,0:T(4,128)S(1)}, u32[]{:S(2)}, u32[]{:S(2)}) %collective-permute-start.48) | collective-permute-done | bytes 12320 | tf_op jit(solution)/shard_map/ppermute | solution.py:769
  213.1 2.7 %collective-permute-start.50 = (f32[4,768]{1,0:T(4,128)S(1)}, f32[4,768]{1,0:T(4,128)S(1)}, u32[]{:S(2)}, u32[]{:S(2)}) collective-permute-start(f32[4,768]{1,0:T(4,128)S(1)} %add.94), channel_id=1, source_target_pairs={{0,16},{2,18},{4,20},{6,22},{8,24},{10,26},{12,28},{14,30},{16,0},... | collective-permute-start | bytes 36872 | tf_op jit(solution)/shard_map/ppermute | solution.py:769
  218.9 2.4 %collective-permute-done.51 = f32[4,768]{1,0:T(4,128)S(1)} collective-permute-done((f32[4,768]{1,0:T(4,128)S(1)}, f32[4,768]{1,0:T(4,128)S(1)}, u32[]{:S(2)}, u32[]{:S(2)}) %collective-permute-start.51) | collective-permute-done | bytes 12320 | tf_op jit(solution)/shard_map/ppermute | solution.py:769
  (204 shorter events, 88.9 us)
Async XLA Ops:
  21.9 16.6 %collective-permute-start.6 = (bf16[48,1920]{1,0:T(8,128)(2,1)}, bf16[48,1920]{1,0:T(8,128)(2,1)}, u32[]{:S(2)}, u32[]{:S(2)}) collective-permute-start(bf16[48,1920]{1,0:T(8,128)(2,1)} %pad_maximum_fusion.3.refs_0_), channel_id=1, source_target_pairs={{0,16},{2,18},{4,20},{6,22},{8,24},{10,26},{12,28},{14,30},{16,0},... | collective-permute-start | bytes 552968 | tf_op jit(solution)/shard_map/ppermute | solution.py:769
  23.0 17.0 %collective-permute-start.7 = (bf16[48,1920]{1,0:T(8,128)(2,1)}, bf16[48,1920]{1,0:T(8,128)(2,1)}, u32[]{:S(2)}, u32[]{:S(2)}) collective-permute-start(bf16[48,1920]{1,0:T(8,128)(2,1)} %pad_maximum_fusion.3.refs_0_), channel_id=1, source_target_pairs={{0,24},{2,26},{4,28},{6,30},{8,16},{10,18},{12,20},{14,22},{16,8},... | collective-permute-start | bytes 552968 | tf_op jit(solution)/shard_map/ppermute | solution.py:769
  44.2 30.1 %collective-permute-start.18 = (bf16[96,1536]{1,0:T(8,128)(2,1)}, bf16[96,1536]{1,0:T(8,128)(2,1)}, u32[]{:S(2)}, u32[]{:S(2)}) collective-permute-start(bf16[96,1536]{1,0:T(8,128)(2,1)} %beside.1.refs_0_), channel_id=1, source_target_pairs={{0,8},{2,10},{4,12},{6,14},{8,0},{10,2},{12,4},{14,6},{16,24},{18,... | collective-permute-start | bytes 884744 | tf_op jit(solution)/shard_map/ppermute | solution.py:769
  46.4 29.3 %collective-permute-start.19 = (bf16[96,1536]{1,0:T(8,128)(2,1)}, bf16[96,1536]{1,0:T(8,128)(2,1)}, u32[]{:S(2)}, u32[]{:S(2)}) collective-permute-start(bf16[96,1536]{1,0:T(8,128)(2,1)} %beside.1.refs_0_), channel_id=1, source_target_pairs={{0,16},{2,18},{4,20},{6,22},{8,24},{10,26},{12,28},{14,30},{16,0},... | collective-permute-start | bytes 884744 | tf_op jit(solution)/shard_map/ppermute | solution.py:769
  47.5 28.3 %collective-permute-start.20 = (bf16[96,1536]{1,0:T(8,128)(2,1)}, bf16[96,1536]{1,0:T(8,128)(2,1)}, u32[]{:S(2)}, u32[]{:S(2)}) collective-permute-start(bf16[96,1536]{1,0:T(8,128)(2,1)} %beside.1.refs_0_), channel_id=1, source_target_pairs={{0,24},{2,26},{4,28},{6,30},{8,16},{10,18},{12,20},{14,22},{16,8},... | collective-permute-start | bytes 884744 | tf_op jit(solution)/shard_map/ppermute | solution.py:769
  59.1 20.2 %collective-permute-start.21 = (bf16[192,1024]{1,0:T(8,128)(2,1)}, bf16[192,1024]{1,0:T(8,128)(2,1)}, u32[]{:S(2)}, u32[]{:S(2)}) collective-permute-start(bf16[192,1024]{1,0:T(8,128)(2,1)} %get-tuple-element.134.wa), channel_id=1, source_target_pairs={{0,2},{2,0},{4,6},{6,4},{8,10},{10,8},{12,14},{14,12},{16,18},{18,... | collective-permute-start | bytes 1179656 | tf_op jit(solution)/shard_map/ppermute | solution.py:769
  60.6 18.7 %collective-permute-start.23 = (bf16[192,896]{1,0:T(8,128)(2,1)}, bf16[192,896]{1,0:T(8,128)(2,1)}, u32[]{:S(2)}, u32[]{:S(2)}) collective-permute-start(bf16[192,896]{1,0:T(8,128)(2,1)} %get-tuple-element.135.wa.we), channel_id=1, source_target_pairs={{0,4},{2,6},{4,0},{6,2},{8,12},{10,14},{12,8},{14,10},{16,20},{18,... | collective-permute-start | bytes 1032200 | tf_op jit(solution)/shard_map/ppermute | solution.py:769
  90.3 21.2 %collective-permute-start.28 = (bf16[384,768]{1,0:T(8,128)(2,1)}, bf16[384,768]{1,0:T(8,128)(2,1)}, u32[]{:S(2)}, u32[]{:S(2)}) collective-permute-start(bf16[384,768]{1,0:T(8,128)(2,1)} %copy-done.12), channel_id=1, source_target_pairs={{0,4},{2,6},{4,0},{6,2},{8,12},{10,14},{12,8},{14,10},{16,20},{18,... | collective-permute-start | bytes 1769480 | tf_op jit(solution)/shard_map/ppermute | solution.py:769
  90.9 20.5 %collective-permute-start.29 = (bf16[384,768]{1,0:T(8,128)(2,1)}, bf16[384,768]{1,0:T(8,128)(2,1)}, u32[]{:S(2)}, u32[]{:S(2)}) collective-permute-start(bf16[384,768]{1,0:T(8,128)(2,1)} %copy-done.14), channel_id=1, source_target_pairs={{0,2},{2,0},{4,6},{6,4},{8,10},{10,8},{12,14},{14,12},{16,18},{18,... | collective-permute-start | bytes 1769480 | tf_op jit(solution)/shard_map/ppermute | solution.py:769
  110.3 36.3 %collective-permute-start.26 = (bf16[384,768]{1,0:T(8,128)(2,1)}, bf16[384,768]{1,0:T(8,128)(2,1)}, u32[]{:S(2)}, u32[]{:S(2)}) collective-permute-start(bf16[384,768]{1,0:T(8,128)(2,1)} %get-tuple-element.156), channel_id=1, source_target_pairs={{0,2},{2,0},{4,6},{6,4},{8,10},{10,8},{12,14},{14,12},{16,18},{18,... | collective-permute-start | bytes 1769480 | tf_op jit(solution)/shard_map/ppermute | solution.py:769
  110.8 35.8 %collective-permute-start.27 = (bf16[384,768]{1,0:T(8,128)(2,1)}, bf16[384,768]{1,0:T(8,128)(2,1)}, u32[]{:S(2)}, u32[]{:S(2)}) collective-permute-start(bf16[384,768]{1,0:T(8,128)(2,1)} %get-tuple-element.158), channel_id=1, source_target_pairs={{0,4},{2,6},{4,0},{6,2},{8,12},{10,14},{12,8},{14,10},{16,20},{18,... | collective-permute-start | bytes 1769480 | tf_op jit(solution)/shard_map/ppermute | solution.py:769
  128.1 18.5 %collective-permute-start.30 = (bf16[384,768]{1,0:T(8,128)(2,1)}, bf16[384,768]{1,0:T(8,128)(2,1)}, u32[]{:S(2)}, u32[]{:S(2)}) collective-permute-start(bf16[384,768]{1,0:T(8,128)(2,1)} %get-tuple-element.169), channel_id=1, source_target_pairs={{0,2},{2,0},{4,6},{6,4},{8,10},{10,8},{12,14},{14,12},{16,18},{18,... | collective-permute-start | bytes 1769480 | tf_op jit(solution)/shard_map/ppermute | solution.py:769
  129.6 17.0 %collective-permute-start.31 = (bf16[384,768]{1,0:T(8,128)(2,1)}, bf16[384,768]{1,0:T(8,128)(2,1)}, u32[]{:S(2)}, u32[]{:S(2)}) collective-permute-start(bf16[384,768]{1,0:T(8,128)(2,1)} %get-tuple-element.171), channel_id=1, source_target_pairs={{0,4},{2,6},{4,0},{6,2},{8,12},{10,14},{12,8},{14,10},{16,20},{18,... | collective-permute-start | bytes 1769480 | tf_op jit(solution)/shard_map/ppermute | solution.py:769
  149.7 17.4 %collective-permute-start.33 = (bf16[192,1536]{1,0:T(8,128)(2,1)}, bf16[192,1536]{1,0:T(8,128)(2,1)}, u32[]{:S(2)}, u32[]{:S(2)}) collective-permute-start(bf16[192,1536]{1,0:T(8,128)(2,1)} %get-tuple-element.186), channel_id=1, source_target_pairs={{0,4},{2,6},{4,0},{6,2},{8,12},{10,14},{12,8},{14,10},{16,20},{18,... | collective-permute-start | bytes 1769480 | tf_op jit(solution)/shard_map/ppermute | solution.py:769
  150.3 16.8 %collective-permute-start.34 = (bf16[192,1536]{1,0:T(8,128)(2,1)}, bf16[192,1536]{1,0:T(8,128)(2,1)}, u32[]{:S(2)}, u32[]{:S(2)}) collective-permute-start(bf16[192,1536]{1,0:T(8,128)(2,1)} %get-tuple-element.188), channel_id=1, source_target_pairs={{0,2},{2,0},{4,6},{6,4},{8,10},{10,8},{12,14},{14,12},{16,18},{18,... | collective-permute-start | bytes 1769480 | tf_op jit(solution)/shard_map/ppermute | solution.py:769
  159.4 18.7 %collective-permute-start.39 = (bf16[384,768]{1,0:T(8,128)(2,1)}, bf16[384,768]{1,0:T(8,128)(2,1)}, u32[]{:S(2)}, u32[]{:S(2)}) collective-permute-start(bf16[384,768]{1,0:T(8,128)(2,1)} %get-tuple-element.194), channel_id=1, source_target_pairs={{0,2},{2,0},{4,6},{6,4},{8,10},{10,8},{12,14},{14,12},{16,18},{18,... | collective-permute-start | bytes 1769480 | tf_op jit(solution)/shard_map/ppermute | solution.py:769
  160.9 18.3 %collective-permute-start.40 = (bf16[384,768]{1,0:T(8,128)(2,1)}, bf16[384,768]{1,0:T(8,128)(2,1)}, u32[]{:S(2)}, u32[]{:S(2)}) collective-permute-start(bf16[384,768]{1,0:T(8,128)(2,1)} %get-tuple-element.196), channel_id=1, source_target_pairs={{0,4},{2,6},{4,0},{6,2},{8,12},{10,14},{12,8},{14,10},{16,20},{18,... | collective-permute-start | bytes 1769480 | tf_op jit(solution)/shard_map/ppermute | solution.py:769
  166.5 15.8 %collective-permute-start.38 = (bf16[1024,768]{1,0:T(8,128)(2,1)}, bf16[1024,768]{1,0:T(8,128)(2,1)}, u32[]{:S(2)}, u32[]{:S(2)}) collective-permute-start(bf16[1024,768]{1,0:T(8,128)(2,1)} %token_back.1.pulled), channel_id=1, source_target_pairs={{0,1},{1,0},{2,3},{3,2},{4,5},{5,4},{6,7},{7,6},{8,9},{9,8},{10,11... | collective-permute-start | bytes 4718600 | tf_op jit(solution)/shard_map/ppermute | solution.py:765
  169.4 24.7 %collective-permute-start.35 = (bf16[48,3072]{1,0:T(8,128)(2,1)}, bf16[48,3072]{1,0:T(8,128)(2,1)}, u32[]{:S(2)}, u32[]{:S(2)}) collective-permute-start(bf16[48,3072]{1,0:T(8,128)(2,1)} %get-tuple-element.204), channel_id=1, source_target_pairs={{0,24},{2,26},{4,28},{6,30},{8,16},{10,18},{12,20},{14,22},{16,8},... | collective-permute-start | bytes 884744 | tf_op jit(solution)/shard_map/ppermute | solution.py:769
  171.4 33.7 %collective-permute-start.36 = (bf16[48,3072]{1,0:T(8,128)(2,1)}, bf16[48,3072]{1,0:T(8,128)(2,1)}, u32[]{:S(2)}, u32[]{:S(2)}) collective-permute-start(bf16[48,3072]{1,0:T(8,128)(2,1)} %get-tuple-element.205), channel_id=1, source_target_pairs={{0,16},{2,18},{4,20},{6,22},{8,24},{10,26},{12,28},{14,30},{16,0},... | collective-permute-start | bytes 884744 | tf_op jit(solution)/shard_map/ppermute | solution.py:769
  178.1 26.9 %collective-permute-start.37 = (bf16[48,3072]{1,0:T(8,128)(2,1)}, bf16[48,3072]{1,0:T(8,128)(2,1)}, u32[]{:S(2)}, u32[]{:S(2)}) collective-permute-start(bf16[48,3072]{1,0:T(8,128)(2,1)} %get-tuple-element.206), channel_id=1, source_target_pairs={{0,8},{2,10},{4,12},{6,14},{8,0},{10,2},{12,4},{14,6},{16,24},{18,... | collective-permute-start | bytes 884744 | tf_op jit(solution)/shard_map/ppermute | solution.py:769
  190.9 22.0 %collective-permute-start.44 = (bf16[48,1536]{1,0:T(8,128)(2,1)S(1)}, bf16[48,1536]{1,0:T(8,128)(2,1)S(1)}, u32[]{:S(2)}, u32[]{:S(2)}) collective-permute-start(bf16[48,1536]{1,0:T(8,128)(2,1)S(1)} %get-tuple-element.227), channel_id=1, source_target_pairs={{0,24},{2,26},{4,28},{6,30},{8,16},{10,18},{12,20},{14,22},{16,8},... | collective-permute-start | bytes 442376 | tf_op jit(solution)/shard_map/ppermute | solution.py:769
  193.1 19.9 %collective-permute-start.45 = (bf16[48,1536]{1,0:T(8,128)(2,1)S(1)}, bf16[48,1536]{1,0:T(8,128)(2,1)S(1)}, u32[]{:S(2)}, u32[]{:S(2)}) collective-permute-start(bf16[48,1536]{1,0:T(8,128)(2,1)S(1)} %get-tuple-element.226), channel_id=1, source_target_pairs={{0,16},{2,18},{4,20},{6,22},{8,24},{10,26},{12,28},{14,30},{16,0},... | collective-permute-start | bytes 442376 | tf_op jit(solution)/shard_map/ppermute | solution.py:769
  194.1 18.9 %collective-permute-start.46 = (bf16[48,1536]{1,0:T(8,128)(2,1)S(1)}, bf16[48,1536]{1,0:T(8,128)(2,1)S(1)}, u32[]{:S(2)}, u32[]{:S(2)}) collective-permute-start(bf16[48,1536]{1,0:T(8,128)(2,1)S(1)} %get-tuple-element.225), channel_id=1, source_target_pairs={{0,8},{2,10},{4,12},{6,14},{8,0},{10,2},{12,4},{14,6},{16,24},{18,... | collective-permute-start | bytes 442376 | tf_op jit(solution)/shard_map/ppermute | solution.py:769
  (62 other events, 599.7 us)

commit v4 on v3

--- a/solution.py
+++ b/solution.py
@@ -789,7 +789,7 @@
     return pl.pallas_call(
         kernel,
         out_shape=shapes,
-        compiler_params=pltpu.CompilerParams(vmem_limit_bytes=24 * 1024 * 1024),
+        compiler_params=pltpu.CompilerParams(vmem_limit_bytes=8 * 1024 * 1024),
         cost_estimate=LONG,
         name=name,
     )(*args)

time: 224 us -> 224 us (level)
    unnamed x68 -> x60, local copies, waits for them, and re-layouts: 5.84 us -> 5.83 us
where the time goes in v4:
time: 224 us; the launch traced here: 223 us
  Pallas kernels  104 us (46%)
  starting transfers between devices  57.8 us (26%)
  waiting for transfers between devices  35.1 us (16%)
  other arithmetic  15.7 us (7%)
  local copies, waits for them, and re-layouts  9.34 us (4%)
    ppermute x46, starting transfers between devices, hop(): return lax.ppermute(values, 'fsdp', [(i, i ^ bits) for i in range(size)])  57.2 us
    ppermute x46, waiting for transfers between devices, hop(): return lax.ppermute(values, 'fsdp', [(i, i ^ bits) for i in range(size)])  33.3 us
    pallas_call x8, Pallas kernels, vmem_call(): pl.pallas_call(kernel, out_shape=shapes, compiler_params=pltpu.CompilerPa...  14.7 us
    pallas_call x1, Pallas kernels, attend(): pl.pallas_call(attend_kernel, grid=(end - begin,), in_specs=[part(0), par...  13 us
    pallas_call x2, Pallas kernels, attend_back(): pl.pallas_call(attend_back_kernel, grid=(end - begin,), in_specs=[part(0)...  11.6 us
    pallas_call x2, Pallas kernels, feed_weight(): pl.pallas_call(functools.partial(feed_weight_kernel, side_bits(size)), gr...  11.1 us
    pallas_call x1, Pallas kernels, feed_tokens(): pl.pallas_call(feed_tokens_kernel, grid_spec=pltpu.PrefetchScalarGridSpec...  10.9 us
    pallas_call x1, Pallas kernels, feed_first(): pl.pallas_call(feed_first_kernel, grid_spec=pltpu.PrefetchScalarGridSpec(...  9.74 us
  transfers between devices with their start and end apart: 52, of which 11 were waited for; matrix products, arithmetic and copies ran while one was open for 8% of the time, Pallas kernels for 43%

profile of v4, /device:TPU:0, one launch (start us, length us, event | category | flops | bytes accessed | tf_op | source)
XLA Modules:
  0.0 223.0 jit_solution(383344963625991535)
XLA Ops:
  3.5 2.8 %collective-permute-start.2 = (bf16[48,1280]{1,0:T(8,128)(2,1)S(1)}, bf16[48,1280]{1,0:T(8,128)(2,1)S(1)}, u32[]{:S(2)}, u32[]{:S(2)}) collective-permute-start(bf16[48,1280]{1,0:T(8,128)(2,1)S(1)} %pad_maximum_fusion.4.refs_0_), channel_id=1, source_target_pairs={{0,8},{2,10},{4,12},{6,14},{8,0},{10,2},{12,4},{14,6},{16,24},{18,... | collective-permute-start | bytes 368648 | tf_op jit(solution)/shard_map/ppermute | solution.py:769
  6.3 2.6 %collective-permute-start.3 = (bf16[48,1280]{1,0:T(8,128)(2,1)S(1)}, bf16[48,1280]{1,0:T(8,128)(2,1)S(1)}, u32[]{:S(2)}, u32[]{:S(2)}) collective-permute-start(bf16[48,1280]{1,0:T(8,128)(2,1)S(1)} %pad_maximum_fusion.4.refs_0_), channel_id=1, source_target_pairs={{0,16},{2,18},{4,20},{6,22},{8,24},{10,26},{12,28},{14,30},{16,0},... | collective-permute-start | bytes 368648 | tf_op jit(solution)/shard_map/ppermute | solution.py:769
  29.1 3.4 %maximum_select_fusion.1.grad = bf16[1024,768]{1,0:T(8,128)(2,1)} fusion(bf16[512,768]{1,0:T(8,128)(2,1)} %collective-permute-done.1, bf16[512,768]{1,0:T(8,128)(2,1)} %param.21, pred[]{:T(512)S(6)} %eq.4), kind=kLoop, calls=%fused_computation.1 | loop fusion | flops 7077888 | bytes 3145729 | tf_op jit(solution)/shard_map/jit(_where)/select_n | solution.py:857
  33.0 5.5 %collective-permute-done.6.refs_2_ = bf16[48,1920]{1,0:T(8,128)(2,1)} collective-permute-done((bf16[48,1920]{1,0:T(8,128)(2,1)}, bf16[48,1920]{1,0:T(8,128)(2,1)}, u32[]{:S(2)}, u32[]{:S(2)}) %collective-permute-start.6) | collective-permute-done | bytes 184352 | tf_op jit(solution)/shard_map/ppermute | solution.py:769
  51.0 6.8 %enter.1 = (bf16[768,1024]{1,0:T(8,128)(2,1)S(1)}, bf16[1024,1152]{1,0:T(8,128)(2,1)S(1)}, bf16[768,1152]{1,0:T(8,128)(2,1)S(1)}, f32[8,768]{1,0:T(8,128)S(1)}) custom-call(s32[64]{0:T(128)S(1)} %pad_add_fusion.table, f32[1024,768]{1,0:T(8,128)S(1)} %maximum_select_fusion.tokens, bf16[192,640]{1,0:T(8,128)(2,1)} %get-tuple-element.127.wa, ...), custom_call_target="tpu_custom_call" | custom-call | flops 9999999827968 | bytes 1000000000 | tf_op jit(solution)/shard_map/enter/pallas_call | solution.py:146
  61.2 13.0 %attend.1 = (bf16[1024,384]{1,0:T(8,128)(2,1)S(1)}, f32[24,1024]{1,0:T(8,128)S(1)}) custom-call(bf16[1024,1152]{1,0:T(8,128)(2,1)S(1)} %get-tuple-element.138.queries.keys.values, bf16[1024,1152]{1,0:T(8,128)(2,1)S(1)} %get-tuple-element.138.queries.keys.values, bf16[1024,1152]{1,0:T(8,128)(2,1)S(1)} %get-tuple-element.138.queries.keys.values, ...), custom_call_target="tpu_custom_call" | custom-call | flops 9999999827968 | bytes 1000000000 | tf_op jit(solution)/shard_map/attend/pallas_call | solution.py:227
  79.3 2.6 %collective-permute-done.24.wd.wh = bf16[192,896]{1,0:T(8,128)(2,1)} collective-permute-done((bf16[192,896]{1,0:T(8,128)(2,1)}, bf16[192,896]{1,0:T(8,128)(2,1)}, u32[]{:S(2)}, u32[]{:S(2)}) %collective-permute-start.24) | collective-permute-done | bytes 344096 | tf_op jit(solution)/shard_map/ppermute | solution.py:769
  83.9 4.7 %leave.1 = (bf16[1024,768]{1,0:T(8,128)(2,1)}, bf16[768,384]{1,0:T(8,128)(2,1)S(1)}) custom-call(s32[64]{0:T(128)S(1)} %pad_add_fusion.table, bf16[1024,384]{1,0:T(8,128)(2,1)S(1)} %get-tuple-element.149.att.out, bf16[192,896]{1,0:T(8,128)(2,1)} %get-tuple-element.135.wa.we, bf16[192,896]{1,0:T(8,128)(2,1)} %collective-permute-done.15.wb.wf, ...), custom_call_target="tpu_custom_call" | custom-call | flops 9999999827968 | bytes 1000000000 | tf_op jit(solution)/shard_map/leave/pallas_call | solution.py:343
  95.1 9.7 %feed_first.1 = (f32[1024,768]{1,0:T(8,128)S(1)}, bf16[768,1024]{1,0:T(8,128)(2,1)S(1)}, bf16[1024,1536]{1,0:T(8,128)(2,1)S(1)}, bf16[1024,1536]{1,0:T(8,128)(2,1)S(1)}, bf16[768,1536]{1,0:T(8,128)(2,1)S(1)}) custom-call(s32[64]{0:T(128)S(1)} %copy-done.9, f32[1024,768]{1,0:T(8,128)S(1)} %copy-done.2, bf16[1024,768]{1,0:T(8,128)(2,1)} %get-tuple-element.150.part, ...), custom_call_target="tpu_custom_call" | custom-call | flops 9999999827968 | bytes 1000000000 | tf_op jit(solution)/shard_map/feed_first/pallas_call | solution.py:420
  104.9 5.4 %feed_weight.2 = (bf16[384,768]{1,0:T(8,128)(2,1)S(1)}, bf16[384,768]{1,0:T(8,128)(2,1)}, bf16[384,768]{1,0:T(8,128)(2,1)S(1)}, bf16[384,768]{1,0:T(8,128)(2,1)}) custom-call(s32[64]{0:T(128)S(1)} %copy-done.9, bf16[768,1024]{1,0:T(8,128)(2,1)S(1)} %copy.24.flip, bf16[1024,1536]{1,0:T(8,128)(2,1)S(1)} %get-tuple-element.154.side.act), custom_call_target="tpu_custom_call" | custom-call | flops 9999999827968 | bytes 1000000000 | tf_op jit(solution)/shard_map/feed_weight/pallas_call | solution.py:526
  111.4 10.9 %feed_tokens.1 = (bf16[1024,768]{1,0:T(8,128)(2,1)S(1)}, bf16[1024,768]{1,0:T(8,128)(2,1)}, bf16[1024,1536]{1,0:T(8,128)(2,1)S(1)}) custom-call(s32[64]{0:T(128)S(1)} %copy-done.9, bf16[1024,768]{1,0:T(8,128)(2,1)S(1)} %copy-done, bf16[1024,1536]{1,0:T(8,128)(2,1)S(1)} %get-tuple-element.154.side.act, bf16[1024,1536]{1,0:T(8,128)(2,1)S(1)} %get-tuple-element.161.slope, ...), custom_call_target="tpu_custom_call" | custom-call | flops 9999999827968 | bytes 1000000000 | tf_op jit(solution)/shard_map/feed_tokens/pallas_call | solution.py:483
  122.4 5.7 %feed_weight.3 = (bf16[384,768]{1,0:T(8,128)(2,1)S(1)}, bf16[384,768]{1,0:T(8,128)(2,1)}, bf16[384,768]{1,0:T(8,128)(2,1)S(1)}, bf16[384,768]{1,0:T(8,128)(2,1)}) custom-call(s32[64]{0:T(128)S(1)} %copy-done.9, bf16[768,1024]{1,0:T(8,128)(2,1)S(1)} %get-tuple-element.159.flip, bf16[1024,1536]{1,0:T(8,128)(2,1)S(1)} %get-tuple-element.167.side), custom_call_target="tpu_custom_call" | custom-call | flops 9999999827968 | bytes 1000000000 | tf_op jit(solution)/shard_map/feed_weight/pallas_call | solution.py:526
  131.0 7.6 %middle_back.1 = (f32[1024,768]{1,0:T(8,128)S(1)}, bf16[1024,384]{1,0:T(8,128)(2,1)S(1)}, bf16[384,768]{1,0:T(8,128)(2,1)S(1)}, bf16[384,768]{1,0:T(8,128)(2,1)}, f32[8,768]{1,0:T(8,128)S(1)}) custom-call(s32[64]{0:T(128)S(1)} %copy-done.9, bf16[1024,768]{1,0:T(8,128)(2,1)} %get-tuple-element.172.pulled, bf16[1024,768]{1,0:T(8,128)(2,1)} %collective-permute-done.32.far, ...), custom_call_target="tpu_custom_call" | custom-call | flops 9999999827968 | bytes 1000000000 | tf_op jit(solution)/shard_map/middle_back/pallas_call | solution.py:592
  138.6 7.8 %attend_back.2.refs_0_ = bf16[3,1024,384]{2,1,0:T(8,128)(2,1)S(1)} custom-call(bf16[1024,1152]{1,0:T(8,128)(2,1)S(1)} %copy-done.15, bf16[1024,1152]{1,0:T(8,128)(2,1)S(1)} %copy-done.15, bf16[1024,1152]{1,0:T(8,128)(2,1)S(1)} %copy-done.15, bf16[1024,384]{1,0:T(8,128)(2,1)S(1)} %copy-done.21, bf16[1024,384]{1,0:T(8,128)(2,1)S(1)} %get-tuple-element.175.grad, ...), custom_call_target="tpu_custom_call" | custom-call | flops 9999999827968 | bytes 1000000000 | tf_op jit(solution)/shard_map/attend_back/pallas_call | solution.py:298
  146.5 3.0 %fold_half.2 = (bf16[192,1536]{1,0:T(8,128)(2,1)S(1)}, bf16[192,1536]{1,0:T(8,128)(2,1)}, bf16[192,1536]{1,0:T(8,128)(2,1)S(1)}, bf16[192,1536]{1,0:T(8,128)(2,1)}) custom-call(bf16[384,768]{1,0:T(8,128)(2,1)S(1)} %get-tuple-element.177.refs_0_, bf16[384,768]{1,0:T(8,128)(2,1)} %collective-permute-done.26.refs_1_, ...), custom_call_target="tpu_custom_call" | custom-call | flops 9999999827968 | bytes 1000000000 | tf_op jit(solution)/shard_map/fold_half/pallas_call | solution.py:789
  150.6 3.8 %attend_back.3.proj_grad = bf16[3,1024,384]{2,1,0:T(8,128)(2,1)S(1)} custom-call(bf16[1024,1152]{1,0:T(8,128)(2,1)S(1)} %copy-done.15, bf16[1024,1152]{1,0:T(8,128)(2,1)S(1)} %copy-done.15, bf16[1024,1152]{1,0:T(8,128)(2,1)S(1)} %copy-done.15, bf16[1024,384]{1,0:T(8,128)(2,1)S(1)} %copy-done.21, ...), custom_call_target="tpu_custom_call", output_to_operand_aliasing={{}: (8, {})} | custom-call | flops 9999999827968 | bytes 1000000000 | tf_op jit(solution)/shard_map/attend_back/pallas_call | solution.py:298
  154.4 4.5 %weight_back.1 = (bf16[384,768]{1,0:T(8,128)(2,1)S(1)}, bf16[384,768]{1,0:T(8,128)(2,1)}, bf16[384,768]{1,0:T(8,128)(2,1)S(1)}, bf16[384,768]{1,0:T(8,128)(2,1)}) custom-call(s32[64]{0:T(128)S(1)} %copy-done.9, bf16[3,1024,384]{2,1,0:T(8,128)(2,1)S(1)} %attend_back.3.proj_grad, ...), custom_call_target="tpu_custom_call", output_to_operand_aliasing={{2}: (3, {}), {3}: (4, {})} | custom-call | flops 9999999827968 | bytes 1000000000 | tf_op jit(solution)/shard_map/weight_back/pallas_call | solution.py:663
  161.8 4.2 %token_back.1.pulled = bf16[1024,768]{1,0:T(8,128)(2,1)} custom-call(bf16[3,1024,384]{2,1,0:T(8,128)(2,1)S(1)} %attend_back.3.proj_grad, bf16[768,1152]{1,0:T(8,128)(2,1)S(1)} %copy-done.17), custom_call_target="tpu_custom_call" | custom-call | flops 9999999827968 | bytes 1000000000 | tf_op jit(solution)/shard_map/token_back/pallas_call | solution.py:695
  166.6 2.3 %fold_quarter.2 = (bf16[48,3072]{1,0:T(8,128)(2,1)S(1)}, bf16[48,3072]{1,0:T(8,128)(2,1)}, bf16[48,3072]{1,0:T(8,128)(2,1)}, bf16[48,3072]{1,0:T(8,128)(2,1)}) custom-call(bf16[192,1536]{1,0:T(8,128)(2,1)S(1)} %get-tuple-element.199.one, bf16[192,1536]{1,0:T(8,128)(2,1)} %collective-permute-done.33.one_far, bf16[192,1536]{1,0:T(8,128)(2,1)S(1)} %get-tuple-element.201.two, ...), custom_call_target="tpu_custom_call" | custom-call | flops 9999999827968 | bytes 1000000000 | tf_op jit(solution)/shard_map/fold_quarter/pallas_call | solution.py:789
  171.3 6.6 %collective-permute-done.39.refs_1_ = bf16[384,768]{1,0:T(8,128)(2,1)} collective-permute-done((bf16[384,768]{1,0:T(8,128)(2,1)}, bf16[384,768]{1,0:T(8,128)(2,1)}, u32[]{:S(2)}, u32[]{:S(2)}) %collective-permute-start.39) | collective-permute-done | bytes 589856 | tf_op jit(solution)/shard_map/ppermute | solution.py:769
  183.2 5.1 %leave_layer.1 = (f32[512,768]{1,0:T(8,128)}, f32[8,768]{1,0:T(8,128)S(1)}) custom-call(s32[1]{0:T(128)} %bitcast.11.core, bf16[1024,768]{1,0:T(8,128)(2,1)} %token_back.1.pulled, bf16[1024,768]{1,0:T(8,128)(2,1)} %collective-permute-done.38.far, f32[1024,768]{1,0:T(8,128)S(1)} %copy-done.3, f32[1024,768]{1,0:T(8,128)S(1)} %get-tuple-element.217.middle_grad, ...), custom_call_target="tpu_custom_call" | custom-call | flops 9999999827968 | bytes 1000000000 | tf_op jit(solution)/shard_map/leave_layer/pallas_call | solution.py:742
  195.1 9.7 %collective-permute-done.36 = bf16[48,3072]{1,0:T(8,128)(2,1)} collective-permute-done((bf16[48,3072]{1,0:T(8,128)(2,1)}, bf16[48,3072]{1,0:T(8,128)(2,1)}, u32[]{:S(2)}, u32[]{:S(2)}) %collective-permute-start.36) | collective-permute-done | bytes 294944 | tf_op jit(solution)/shard_map/ppermute | solution.py:769
  212.6 2.9 %collective-permute-start.50 = (f32[4,768]{1,0:T(4,128)S(1)}, f32[4,768]{1,0:T(4,128)S(1)}, u32[]{:S(2)}, u32[]{:S(2)}) collective-permute-start(f32[4,768]{1,0:T(4,128)S(1)} %add.94), channel_id=1, source_target_pairs={{0,16},{2,18},{4,20},{6,22},{8,24},{10,26},{12,28},{14,30},{16,0},... | collective-permute-start | bytes 36872 | tf_op jit(solution)/shard_map/ppermute | solution.py:769
  218.4 2.6 %collective-permute-done.51 = f32[4,768]{1,0:T(4,128)S(1)} collective-permute-done((f32[4,768]{1,0:T(4,128)S(1)}, f32[4,768]{1,0:T(4,128)S(1)}, u32[]{:S(2)}, u32[]{:S(2)}) %collective-permute-start.51) | collective-permute-done | bytes 12320 | tf_op jit(solution)/shard_map/ppermute | solution.py:769
  (196 shorter events, 88.8 us)
Async XLA Ops:
  21.9 16.6 %collective-permute-start.6 = (bf16[48,1920]{1,0:T(8,128)(2,1)}, bf16[48,1920]{1,0:T(8,128)(2,1)}, u32[]{:S(2)}, u32[]{:S(2)}) collective-permute-start(bf16[48,1920]{1,0:T(8,128)(2,1)} %pad_maximum_fusion.3.refs_0_), channel_id=1, source_target_pairs={{0,16},{2,18},{4,20},{6,22},{8,24},{10,26},{12,28},{14,30},{16,0},... | collective-permute-start | bytes 552968 | tf_op jit(solution)/shard_map/ppermute | solution.py:769
  23.0 17.0 %collective-permute-start.7 = (bf16[48,1920]{1,0:T(8,128)(2,1)}, bf16[48,1920]{1,0:T(8,128)(2,1)}, u32[]{:S(2)}, u32[]{:S(2)}) collective-permute-start(bf16[48,1920]{1,0:T(8,128)(2,1)} %pad_maximum_fusion.3.refs_0_), channel_id=1, source_target_pairs={{0,24},{2,26},{4,28},{6,30},{8,16},{10,18},{12,20},{14,22},{16,8},... | collective-permute-start | bytes 552968 | tf_op jit(solution)/shard_map/ppermute | solution.py:769
  44.2 30.1 %collective-permute-start.18 = (bf16[96,1536]{1,0:T(8,128)(2,1)}, bf16[96,1536]{1,0:T(8,128)(2,1)}, u32[]{:S(2)}, u32[]{:S(2)}) collective-permute-start(bf16[96,1536]{1,0:T(8,128)(2,1)} %beside.1.refs_0_), channel_id=1, source_target_pairs={{0,8},{2,10},{4,12},{6,14},{8,0},{10,2},{12,4},{14,6},{16,24},{18,... | collective-permute-start | bytes 884744 | tf_op jit(solution)/shard_map/ppermute | solution.py:769
  46.4 29.4 %collective-permute-start.19 = (bf16[96,1536]{1,0:T(8,128)(2,1)}, bf16[96,1536]{1,0:T(8,128)(2,1)}, u32[]{:S(2)}, u32[]{:S(2)}) collective-permute-start(bf16[96,1536]{1,0:T(8,128)(2,1)} %beside.1.refs_0_), channel_id=1, source_target_pairs={{0,16},{2,18},{4,20},{6,22},{8,24},{10,26},{12,28},{14,30},{16,0},... | collective-permute-start | bytes 884744 | tf_op jit(solution)/shard_map/ppermute | solution.py:769
  47.5 28.3 %collective-permute-start.20 = (bf16[96,1536]{1,0:T(8,128)(2,1)}, bf16[96,1536]{1,0:T(8,128)(2,1)}, u32[]{:S(2)}, u32[]{:S(2)}) collective-permute-start(bf16[96,1536]{1,0:T(8,128)(2,1)} %beside.1.refs_0_), channel_id=1, source_target_pairs={{0,24},{2,26},{4,28},{6,30},{8,16},{10,18},{12,20},{14,22},{16,8},... | collective-permute-start | bytes 884744 | tf_op jit(solution)/shard_map/ppermute | solution.py:769
  59.1 20.2 %collective-permute-start.21 = (bf16[192,1024]{1,0:T(8,128)(2,1)}, bf16[192,1024]{1,0:T(8,128)(2,1)}, u32[]{:S(2)}, u32[]{:S(2)}) collective-permute-start(bf16[192,1024]{1,0:T(8,128)(2,1)} %get-tuple-element.134.wa), channel_id=1, source_target_pairs={{0,2},{2,0},{4,6},{6,4},{8,10},{10,8},{12,14},{14,12},{16,18},{18,... | collective-permute-start | bytes 1179656 | tf_op jit(solution)/shard_map/ppermute | solution.py:769
  60.6 18.7 %collective-permute-start.23 = (bf16[192,896]{1,0:T(8,128)(2,1)}, bf16[192,896]{1,0:T(8,128)(2,1)}, u32[]{:S(2)}, u32[]{:S(2)}) collective-permute-start(bf16[192,896]{1,0:T(8,128)(2,1)} %get-tuple-element.135.wa.we), channel_id=1, source_target_pairs={{0,4},{2,6},{4,0},{6,2},{8,12},{10,14},{12,8},{14,10},{16,20},{18,... | collective-permute-start | bytes 1032200 | tf_op jit(solution)/shard_map/ppermute | solution.py:769
  90.2 21.2 %collective-permute-start.28 = (bf16[384,768]{1,0:T(8,128)(2,1)}, bf16[384,768]{1,0:T(8,128)(2,1)}, u32[]{:S(2)}, u32[]{:S(2)}) collective-permute-start(bf16[384,768]{1,0:T(8,128)(2,1)} %copy-done.10), channel_id=1, source_target_pairs={{0,4},{2,6},{4,0},{6,2},{8,12},{10,14},{12,8},{14,10},{16,20},{18,... | collective-permute-start | bytes 1769480 | tf_op jit(solution)/shard_map/ppermute | solution.py:769
  90.9 20.5 %collective-permute-start.29 = (bf16[384,768]{1,0:T(8,128)(2,1)}, bf16[384,768]{1,0:T(8,128)(2,1)}, u32[]{:S(2)}, u32[]{:S(2)}) collective-permute-start(bf16[384,768]{1,0:T(8,128)(2,1)} %copy-done.12), channel_id=1, source_target_pairs={{0,2},{2,0},{4,6},{6,4},{8,10},{10,8},{12,14},{14,12},{16,18},{18,... | collective-permute-start | bytes 1769480 | tf_op jit(solution)/shard_map/ppermute | solution.py:769
  110.3 36.2 %collective-permute-start.26 = (bf16[384,768]{1,0:T(8,128)(2,1)}, bf16[384,768]{1,0:T(8,128)(2,1)}, u32[]{:S(2)}, u32[]{:S(2)}) collective-permute-start(bf16[384,768]{1,0:T(8,128)(2,1)} %get-tuple-element.156), channel_id=1, source_target_pairs={{0,2},{2,0},{4,6},{6,4},{8,10},{10,8},{12,14},{14,12},{16,18},{18,... | collective-permute-start | bytes 1769480 | tf_op jit(solution)/shard_map/ppermute | solution.py:769
  110.8 35.7 %collective-permute-start.27 = (bf16[384,768]{1,0:T(8,128)(2,1)}, bf16[384,768]{1,0:T(8,128)(2,1)}, u32[]{:S(2)}, u32[]{:S(2)}) collective-permute-start(bf16[384,768]{1,0:T(8,128)(2,1)} %get-tuple-element.158), channel_id=1, source_target_pairs={{0,4},{2,6},{4,0},{6,2},{8,12},{10,14},{12,8},{14,10},{16,20},{18,... | collective-permute-start | bytes 1769480 | tf_op jit(solution)/shard_map/ppermute | solution.py:769
  128.0 18.4 %collective-permute-start.30 = (bf16[384,768]{1,0:T(8,128)(2,1)}, bf16[384,768]{1,0:T(8,128)(2,1)}, u32[]{:S(2)}, u32[]{:S(2)}) collective-permute-start(bf16[384,768]{1,0:T(8,128)(2,1)} %get-tuple-element.169), channel_id=1, source_target_pairs={{0,2},{2,0},{4,6},{6,4},{8,10},{10,8},{12,14},{14,12},{16,18},{18,... | collective-permute-start | bytes 1769480 | tf_op jit(solution)/shard_map/ppermute | solution.py:769
  129.5 16.9 %collective-permute-start.31 = (bf16[384,768]{1,0:T(8,128)(2,1)}, bf16[384,768]{1,0:T(8,128)(2,1)}, u32[]{:S(2)}, u32[]{:S(2)}) collective-permute-start(bf16[384,768]{1,0:T(8,128)(2,1)} %get-tuple-element.171), channel_id=1, source_target_pairs={{0,4},{2,6},{4,0},{6,2},{8,12},{10,14},{12,8},{14,10},{16,20},{18,... | collective-permute-start | bytes 1769480 | tf_op jit(solution)/shard_map/ppermute | solution.py:769
  149.4 17.1 %collective-permute-start.33 = (bf16[192,1536]{1,0:T(8,128)(2,1)}, bf16[192,1536]{1,0:T(8,128)(2,1)}, u32[]{:S(2)}, u32[]{:S(2)}) collective-permute-start(bf16[192,1536]{1,0:T(8,128)(2,1)} %get-tuple-element.186), channel_id=1, source_target_pairs={{0,4},{2,6},{4,0},{6,2},{8,12},{10,14},{12,8},{14,10},{16,20},{18,... | collective-permute-start | bytes 1769480 | tf_op jit(solution)/shard_map/ppermute | solution.py:769
  150.0 16.6 %collective-permute-start.34 = (bf16[192,1536]{1,0:T(8,128)(2,1)}, bf16[192,1536]{1,0:T(8,128)(2,1)}, u32[]{:S(2)}, u32[]{:S(2)}) collective-permute-start(bf16[192,1536]{1,0:T(8,128)(2,1)} %get-tuple-element.188), channel_id=1, source_target_pairs={{0,2},{2,0},{4,6},{6,4},{8,10},{10,8},{12,14},{14,12},{16,18},{18,... | collective-permute-start | bytes 1769480 | tf_op jit(solution)/shard_map/ppermute | solution.py:769
  158.9 19.0 %collective-permute-start.39 = (bf16[384,768]{1,0:T(8,128)(2,1)}, bf16[384,768]{1,0:T(8,128)(2,1)}, u32[]{:S(2)}, u32[]{:S(2)}) collective-permute-start(bf16[384,768]{1,0:T(8,128)(2,1)} %get-tuple-element.194), channel_id=1, source_target_pairs={{0,2},{2,0},{4,6},{6,4},{8,10},{10,8},{12,14},{14,12},{16,18},{18,... | collective-permute-start | bytes 1769480 | tf_op jit(solution)/shard_map/ppermute | solution.py:769
  160.3 18.6 %collective-permute-start.40 = (bf16[384,768]{1,0:T(8,128)(2,1)}, bf16[384,768]{1,0:T(8,128)(2,1)}, u32[]{:S(2)}, u32[]{:S(2)}) collective-permute-start(bf16[384,768]{1,0:T(8,128)(2,1)} %get-tuple-element.196), channel_id=1, source_target_pairs={{0,4},{2,6},{4,0},{6,2},{8,12},{10,14},{12,8},{14,10},{16,20},{18,... | collective-permute-start | bytes 1769480 | tf_op jit(solution)/shard_map/ppermute | solution.py:769
  166.0 16.1 %collective-permute-start.38 = (bf16[1024,768]{1,0:T(8,128)(2,1)}, bf16[1024,768]{1,0:T(8,128)(2,1)}, u32[]{:S(2)}, u32[]{:S(2)}) collective-permute-start(bf16[1024,768]{1,0:T(8,128)(2,1)} %token_back.1.pulled), channel_id=1, source_target_pairs={{0,1},{1,0},{2,3},{3,2},{4,5},{5,4},{6,7},{7,6},{8,9},{9,8},{10,11... | collective-permute-start | bytes 4718600 | tf_op jit(solution)/shard_map/ppermute | solution.py:765
  168.9 24.9 %collective-permute-start.35 = (bf16[48,3072]{1,0:T(8,128)(2,1)}, bf16[48,3072]{1,0:T(8,128)(2,1)}, u32[]{:S(2)}, u32[]{:S(2)}) collective-permute-start(bf16[48,3072]{1,0:T(8,128)(2,1)} %get-tuple-element.204), channel_id=1, source_target_pairs={{0,24},{2,26},{4,28},{6,30},{8,16},{10,18},{12,20},{14,22},{16,8},... | collective-permute-start | bytes 884744 | tf_op jit(solution)/shard_map/ppermute | solution.py:769
  171.1 33.7 %collective-permute-start.36 = (bf16[48,3072]{1,0:T(8,128)(2,1)}, bf16[48,3072]{1,0:T(8,128)(2,1)}, u32[]{:S(2)}, u32[]{:S(2)}) collective-permute-start(bf16[48,3072]{1,0:T(8,128)(2,1)} %get-tuple-element.205), channel_id=1, source_target_pairs={{0,16},{2,18},{4,20},{6,22},{8,24},{10,26},{12,28},{14,30},{16,0},... | collective-permute-start | bytes 884744 | tf_op jit(solution)/shard_map/ppermute | solution.py:769
  177.9 26.9 %collective-permute-start.37 = (bf16[48,3072]{1,0:T(8,128)(2,1)}, bf16[48,3072]{1,0:T(8,128)(2,1)}, u32[]{:S(2)}, u32[]{:S(2)}) collective-permute-start(bf16[48,3072]{1,0:T(8,128)(2,1)} %get-tuple-element.206), channel_id=1, source_target_pairs={{0,8},{2,10},{4,12},{6,14},{8,0},{10,2},{12,4},{14,6},{16,24},{18,... | collective-permute-start | bytes 884744 | tf_op jit(solution)/shard_map/ppermute | solution.py:769
  190.7 21.8 %collective-permute-start.44 = (bf16[48,1536]{1,0:T(8,128)(2,1)S(1)}, bf16[48,1536]{1,0:T(8,128)(2,1)S(1)}, u32[]{:S(2)}, u32[]{:S(2)}) collective-permute-start(bf16[48,1536]{1,0:T(8,128)(2,1)S(1)} %get-tuple-element.227), channel_id=1, source_target_pairs={{0,24},{2,26},{4,28},{6,30},{8,16},{10,18},{12,20},{14,22},{16,8},... | collective-permute-start | bytes 442376 | tf_op jit(solution)/shard_map/ppermute | solution.py:769
  192.8 19.7 %collective-permute-start.45 = (bf16[48,1536]{1,0:T(8,128)(2,1)S(1)}, bf16[48,1536]{1,0:T(8,128)(2,1)S(1)}, u32[]{:S(2)}, u32[]{:S(2)}) collective-permute-start(bf16[48,1536]{1,0:T(8,128)(2,1)S(1)} %get-tuple-element.226), channel_id=1, source_target_pairs={{0,16},{2,18},{4,20},{6,22},{8,24},{10,26},{12,28},{14,30},{16,0},... | collective-permute-start | bytes 442376 | tf_op jit(solution)/shard_map/ppermute | solution.py:769
  193.8 18.7 %collective-permute-start.46 = (bf16[48,1536]{1,0:T(8,128)(2,1)S(1)}, bf16[48,1536]{1,0:T(8,128)(2,1)S(1)}, u32[]{:S(2)}, u32[]{:S(2)}) collective-permute-start(bf16[48,1536]{1,0:T(8,128)(2,1)S(1)} %get-tuple-element.225), channel_id=1, source_target_pairs={{0,8},{2,10},{4,12},{6,14},{8,0},{10,2},{12,4},{14,6},{16,24},{18,... | collective-permute-start | bytes 442376 | tf_op jit(solution)/shard_map/ppermute | solution.py:769
  (58 other events, 582.1 us)
